TPU v7x, 32 devices: a whole 2x2x4 slice. The times are simulated.
32 devices in a mesh: gx: 2 (over y), gy: 16 (over z, x, core).
Axes of the slice: x: 2, y: 2, z: 4, core: 2. Of those that a mesh axis runs over, the one named last changes fastest.
Arguments:
- state: float32 [5, 8, 1024, 768], P(None, None, 'gy', 'gx'), may hold values from -6 to 6
- driving: float32 [5, 8, 1024, 768], P(None, None, 'gy', 'gx'), may hold values from -6 to 6
- rate: float32 [5, 8], replicated, may hold values from 1 to 6
- sound_square: float32 [8, 1024, 768], P(None, 'gy', 'gx'), may hold values from 0.3 to 1
Outputs:
- nudged: float32 [5, 8, 1024, 768], P(None, None, 'gy', 'gx')
All inputs are finite; a program needn't handle non-finite values.
Results may differ from a plain program's by a relative error of at most 0.000064.
Values sent between devices are 32-bit elements; how exact they have to be, the bound alone decides.
No kernel may reach another device: no remote copies, remote signals or barrier semaphores. Data moves between devices by JAX's collectives and lax.ppermute only.
A program may use at most 128 MiB of HBM per device.

v0:
```python
import functools

import jax
import jax.numpy as jnp
import numpy as np
from jax import lax
from jax.experimental import pallas as pl
from jax.experimental.pallas import tpu as pltpu
from jax.sharding import PartitionSpec as P


MODES = 64
SUBSTEPS = 3
COURANT = 0.5
LANES = 128
SUB = 8
GUARD = 8
VMEM_LIMIT = 32 << 20

REACH_X = (5, 4, 4, 6, 4, 4)
GROUP_X = (0, 0, 1, 0, 1, 1)


def lane_starts(levels):
    used = [0, 0]
    starts = []
    for width, group in zip(REACH_X, GROUP_X):
        starts.append(used[group])
        used[group] += width * levels
    assert max(used) <= LANES
    return starts


def bases(count, total):
    index = np.arange(total, dtype=np.int64)
    order = np.arange(count, dtype=np.int64)
    freq = np.where(order < count // 2, order, order - count // 2 + 1)
    wrapped = (freq[:, None] * (2 * index[None, :] + 1)) % (2 * total)
    phase = np.pi * wrapped.astype(np.float64) / total
    basis = np.where(order[:, None] < count // 2, np.cos(phase), np.sin(phase))
    scaling = np.where(order == 0, 1.0 / total, 2.0 / total)
    basis32 = basis.astype(np.float32)
    weight32 = (basis * scaling[:, None]).astype(np.float32)
    return basis32, weight32


def halves(table):
    high = table.astype(jnp.bfloat16)
    low = (table - high.astype(np.float32)).astype(jnp.bfloat16)
    return np.asarray(high), np.asarray(low)


def split(value):
    high = value.astype(jnp.bfloat16)
    low = (value - high.astype(jnp.float32)).astype(jnp.bfloat16)
    return high, low


def dot(left, right):
    return jnp.dot(left, right, preferred_element_type=jnp.float32)


def masks_of(bits):
    masks = [0]
    for bit in bits:
        masks = masks + [mask | (1 << bit) for mask in masks]
    return masks


def stages_of(devices):
    total = devices.bit_length() - 1
    assert devices == 1 << total
    left = list(range(total))
    stages = []
    if left:
        stages.append([left.pop(0)])
    while len(left) > 3 and len(stages) < 3:
        stages.append([left.pop(0), left.pop()])
    return stages, left


def slab_kernel(facts, state_ref, sound_ref, a_ref, b_ref, extra_ref, sem):
    levels, _, _, cols = a_ref.shape
    rows = state_ref.shape[2]
    bottom = facts[4]
    copies = []
    for phase, out_ref in enumerate((a_ref, b_ref)):
        last = bottom if phase == 0 else 1 - bottom
        here = pl.ds(pl.multiple_of(last * (rows - SUB), SUB), SUB)
        for place, (source, target) in enumerate(
            (
                (state_ref.at[3], out_ref.at[:, 0]),
                (state_ref.at[1], out_ref.at[:, 1]),
                (state_ref.at[0], out_ref.at[:, 2]),
                (state_ref.at[4], out_ref.at[:, 3]),
                (state_ref.at[2], extra_ref.at[phase, 0]),
                (sound_ref, extra_ref.at[phase, 1]),
            )
        ):
            copies.append(pltpu.make_async_copy(source.at[:, here], target, sem.at[phase, place]))
    for copy in copies:
        copy.start()
    for copy in copies:
        copy.wait()
    index = lax.broadcasted_iota(jnp.int32, (SUB, cols), 0)
    for phase, out_ref in enumerate((a_ref, b_ref)):
        last = bottom if phase == 0 else 1 - bottom
        own = (index // 4) == last
        for level in range(levels):
            for place in range(2):
                turned = pltpu.roll(extra_ref[phase, place, level], 4, 0)
                out_ref[level, 2 + place] = jnp.where(own, out_ref[level, 2 + place], turned)


def project_kernel(
    facts, state_ref, driving_ref, wx_hbm, wy_hbm, keep_ref, send_ref, held, other, wx_ref, wy_ref, packed_ref, modes_ref, sem
):
    fields, levels, rows, cols = state_ref.shape
    half = levels // 2
    pieces = 2 * keep_ref.shape[0]
    chunk = keep_ref.shape[2]
    tables = [
        pltpu.make_async_copy(wx_hbm.at[facts[0]], wx_ref, sem.at[fields, 0]),
        pltpu.make_async_copy(wy_hbm.at[facts[1]], wy_ref, sem.at[fields, 1]),
    ]
    loads = [
        [
            pltpu.make_async_copy(state_ref.at[field], held.at[field], sem.at[field, 0]),
            pltpu.make_async_copy(driving_ref.at[field], other.at[field], sem.at[field, 1]),
        ]
        for field in range(fields)
    ]
    for copy in [*loads[0], *tables, *(copy for load in loads[1:] for copy in load)]:
        copy.start()
    lane = lax.broadcasted_iota(jnp.int32, (half * rows, LANES), 1)
    for copy in tables:
        copy.wait()
    weights = wx_ref[...]
    for field in range(fields):
        for copy in loads[field]:
            copy.wait()
        sides = []
        for side in range(2):
            part = pl.ds(side * half, half)
            diff = (held[field, part] - other[field, part]).reshape(half * rows, cols)
            high, low = split(diff)
            both = dot(high, weights) + dot(low, weights)
            sides.append(both + pltpu.roll(both, MODES, 1))
        high, low = split(jnp.where(lane < MODES, sides[0], sides[1]))
        packed_ref[field, :, :LANES] = high
        packed_ref[field, :, LANES:] = low
    for field in range(fields):
        for pair in range(half):
            out = dot(wy_ref[...], packed_ref[field, pair * rows : (pair + 1) * rows])
            out = out[:MODES] + out[MODES:]
            modes_ref[field, pair * MODES : (pair + 1) * MODES] = out[:, :LANES] + out[:, LANES:]
    mine = facts[2]
    for piece in range(pieces):
        source = pl.multiple_of(jnp.bitwise_xor(mine, piece) * chunk, SUB)
        target = keep_ref if piece < pieces // 2 else send_ref
        target[piece % (pieces // 2)] = modes_ref[:, pl.ds(source, chunk)]


def nudge_kernel(facts, rate_ref, ext_ref, own_ref, far_ref, wide_ref, by_ref, out_ref, modes_ref, back_ref, done_ref, sem):
    fields, levels, rows, cols = out_ref.shape
    tiles = cols // LANES
    half = levels // 2
    pieces = 2 * own_ref.shape[0]
    chunk = own_ref.shape[2]
    mine = facts[2]
    for piece in range(pieces):
        target = pl.multiple_of(jnp.bitwise_xor(mine, piece) * chunk, SUB)
        source = own_ref if piece < pieces // 2 else far_ref
        modes_ref[:, pl.ds(target, chunk)] = source[piece % (pieces // 2)]
    lane = lax.broadcasted_iota(jnp.int32, (MODES, LANES), 1)
    for field in range(fields):
        for pair in range(half):
            factor = jnp.where(lane < MODES, rate_ref[field, pair], rate_ref[field, pair + half])
            high, low = split(modes_ref[field, pair * MODES : (pair + 1) * MODES] * factor)
            out = dot(by_ref[...], jnp.concatenate([high, low], axis=1))
            out = out[:rows] + out[rows:]
            high, low = split(out[:, :LANES] + out[:, LANES:])
            back_ref[field, pair * rows : (pair + 1) * rows, :LANES] = high
            back_ref[field, pair * rows : (pair + 1) * rows, LANES:] = low
    main = pl.ds(GUARD + SUB, rows)
    stores = []
    for field in range(fields):
        left = back_ref[field]
        tendency = dot(left, wide_ref[: 4 * MODES]) + dot(left[:, :LANES], wide_ref[4 * MODES :])
        for level in range(levels):
            first = (level % half) * rows
            for tile in range(tiles):
                lanes = pl.ds(tile * LANES, LANES)
                column = (level // half) * cols + tile * LANES
                done_ref[field, level, :, lanes] = (
                    ext_ref[field, level, tile, main] - tendency[first : first + rows, column : column + LANES]
                )
        stores.append(pltpu.make_async_copy(done_ref.at[field], out_ref.at[field], sem.at[field]))
        stores[-1].start()
    for copy in stores:
        copy.wait()


def band_lanes(level_count):
    starts = lane_starts(level_count)
    for item in range(6):
        for level in range(level_count):
            yield item, level, REACH_X[item], GROUP_X[item], starts[item] + REACH_X[item] * level


def load_kernel(facts, state_ref, sound_ref, a_ref, b_ref, bx_hbm, by_hbm, ext_ref, wide_ref, by_ref, *refs):
    *bands, sem = refs
    _, levels, rows, cols = state_ref.shape
    tiles = cols // LANES
    main = GUARD + SUB
    loads = []
    for tile in dict.fromkeys((0, tiles - 1, *range(tiles))):
        for item in range(6):
            source = state_ref.at[item] if item < 5 else sound_ref
            loads.append(
                pltpu.make_async_copy(
                    source.at[:, :, pl.ds(tile * LANES, LANES)],
                    ext_ref.at[item, :, tile, pl.ds(main, rows)],
                    sem.at[item, tile],
                )
            )
    tables = [pltpu.make_async_copy(by_hbm.at[facts[1]], by_ref, sem.at[6, 0])]
    for copy in range(3):
        for side in range(2):
            target = wide_ref.at[
                pl.ds((2 * copy + side) * MODES, MODES), pl.ds(side * cols, cols)
            ]
            tables.append(pltpu.make_async_copy(bx_hbm.at[facts[0], copy // 2], target, sem.at[7 + copy, side]))
    for copy in loads + tables:
        copy.start()

    blank = jnp.zeros((MODES, cols), wide_ref.dtype)
    for block in range(6):
        wide_ref[block * MODES : (block + 1) * MODES, (1 - block % 2) * cols : (2 - block % 2) * cols] = blank
    zero = jnp.zeros((SUB, LANES), jnp.float32)
    for item in (1, 3):
        for level in range(levels):
            for tile in range(tiles + 1):
                ext_ref[item, level, tile, pl.ds(0, SUB)] = zero
                ext_ref[item, level, tile, pl.ds(main + rows + SUB, SUB)] = zero

    def place_slabs(odd):
        for phase, slab in enumerate((a_ref, b_ref)):
            base = GUARD if (odd == 1) == (phase == 0) else main + rows
            for item, place, turn in ((3, 0, 0), (1, 1, 0), (0, 2, 0), (2, 2, 4), (4, 3, 0), (5, 3, 4)):
                for level in range(levels):
                    for tile in range(tiles):
                        value = slab[level, place, :, tile * LANES : (tile + 1) * LANES]
                        if turn:
                            value = pltpu.roll(value, turn, 0)
                        ext_ref[item, level, tile, pl.ds(base, SUB)] = value

    for odd in range(2):
        pl.when(facts[6] == odd)(functools.partial(place_slabs, odd))
    edges = 6 * len({0, tiles - 1})
    for copy in loads[:edges]:
        copy.wait()

    lane = lax.broadcasted_iota(jnp.int32, (SUB, LANES), 1)

    def pack_band(band, right):
        def pack_rows(part, _):
            row = pl.multiple_of(part * SUB, SUB)
            packed = [jnp.zeros((SUB, LANES), jnp.float32) for _ in range(2)]
            for item, level, width, group, first in band_lanes(levels):
                tile = ext_ref[item, level, (tiles - 1) * right, pl.ds(row + GUARD, SUB)]
                moved = pltpu.roll(tile, (first + right * width) % LANES, 1)
                packed[group] = jnp.where((lane >= first) & (lane < first + width), moved, packed[group])
            for group in range(2):
                band[pl.ds(row, SUB), group * LANES : (group + 1) * LANES] = packed[group]
            return 0

        lax.fori_loop(0, rows // SUB + 2, pack_rows, 0)

    for index, band in enumerate(bands):
        for right in range(2):
            pl.when((facts[3] ^ index) == right)(functools.partial(pack_band, band, right))
    for copy in loads[edges:] + tables:
        copy.wait()


def substep_kernel(facts, *refs, step, levels, rows, cols):
    bands, ext_ref, d_ref = refs[1:-2], refs[-2], refs[-1]
    tiles = cols // LANES
    chunks = rows // SUB
    lane = lax.broadcasted_iota(jnp.int32, (SUB, LANES), 1)

    def unpack_bands(odd):
        def unpack_rows(part, _):
            row = pl.multiple_of(part * SUB, SUB)
            sources = [
                [band[pl.ds(row, SUB), group * LANES : (group + 1) * LANES] for group in range(2)] for band in bands
            ]
            for item, level, width, group, first in band_lanes(levels):
                value = jnp.zeros((SUB, LANES), jnp.float32)
                for phase, source in enumerate(sources):
                    left = odd if phase == 0 else 1 - odd
                    moved = pltpu.roll(source[group], (2 * LANES - first - left * width) % LANES, 1)
                    value = jnp.where(lane >= LANES - width if left else lane < width, moved, value)
                ext_ref[item, level, tiles, pl.ds(row + GUARD, SUB)] = value
            return 0

        lax.fori_loop(0, chunks + 2, unpack_rows, 0)

    if step == 0:
        for odd in range(2):
            pl.when(facts[5] == odd)(functools.partial(unpack_bands, odd))

    quarter = 0.5 * COURANT
    sides = [jnp.where(facts[place] == 1, 1.0, 0.0) for place in (7, 8, 9, 10)]
    has_left, has_right, has_top, has_bottom = sides
    inner = jnp.where(lane == LANES - 1, has_right, 1.0)
    outer = jnp.where(lane < LANES // 2, has_right, jnp.where(lane == LANES - 1, 1.0, has_left))
    ring = tiles + 1

    def ahead(values, tile, count):
        moved = jnp.where(lane < count, values[(tile + 1) % ring], values[tile])
        return pltpu.roll(moved, LANES - count, 1)

    def behind(values, tile, count):
        moved = jnp.where(lane >= LANES - count, values[(tile - 1) % ring], values[tile])
        return pltpu.roll(moved, count, 1)

    u_ref, v_ref, w_ref, p_ref, t_ref, s_ref = (ext_ref.at[item] for item in range(6))
    first, last = step == 0, step == SUBSTEPS - 1

    def flush(pending):
        for ref, level, tile, here, value in pending:
            ref[level, tile, here] = value

    def winds(chunk, only_v=False):
        row = GUARD + chunk * SUB
        here = pl.ds(row, SUB)
        x_tiles = tiles if last else ring
        limit = {0: has_top, chunks + 1: has_bottom}.get(chunk)
        before = None
        line = None if only_v else [p_ref[0, tile, here] for tile in range(ring)]
        for level in range(levels):
            made = []
            for tile in range(x_tiles):
                slope = p_ref[level, tile, pl.ds(row + 1, SUB)] - p_ref[level, tile, pl.ds(row - 1, SUB)]
                if first:
                    slope = slope * (quarter if limit is None else quarter * limit)
                elif limit is not None:
                    slope = slope * limit
                made.append((v_ref, level, tile, here, v_ref[level, tile, here] - slope))
            if only_v:
                flush(made)
                continue
            old = [u_ref[level, tile, here] for tile in range(ring)]
            fresh = []
            for tile in range(ring):
                slope = ahead(line, tile, 2) - line[tile]
                edge = {tiles - 1: inner, tiles: outer}.get(tile)
                if first:
                    slope = slope * (quarter if edge is None else quarter * edge)
                elif edge is not None:
                    slope = slope * edge
                fresh.append((ahead(old, tile, 1) if first else old[tile]) - slope)
            if last:
                for tile in range(tiles):
                    made.append((u_ref, level, tile, here, behind(fresh, tile, 1)))
                    made.append((d_ref, level, tile, here, fresh[tile] - behind(fresh, tile, 2)))
            else:
                for tile in range(ring):
                    made.append((u_ref, level, tile, here, fresh[tile]))
            after = None
            if level + 1 < levels:
                after = [p_ref[level + 1, tile, here] for tile in range(ring)]
            for tile in range(x_tiles):
                if level == 0:
                    lift = after[tile]
                elif level == levels - 1:
                    lift = -before[tile]
                else:
                    lift = after[tile] - before[tile]
                warm = t_ref[level, tile, here]
                if first:
                    lift, warm = quarter * lift, COURANT * warm
                made.append((w_ref, level, tile, here, w_ref[level, tile, here] - (lift - warm)))
            before, line = line, after
            flush(made)

    def scalars(chunk):
        row = GUARD + chunk * SUB
        here = pl.ds(row, SUB)
        x_tiles = tiles if last else ring
        before, now = None, [w_ref[0, tile, here] for tile in range(x_tiles)]
        for level in range(levels):
            made = []
            line = None if last else [u_ref[level, tile, here] for tile in range(ring)]
            after = None
            if level + 1 < levels:
                after = [w_ref[level + 1, tile, here] for tile in range(x_tiles)]
            for tile in range(x_tiles):
                if last:
                    spread = d_ref[level, tile, here]
                else:
                    spread = line[tile] - behind(line, tile, 2)
                spread += v_ref[level, tile, pl.ds(row + 1, SUB)] - v_ref[level, tile, pl.ds(row - 1, SUB)]
                if level == 0:
                    spread += after[tile]
                elif level == levels - 1:
                    spread -= before[tile]
                else:
                    spread += after[tile] - before[tile]
                press, warm, speed = (ref[level, tile, here] for ref in (p_ref, t_ref, s_ref))
                if first:
                    press, warm, speed = quarter * press, COURANT * warm, (quarter * quarter) * speed
                    made.append((s_ref, level, tile, here, speed))
                press = press - speed * spread
                warm = warm - (COURANT * COURANT) * now[tile]
                if last:
                    press, warm = press * (1.0 / quarter), warm * (1.0 / COURANT)
                made.append((p_ref, level, tile, here, press))
                made.append((t_ref, level, tile, here, warm))
            before, now = now, after
            flush(made)

    if last:
        winds(0, True)
        winds(chunks + 1, True)
    span = range(1, chunks + 1) if last else range(chunks + 2)
    for chunk in span:
        winds(chunk)
    for chunk in span:
        scalars(chunk)


def solution(mesh):
    nx, ny = mesh.shape["gx"], mesh.shape["gy"]
    devices = nx * ny
    stages, middle = stages_of(devices)
    pieces = 1
    for stage in stages:
        pieces *= 1 << len(stage)
    pieces = max(pieces, 2)

    def decode(ref):
        number = ref[0]
        gx, gy = lax.div(number, ny), lax.rem(number, ny)
        mine = 0
        for stage in stages:
            for bit in reversed(stage):
                mine = mine * 2 + ((number >> bit) & 1)
        return (
            gx,
            gy,
            mine,
            (gx + 1) % 2,
            (gy + 1) % 2,
            gx % 2,
            gy % 2,
            jnp.where(gx > 0, 1, 0),
            jnp.where(gx < nx - 1, 1, 0),
            jnp.where(gy > 0, 1, 0),
            jnp.where(gy < ny - 1, 1, 0),
        )

    def informed(kernel, **static):
        def body(info, *refs):
            return kernel(decode(info), *refs, **static)

        return body

    x_phases = 1 if nx == 2 else 2

    def swap(value, mask):
        return lax.ppermute(value, ("gx", "gy"), [(i, i ^ mask) for i in range(devices)])

    def neighbours(value, axis, count, phase):
        pairs = []
        for low in range(phase, count - 1, 2):
            pairs += [(low, low + 1), (low + 1, low)]
        return lax.ppermute(value, axis, pairs)

    def on_device(state, driving, rate, sound_square):
        fields, levels, rows, cols = state.shape
        half = levels // 2
        chunk = half * MODES // pieces
        info = (lax.axis_index("gx") * ny + lax.axis_index("gy")).reshape(1)

        basis_x, weight_x = bases(MODES, cols * nx)
        basis_y, weight_y = bases(MODES, rows * ny)
        high, low = halves(weight_x)
        wx = np.concatenate([high, low], axis=0).T.reshape(nx, cols, 2 * MODES)
        high, low = halves(weight_y)
        wy = np.concatenate([high, low], axis=0).reshape(2 * MODES, ny, rows).transpose(1, 0, 2)
        high, low = halves(basis_x)
        bx = np.stack([high, low]).reshape(2, MODES, nx, cols).transpose(2, 0, 1, 3)
        high, low = halves(basis_y)
        by = np.stack([high, low]).reshape(2, MODES, ny, rows).transpose(2, 0, 3, 1).reshape(ny, 2 * rows, MODES)
        wx, wy, bx, by = (jnp.asarray(np.ascontiguousarray(t)) for t in (wx, wy, bx, by))

        hbm = pl.BlockSpec(memory_space=pltpu.HBM)
        vmem = pl.BlockSpec(memory_space=pltpu.VMEM)

        def call(kernel, name, shapes, ins, scratch, operands, flops=0, data=0, prefetch=1, aliases=None):
            return pl.pallas_call(
                kernel,
                grid_spec=pltpu.PrefetchScalarGridSpec(
                    num_scalar_prefetch=prefetch,
                    grid=(),
                    in_specs=ins,
                    out_specs=[vmem if name != "nudge" else hbm for _ in shapes],
                    scratch_shapes=scratch,
                ),
                out_shape=shapes,
                input_output_aliases=aliases or {},
                compiler_params=pltpu.CompilerParams(vmem_limit_bytes=VMEM_LIMIT),
                cost_estimate=pl.CostEstimate(flops=flops, bytes_accessed=data, transcendentals=0),
            )(*operands)

        def array(shape, dtype=jnp.float32):
            return jax.ShapeDtypeStruct(shape, dtype)

        tiles = cols // LANES
        slab_shape = (levels, 4, SUB, cols)
        slab_a, slab_b = call(
            informed(slab_kernel),
            "slabs",
            [array(slab_shape)] * 2,
            [hbm, hbm],
            [pltpu.VMEM((2, 2, levels, SUB, cols), jnp.float32), pltpu.SemaphoreType.DMA((2, 6))],
            (info, state, sound_square),
        )
        slab_a = neighbours(slab_a, "gy", ny, 0)
        slab_b = neighbours(slab_b, "gy", ny, 1)

        piece_shape = (pieces // 2, fields, chunk, LANES)
        keep, send = call(
            informed(project_kernel),
            "project",
            [array(piece_shape)] * 2,
            [hbm] * 4,
            [
                pltpu.VMEM((fields, levels, rows, cols), jnp.float32),
                pltpu.VMEM((fields, levels, rows, cols), jnp.float32),
                pltpu.VMEM((cols, 2 * MODES), jnp.bfloat16),
                pltpu.VMEM((2 * MODES, rows), jnp.bfloat16),
                pltpu.VMEM((fields, half * rows, 2 * LANES), jnp.bfloat16),
                pltpu.VMEM((fields, half * MODES, LANES), jnp.float32),
                pltpu.SemaphoreType.DMA((fields + 1, 2)),
            ],
            (info, state, driving, wx, wy),
            600_000_000,
            8_500_000,
        )

        ext_shape = (6, levels, tiles + 1, rows + 2 * SUB + 2 * GUARD, LANES)
        band_shape = (rows + 2 * SUB, 2 * LANES)
        ext, wide, back, *bands = call(
            informed(load_kernel),
            "load",
            [
                array(ext_shape),
                array((6 * MODES, 2 * cols), jnp.bfloat16),
                array((2 * rows, MODES), jnp.bfloat16),
            ]
            + [array(band_shape)] * x_phases,
            [hbm, hbm, vmem, vmem, hbm, hbm],
            [pltpu.SemaphoreType.DMA((10, max(tiles, 2)))],
            (info, state, sound_square, slab_a, slab_b, bx, by),
            1_000_000,
            10_000_000,
        )
        bands = [neighbours(band, "gx", nx, index) for index, band in enumerate(bands)]

        for step in range(SUBSTEPS):
            extra = bands if step == 0 else []
            (ext,) = call(
                informed(substep_kernel, step=step, levels=levels, rows=rows, cols=cols),
                f"substep_{step}",
                [array(ext_shape)],
                [vmem] * (1 + len(extra)),
                [pltpu.VMEM(ext_shape[1:], jnp.float32)],
                (info, ext, *extra),
                10_000_000,
                8_000_000,
                aliases={1: 0},
            )

        value = None
        for place, stage in enumerate(stages):
            masks = masks_of(stage)
            if place == 0:
                value = keep + swap(send, masks[1])
                continue
            value = value.reshape((len(masks), value.shape[0] // len(masks)) + value.shape[1:])
            moved = [swap(value[i], masks[i]) for i in range(1, len(masks))]
            value = functools.reduce(jnp.add, moved, value[0])
        moved = [swap(value, mask) for i, mask in enumerate(masks_of(middle)) if i]
        value = functools.reduce(jnp.add, moved, value)
        for place in reversed(range(1, len(stages))):
            moved = [swap(value, mask) for i, mask in enumerate(masks_of(stages[place])) if i]
            value = jnp.concatenate([value] + moved, axis=0)
        far = swap(value, masks_of(stages[0])[1])

        (out,) = call(
            informed(nudge_kernel),
            "nudge",
            [array(state.shape)],
            [vmem] * 5,
            [
                pltpu.VMEM((fields, half * MODES, LANES), jnp.float32),
                pltpu.VMEM((fields, half * rows, 2 * LANES), jnp.bfloat16),
                pltpu.VMEM((fields, levels, rows, cols), jnp.float32),
                pltpu.SemaphoreType.DMA((fields,)),
            ],
            (info, rate, ext, value, far, wide, back),
            600_000_000,
            8_500_000,
            prefetch=2,
        )
        return out

    return jax.shard_map(
        on_device,
        mesh=mesh,
        in_specs=(P(None, None, "gy", "gx"), P(None, None, "gy", "gx"), P(), P(None, "gy", "gx")),
        out_specs=P(None, None, "gy", "gx"),
        check_vma=False,
    )
```

profile of v0, /device:TPU:2, one launch (start us, length us, event | category | flops | bytes accessed | tf_op | source)
XLA Modules:
  0.0 66.1 jit_solution(10447090975279867471)
XLA Ops:
  0.0 2.1 %copy-done = f32[5,8,64,384]{3,2,1,0:T(8,128)S(1)} copy-done((f32[5,8,64,384]{3,2,1,0:T(8,128)S(1)}, f32[5,8,64,384]{3,2,1,0:T(8,128)}, u32[]{:S(2)}) %copy-start) | copy-done | bytes 3932184
  2.1 2.1 %copy-done.1 = f32[5,8,64,384]{3,2,1,0:T(8,128)S(1)} copy-done((f32[5,8,64,384]{3,2,1,0:T(8,128)S(1)}, f32[5,8,64,384]{3,2,1,0:T(8,128)}, u32[]{:S(2)}) %copy-start.1) | copy-done | bytes 3932184
  4.2 1.0 %copy-done.4 = bf16[16,128,64]{2,1,0:T(8,128)(2,1)S(1)} copy-done((bf16[16,128,64]{2,1,0:T(8,128)(2,1)S(1)}, bf16[16,128,64]{2,1,0:T(8,128)(2,1)}, u32[]{:S(2)}) %copy-start.4) | copy-done | bytes 262168
  5.3 0.9 %copy-done.6 = bf16[2,384,128]{2,1,0:T(8,128)(2,1)S(1)} copy-done((bf16[2,384,128]{2,1,0:T(8,128)(2,1)S(1)}, bf16[2,384,128]{2,1,0:T(8,128)(2,1)}, u32[]{:S(2)}) %copy-start.6) | copy-done | bytes 196632
  6.2 3.3 %shard_map.87 = (f32[4,5,32,128]{3,2,1,0:T(8,128)S(1)}, f32[4,5,32,128]{3,2,1,0:T(8,128)S(1)}) custom-call(s32[1]{0:T(128)} %bitcast.info, f32[5,8,64,384]{3,2,1,0:T(8,128)S(1)} %copy-done, f32[5,8,64,384]{3,2,1,0:T(8,128)S(1)} %copy-done.1, bf16[2,384,128]{2,1,0:T(8,128)(2,1)S(1)} %copy-done.6, bf16[16,128,64]{2,1,0:T(8,128)(2,1)S(1)} %copy-done.4), custom_call_target="tpu_custom_call" | custom-call | flops 600000000 | bytes 8500000 | tf_op jit(solution)/shard_map/pallas_call | solution.py:504
  9.6 1.6 %collective-permute-done.3 = f32[4,5,32,128]{3,2,1,0:T(8,128)S(1)} collective-permute-done((f32[4,5,32,128]{3,2,1,0:T(8,128)S(1)}, f32[4,5,32,128]{3,2,1,0:T(8,128)S(1)}, u32[]{:S(2)}, u32[]{:S(2)}) %collective-permute-start.3) | collective-permute-done | bytes 327712 | tf_op jit(solution)/shard_map/ppermute | solution.py:474
  11.3 1.6 %collective-permute-start.6 = (f32[1,5,32,128]{3,2,1,0:T(8,128)S(1)}, f32[1,5,32,128]{3,2,1,0:T(8,128)S(1)}, u32[]{:S(2)}, u32[]{:S(2)}) collective-permute-start(f32[1,5,32,128]{3,2,1,0:T(8,128)S(1)} %get-tuple-element.22), channel_id=1, source_target_pairs={{0,18},{1,19},{2,16},{3,17},{4,22},{5,23},{6,20},{7,21},{8,26},{9,... | collective-permute-start | bytes 245768 | tf_op jit(solution)/shard_map/ppermute | solution.py:474
  13.0 1.9 %collective-permute-start.4 = (f32[1,5,32,128]{3,2,1,0:T(8,128)S(1)}, f32[1,5,32,128]{3,2,1,0:T(8,128)S(1)}, u32[]{:S(2)}, u32[]{:S(2)}) collective-permute-start(f32[1,5,32,128]{3,2,1,0:T(8,128)S(1)} %get-tuple-element.21), channel_id=1, source_target_pairs={{0,2},{1,3},{2,0},{3,1},{4,6},{5,7},{6,4},{7,5},{8,10},{9,11},{10,... | collective-permute-start | bytes 245768 | tf_op jit(solution)/shard_map/ppermute | solution.py:474
  14.9 2.2 %collective-permute-done.6 = f32[1,5,32,128]{3,2,1,0:T(8,128)S(1)} collective-permute-done((f32[1,5,32,128]{3,2,1,0:T(8,128)S(1)}, f32[1,5,32,128]{3,2,1,0:T(8,128)S(1)}, u32[]{:S(2)}, u32[]{:S(2)}) %collective-permute-start.6) | collective-permute-done | bytes 81952 | tf_op jit(solution)/shard_map/ppermute | solution.py:474
  17.0 1.5 %collective-permute-done.5 = f32[1,5,32,128]{3,2,1,0:T(8,128)S(1)} collective-permute-done((f32[1,5,32,128]{3,2,1,0:T(8,128)S(1)}, f32[1,5,32,128]{3,2,1,0:T(8,128)S(1)}, u32[]{:S(2)}, u32[]{:S(2)}) %collective-permute-start.5) | collective-permute-done | bytes 81952 | tf_op jit(solution)/shard_map/ppermute | solution.py:474
  18.6 3.7 %collective-permute-start.9 = (f32[1,5,32,128]{3,2,1,0:T(8,128)S(1)}, f32[1,5,32,128]{3,2,1,0:T(8,128)S(1)}, u32[]{:S(2)}, u32[]{:S(2)}) collective-permute-start(f32[1,5,32,128]{3,2,1,0:T(8,128)S(1)} %fusion.1), channel_id=1, source_target_pairs={{0,12},{1,13},{2,14},{3,15},{4,8},{5,9},{6,10},{7,11},{8,4},{9,5},... | collective-permute-start | bytes 245768 | tf_op jit(solution)/shard_map/ppermute | solution.py:474
  22.3 0.8 %collective-permute-start.7 = (f32[1,5,32,128]{3,2,1,0:T(8,128)S(1)}, f32[1,5,32,128]{3,2,1,0:T(8,128)S(1)}, u32[]{:S(2)}, u32[]{:S(2)}) collective-permute-start(f32[1,5,32,128]{3,2,1,0:T(8,128)S(1)} %fusion.1), channel_id=1, source_target_pairs={{0,4},{1,5},{2,6},{3,7},{4,0},{5,1},{6,2},{7,3},{8,12},{9,13},{10,... | collective-permute-start | bytes 245768 | tf_op jit(solution)/shard_map/ppermute | solution.py:474
  23.0 2.4 %collective-permute-done.9 = f32[1,5,32,128]{3,2,1,0:T(8,128)S(1)} collective-permute-done((f32[1,5,32,128]{3,2,1,0:T(8,128)S(1)}, f32[1,5,32,128]{3,2,1,0:T(8,128)S(1)}, u32[]{:S(2)}, u32[]{:S(2)}) %collective-permute-start.9) | collective-permute-done | bytes 81952 | tf_op jit(solution)/shard_map/ppermute | solution.py:474
  25.4 3.8 %collective-permute-done.8 = f32[1,5,32,128]{3,2,1,0:T(8,128)S(1)} collective-permute-done((f32[1,5,32,128]{3,2,1,0:T(8,128)S(1)}, f32[1,5,32,128]{3,2,1,0:T(8,128)S(1)}, u32[]{:S(2)}, u32[]{:S(2)}) %collective-permute-start.8) | collective-permute-done | bytes 81952 | tf_op jit(solution)/shard_map/ppermute | solution.py:474
  29.3 1.6 %collective-permute-start.12 = (f32[1,5,32,128]{3,2,1,0:T(8,128)S(1)}, f32[1,5,32,128]{3,2,1,0:T(8,128)S(1)}, u32[]{:S(2)}, u32[]{:S(2)}) collective-permute-start(f32[1,5,32,128]{3,2,1,0:T(8,128)S(1)} %add_add_fusion), channel_id=1, source_target_pairs={{0,18},{1,19},{2,16},{3,17},{4,22},{5,23},{6,20},{7,21},{8,26},{9,... | collective-permute-start | bytes 245768 | tf_op jit(solution)/shard_map/ppermute | solution.py:474
  30.8 2.0 %collective-permute-start.10 = (f32[1,5,32,128]{3,2,1,0:T(8,128)S(1)}, f32[1,5,32,128]{3,2,1,0:T(8,128)S(1)}, u32[]{:S(2)}, u32[]{:S(2)}) collective-permute-start(f32[1,5,32,128]{3,2,1,0:T(8,128)S(1)} %add_add_fusion), channel_id=1, source_target_pairs={{0,2},{1,3},{2,0},{3,1},{4,6},{5,7},{6,4},{7,5},{8,10},{9,11},{10,... | collective-permute-start | bytes 245768 | tf_op jit(solution)/shard_map/ppermute | solution.py:474
  33.3 2.0 %collective-permute-start.1 = (f32[8,4,8,384]{3,2,1,0:T(8,128)S(1)}, f32[8,4,8,384]{3,2,1,0:T(8,128)S(1)}, u32[]{:S(2)}, u32[]{:S(2)}) collective-permute-start(f32[8,4,8,384]{3,2,1,0:T(8,128)S(1)} %get-tuple-element.14), channel_id=1, source_target_pairs={{1,2},{2,1},{3,4},{4,3},{5,6},{6,5},{7,8},{8,7},{9,10},{10,9},{11,... | collective-permute-start | bytes 1179656 | tf_op jit(solution)/shard_map/ppermute | solution.py:480
  36.0 10.6 %collective-permute-done.1.refs_3_ = f32[8,4,8,384]{3,2,1,0:T(8,128)S(1)} collective-permute-done((f32[8,4,8,384]{3,2,1,0:T(8,128)S(1)}, f32[8,4,8,384]{3,2,1,0:T(8,128)S(1)}, u32[]{:S(2)}, u32[]{:S(2)}) %collective-permute-start.1) | collective-permute-done | bytes 393248 | tf_op jit(solution)/shard_map/ppermute | solution.py:480
  46.6 2.1 %shard_map.83 = (f32[6,8,4,96,128]{4,3,2,1,0:T(8,128)S(1)}, bf16[384,768]{1,0:T(8,128)(2,1)S(1)}, bf16[128,64]{1,0:T(8,128)(2,1)S(1)}, f32[80,256]{1,0:T(8,128)S(1)}) custom-call(s32[1]{0:T(128)} %bitcast.info, f32[5,8,64,384]{3,2,1,0:T(8,128)S(1)} %copy-done, f32[8,64,384]{2,1,0:T(8,128)S(1)} %copy-done.2, ...), custom_call_target="tpu_custom_call" | custom-call | flops 1000000 | bytes 10000000 | tf_op jit(solution)/shard_map/pallas_call | solution.py:504
  49.2 4.0 %collective-permute-done.2.refs_1_ = f32[80,256]{1,0:T(8,128)S(1)} collective-permute-done((f32[80,256]{1,0:T(8,128)S(1)}, f32[80,256]{1,0:T(8,128)S(1)}, u32[]{:S(2)}, u32[]{:S(2)}) %collective-permute-start.2) | collective-permute-done | bytes 81952 | tf_op jit(solution)/shard_map/ppermute | solution.py:480
  53.3 3.3 %shard_map.84.refs_0_ = f32[6,8,4,96,128]{4,3,2,1,0:T(8,128)S(1)} custom-call(s32[1]{0:T(128)} %bitcast.info, f32[6,8,4,96,128]{4,3,2,1,0:T(8,128)S(1)} %get-tuple-element.15.refs_0_, f32[80,256]{1,0:T(8,128)S(1)} %collective-permute-done.2.refs_1_), custom_call_target="tpu_custom_call", output_to_operand_aliasing={{}: (1, {})} | custom-call | flops 10000000 | bytes 8000000 | tf_op jit(solution)/shard_map/pallas_call | solution.py:504
  56.6 1.8 %shard_map.85.refs_0_ = f32[6,8,4,96,128]{4,3,2,1,0:T(8,128)S(1)} custom-call(s32[1]{0:T(128)} %bitcast.info, f32[6,8,4,96,128]{4,3,2,1,0:T(8,128)S(1)} %shard_map.84.refs_0_), custom_call_target="tpu_custom_call", output_to_operand_aliasing={{}: (1, {})} | custom-call | flops 10000000 | bytes 8000000 | tf_op jit(solution)/shard_map/pallas_call | solution.py:504
  58.4 4.4 %shard_map.86.refs_1_ = f32[6,8,4,96,128]{4,3,2,1,0:T(8,128)S(1)} custom-call(s32[1]{0:T(128)} %bitcast.info, f32[6,8,4,96,128]{4,3,2,1,0:T(8,128)S(1)} %shard_map.85.refs_0_), custom_call_target="tpu_custom_call", output_to_operand_aliasing={{}: (1, {})} | custom-call | flops 10000000 | bytes 8000000 | tf_op jit(solution)/shard_map/pallas_call | solution.py:504
  62.8 3.3 %shard_map.88 = f32[5,8,64,384]{3,2,1,0:T(8,128)} custom-call(s32[1]{0:T(128)} %bitcast.info, f32[5,8]{1,0:T(8,128)S(1)} %copy-done.7, f32[6,8,4,96,128]{4,3,2,1,0:T(8,128)S(1)} %shard_map.86.refs_1_, f32[4,5,32,128]{3,2,1,0:T(8,128)S(1)} %pad_maximum_fusion.refs_2_, f32[4,5,32,128]{3,2,1,0:T(8,128)S(1)} %collective-permute-done.13.refs_3_, ...), custom_call_target="tpu_custom_call" | custom-call | flops 600000000 | bytes 8500000 | tf_op jit(solution)/shard_map/pallas_call | solution.py:504
  (32 shorter events, 1.9 us)
Async XLA Ops:
  0.0 2.1 %copy-start = (f32[5,8,64,384]{3,2,1,0:T(8,128)S(1)}, f32[5,8,64,384]{3,2,1,0:T(8,128)}, u32[]{:S(2)}) copy-start(f32[5,8,64,384]{3,2,1,0:T(8,128)} %refs_0_.6) | copy-start | bytes 11796484
  2.1 2.1 %copy-start.1 = (f32[5,8,64,384]{3,2,1,0:T(8,128)S(1)}, f32[5,8,64,384]{3,2,1,0:T(8,128)}, u32[]{:S(2)}) copy-start(f32[5,8,64,384]{3,2,1,0:T(8,128)} %refs_1_.5) | copy-start | bytes 11796484
  4.2 1.0 %copy-start.4 = (bf16[16,128,64]{2,1,0:T(8,128)(2,1)S(1)}, bf16[16,128,64]{2,1,0:T(8,128)(2,1)}, u32[]{:S(2)}) copy-start(bf16[16,128,64]{2,1,0:T(8,128)(2,1)} %constant.20.clone.refs_3_) | copy-start | bytes 786436
  5.3 0.9 %copy-start.6 = (bf16[2,384,128]{2,1,0:T(8,128)(2,1)S(1)}, bf16[2,384,128]{2,1,0:T(8,128)(2,1)}, u32[]{:S(2)}) copy-start(bf16[2,384,128]{2,1,0:T(8,128)(2,1)} %constant.19.clone.refs_2_) | copy-start | bytes 589828
  6.2 26.6 %copy-start.2 = (f32[8,64,384]{2,1,0:T(8,128)S(1)}, f32[8,64,384]{2,1,0:T(8,128)}, u32[]{:S(2)}) copy-start(f32[8,64,384]{2,1,0:T(8,128)} %refs_1_.4) | copy-start | bytes 2359300
  6.2 40.4 %copy-start.3 = (bf16[16,128,64]{2,1,0:T(8,128)(2,1)S(1)}, bf16[16,128,64]{2,1,0:T(8,128)(2,1)}, u32[]{:S(2)}) copy-start(bf16[16,128,64]{2,1,0:T(8,128)(2,1)} %constant.22.clone.refs_5_) | copy-start | bytes 786436
  6.2 40.4 %copy-start.5 = (bf16[2,2,64,384]{3,2,1,0:T(8,128)(2,1)S(1)}, bf16[2,2,64,384]{3,2,1,0:T(8,128)(2,1)}, u32[]{:S(2)}) copy-start(bf16[2,2,64,384]{3,2,1,0:T(8,128)(2,1)} %constant.21.clone.refs_4_) | copy-start | bytes 589828
  9.5 1.7 %collective-permute-start.3 = (f32[4,5,32,128]{3,2,1,0:T(8,128)S(1)}, f32[4,5,32,128]{3,2,1,0:T(8,128)S(1)}, u32[]{:S(2)}, u32[]{:S(2)}) collective-permute-start(f32[4,5,32,128]{3,2,1,0:T(8,128)S(1)} %get-tuple-element.18), channel_id=1, source_target_pairs={{0,1},{1,0},{2,3},{3,2},{4,5},{5,4},{6,7},{7,6},{8,9},{9,8},{10,11... | collective-permute-start | bytes 983048 | tf_op jit(solution)/shard_map/ppermute | solution.py:474
  11.3 5.7 %collective-permute-start.6 = (f32[1,5,32,128]{3,2,1,0:T(8,128)S(1)}, f32[1,5,32,128]{3,2,1,0:T(8,128)S(1)}, u32[]{:S(2)}, u32[]{:S(2)}) collective-permute-start(f32[1,5,32,128]{3,2,1,0:T(8,128)S(1)} %get-tuple-element.22), channel_id=1, source_target_pairs={{0,18},{1,19},{2,16},{3,17},{4,22},{5,23},{6,20},{7,21},{8,26},{9,... | collective-permute-start | bytes 245768 | tf_op jit(solution)/shard_map/ppermute | solution.py:474
  12.9 5.6 %collective-permute-start.5 = (f32[1,5,32,128]{3,2,1,0:T(8,128)S(1)}, f32[1,5,32,128]{3,2,1,0:T(8,128)S(1)}, u32[]{:S(2)}, u32[]{:S(2)}) collective-permute-start(f32[1,5,32,128]{3,2,1,0:T(8,128)S(1)} %get-tuple-element.23), channel_id=1, source_target_pairs={{0,16},{1,17},{2,18},{3,19},{4,20},{5,21},{6,22},{7,23},{8,24},{9,... | collective-permute-start | bytes 245768 | tf_op jit(solution)/shard_map/ppermute | solution.py:474
  13.0 5.6 %collective-permute-start.4 = (f32[1,5,32,128]{3,2,1,0:T(8,128)S(1)}, f32[1,5,32,128]{3,2,1,0:T(8,128)S(1)}, u32[]{:S(2)}, u32[]{:S(2)}) collective-permute-start(f32[1,5,32,128]{3,2,1,0:T(8,128)S(1)} %get-tuple-element.21), channel_id=1, source_target_pairs={{0,2},{1,3},{2,0},{3,1},{4,6},{5,7},{6,4},{7,5},{8,10},{9,11},{10,... | collective-permute-start | bytes 245768 | tf_op jit(solution)/shard_map/ppermute | solution.py:474
  18.6 6.8 %collective-permute-start.9 = (f32[1,5,32,128]{3,2,1,0:T(8,128)S(1)}, f32[1,5,32,128]{3,2,1,0:T(8,128)S(1)}, u32[]{:S(2)}, u32[]{:S(2)}) collective-permute-start(f32[1,5,32,128]{3,2,1,0:T(8,128)S(1)} %fusion.1), channel_id=1, source_target_pairs={{0,12},{1,13},{2,14},{3,15},{4,8},{5,9},{6,10},{7,11},{8,4},{9,5},... | collective-permute-start | bytes 245768 | tf_op jit(solution)/shard_map/ppermute | solution.py:474
  22.3 7.0 %collective-permute-start.8 = (f32[1,5,32,128]{3,2,1,0:T(8,128)S(1)}, f32[1,5,32,128]{3,2,1,0:T(8,128)S(1)}, u32[]{:S(2)}, u32[]{:S(2)}) collective-permute-start(f32[1,5,32,128]{3,2,1,0:T(8,128)S(1)} %fusion.1), channel_id=1, source_target_pairs={{0,8},{1,9},{2,10},{3,11},{4,12},{5,13},{6,14},{7,15},{8,0},{9,1},... | collective-permute-start | bytes 245768 | tf_op jit(solution)/shard_map/ppermute | solution.py:474
  22.3 7.0 %collective-permute-start.7 = (f32[1,5,32,128]{3,2,1,0:T(8,128)S(1)}, f32[1,5,32,128]{3,2,1,0:T(8,128)S(1)}, u32[]{:S(2)}, u32[]{:S(2)}) collective-permute-start(f32[1,5,32,128]{3,2,1,0:T(8,128)S(1)} %fusion.1), channel_id=1, source_target_pairs={{0,4},{1,5},{2,6},{3,7},{4,0},{5,1},{6,2},{7,3},{8,12},{9,13},{10,... | collective-permute-start | bytes 245768 | tf_op jit(solution)/shard_map/ppermute | solution.py:474
  29.3 6.3 %collective-permute-start.12 = (f32[1,5,32,128]{3,2,1,0:T(8,128)S(1)}, f32[1,5,32,128]{3,2,1,0:T(8,128)S(1)}, u32[]{:S(2)}, u32[]{:S(2)}) collective-permute-start(f32[1,5,32,128]{3,2,1,0:T(8,128)S(1)} %add_add_fusion), channel_id=1, source_target_pairs={{0,18},{1,19},{2,16},{3,17},{4,22},{5,23},{6,20},{7,21},{8,26},{9,... | collective-permute-start | bytes 245768 | tf_op jit(solution)/shard_map/ppermute | solution.py:474
  30.8 5.0 %collective-permute-start.11 = (f32[1,5,32,128]{3,2,1,0:T(8,128)S(1)}, f32[1,5,32,128]{3,2,1,0:T(8,128)S(1)}, u32[]{:S(2)}, u32[]{:S(2)}) collective-permute-start(f32[1,5,32,128]{3,2,1,0:T(8,128)S(1)} %add_add_fusion), channel_id=1, source_target_pairs={{0,16},{1,17},{2,18},{3,19},{4,20},{5,21},{6,22},{7,23},{8,24},{9,... | collective-permute-start | bytes 245768 | tf_op jit(solution)/shard_map/ppermute | solution.py:474
  30.8 5.0 %collective-permute-start.10 = (f32[1,5,32,128]{3,2,1,0:T(8,128)S(1)}, f32[1,5,32,128]{3,2,1,0:T(8,128)S(1)}, u32[]{:S(2)}, u32[]{:S(2)}) collective-permute-start(f32[1,5,32,128]{3,2,1,0:T(8,128)S(1)} %add_add_fusion), channel_id=1, source_target_pairs={{0,2},{1,3},{2,0},{3,1},{4,6},{5,7},{6,4},{7,5},{8,10},{9,11},{10,... | collective-permute-start | bytes 245768 | tf_op jit(solution)/shard_map/ppermute | solution.py:474
  33.2 2.7 %collective-permute-start = (f32[8,4,8,384]{3,2,1,0:T(8,128)S(1)}, f32[8,4,8,384]{3,2,1,0:T(8,128)S(1)}, u32[]{:S(2)}, u32[]{:S(2)}) collective-permute-start(f32[8,4,8,384]{3,2,1,0:T(8,128)S(1)} %get-tuple-element.13), channel_id=1, source_target_pairs={{0,1},{1,0},{2,3},{3,2},{4,5},{5,4},{6,7},{7,6},{8,9},{9,8},{10,11... | collective-permute-start | bytes 1179656 | tf_op jit(solution)/shard_map/ppermute | solution.py:480
  33.3 13.3 %collective-permute-start.1 = (f32[8,4,8,384]{3,2,1,0:T(8,128)S(1)}, f32[8,4,8,384]{3,2,1,0:T(8,128)S(1)}, u32[]{:S(2)}, u32[]{:S(2)}) collective-permute-start(f32[8,4,8,384]{3,2,1,0:T(8,128)S(1)} %get-tuple-element.14), channel_id=1, source_target_pairs={{1,2},{2,1},{3,4},{4,3},{5,6},{6,5},{7,8},{8,7},{9,10},{10,9},{11,... | collective-permute-start | bytes 1179656 | tf_op jit(solution)/shard_map/ppermute | solution.py:480
  35.9 26.9 %collective-permute-start.13 = (f32[4,5,32,128]{3,2,1,0:T(8,128)S(1)}, f32[4,5,32,128]{3,2,1,0:T(8,128)S(1)}, u32[]{:S(2)}, u32[]{:S(2)}) collective-permute-start(f32[4,5,32,128]{3,2,1,0:T(8,128)S(1)} %pad_maximum_fusion.refs_2_), channel_id=1, source_target_pairs={{0,1},{1,0},{2,3},{3,2},{4,5},{5,4},{6,7},{7,6},{8,9},{9,8},{10,11... | collective-permute-start | bytes 983048 | tf_op jit(solution)/shard_map/ppermute | solution.py:474
  48.8 4.5 %collective-permute-start.2 = (f32[80,256]{1,0:T(8,128)S(1)}, f32[80,256]{1,0:T(8,128)S(1)}, u32[]{:S(2)}, u32[]{:S(2)}) collective-permute-start(f32[80,256]{1,0:T(8,128)S(1)} %get-tuple-element.16), channel_id=1, source_target_pairs={{0,16},{16,0},{1,17},{17,1},{2,18},{18,2},{3,19},{19,3},{4,20},{20... | collective-permute-start | bytes 245768 | tf_op jit(solution)/shard_map/ppermute | solution.py:480
  58.4 4.4 %copy-start.7 = (f32[5,8]{1,0:T(8,128)S(1)}, f32[5,8]{1,0:T(8,128)}, u32[]{:S(2)}) copy-start(f32[5,8]{1,0:T(8,128)} %refs_0_.7) | copy-start | bytes 484
where the time goes:
time: 66.4 us; the launch traced here: 66.1 us
  waiting for transfers between devices  26.7 us (40%)
  Pallas kernels  18.7 us (28%)
  starting transfers between devices  14.3 us (22%)
  local copies, waits for them, and re-layouts  6.23 us (9%)
    pallas_call x7, Pallas kernels, call(): pl.pallas_call(kernel, grid_spec=pltpu.PrefetchScalarGridSpec(num_scalar_...  18.7 us
    ppermute x3, waiting for transfers between devices, neighbours(): return lax.ppermute(value, axis, pairs)  14.7 us
    ppermute x11, waiting for transfers between devices, swap(): lax.ppermute(value, ('gx', 'gy'), [(i, i ^ mask) for i in range(devices)])  12.1 us
    ppermute x11, starting transfers between devices, swap(): lax.ppermute(value, ('gx', 'gy'), [(i, i ^ mask) for i in range(devices)])  11.7 us
    unnamed x16, local copies, waits for them, and re-layouts  6.21 us
    ppermute x3, starting transfers between devices, neighbours(): return lax.ppermute(value, axis, pairs)  2.56 us
  transfers between devices with their start and end apart: 14, of which 10 were waited for; matrix products, arithmetic and copies ran while one was open for 0% of the time, Pallas kernels for 18%

commit v1 on v0

--- a/solution.py
+++ b/solution.py
@@ -79,86 +79,104 @@
     return stages, left
 
 
-def slab_kernel(facts, state_ref, sound_ref, a_ref, b_ref, extra_ref, sem):
-    levels, _, _, cols = a_ref.shape
-    rows = state_ref.shape[2]
-    bottom = facts[4]
-    copies = []
-    for phase, out_ref in enumerate((a_ref, b_ref)):
-        last = bottom if phase == 0 else 1 - bottom
-        here = pl.ds(pl.multiple_of(last * (rows - SUB), SUB), SUB)
-        for place, (source, target) in enumerate(
-            (
-                (state_ref.at[3], out_ref.at[:, 0]),
-                (state_ref.at[1], out_ref.at[:, 1]),
-                (state_ref.at[0], out_ref.at[:, 2]),
-                (state_ref.at[4], out_ref.at[:, 3]),
-                (state_ref.at[2], extra_ref.at[phase, 0]),
-                (sound_ref, extra_ref.at[phase, 1]),
-            )
-        ):
-            copies.append(pltpu.make_async_copy(source.at[:, here], target, sem.at[phase, place]))
-    for copy in copies:
-        copy.start()
-    for copy in copies:
-        copy.wait()
-    index = lax.broadcasted_iota(jnp.int32, (SUB, cols), 0)
-    for phase, out_ref in enumerate((a_ref, b_ref)):
-        last = bottom if phase == 0 else 1 - bottom
-        own = (index // 4) == last
-        for level in range(levels):
-            for place in range(2):
-                turned = pltpu.roll(extra_ref[phase, place, level], 4, 0)
-                out_ref[level, 2 + place] = jnp.where(own, out_ref[level, 2 + place], turned)
-
-
-def project_kernel(
-    facts, state_ref, driving_ref, wx_hbm, wy_hbm, keep_ref, send_ref, held, other, wx_ref, wy_ref, packed_ref, modes_ref, sem
+def head_kernel(
+    facts,
+    state_ref,
+    driving_ref,
+    sound_ref,
+    wx_hbm,
+    wy_hbm,
+    ext_ref,
+    a_ref,
+    b_ref,
+    keep_ref,
+    send_ref,
+    other_ref,
+    wx_ref,
+    wy_ref,
+    packed_ref,
+    modes_ref,
+    sem,
 ):
     fields, levels, rows, cols = state_ref.shape
+    tiles = cols // LANES
     half = levels // 2
     pieces = 2 * keep_ref.shape[0]
     chunk = keep_ref.shape[2]
+    main = pl.ds(GUARD + SUB, rows)
+
+    def fetch(item):
+        source = state_ref.at[item] if item < fields else sound_ref
+        copies = [
+            pltpu.make_async_copy(
+                source.at[:, :, pl.ds(tile * LANES, LANES)], ext_ref.at[item, :, tile, main], sem.at[item, tile]
+            )
+            for tile in range(tiles)
+        ]
+        if item < fields:
+            copies.append(pltpu.make_async_copy(driving_ref.at[item], other_ref.at[item], sem.at[item, tiles]))
+        return copies
+
     tables = [
-        pltpu.make_async_copy(wx_hbm.at[facts[0]], wx_ref, sem.at[fields, 0]),
-        pltpu.make_async_copy(wy_hbm.at[facts[1]], wy_ref, sem.at[fields, 1]),
+        pltpu.make_async_copy(wx_hbm.at[facts[0]], wx_ref, sem.at[fields + 1, 0]),
+        pltpu.make_async_copy(wy_hbm.at[facts[1]], wy_ref, sem.at[fields + 1, 1]),
     ]
-    loads = [
-        [
-            pltpu.make_async_copy(state_ref.at[field], held.at[field], sem.at[field, 0]),
-            pltpu.make_async_copy(driving_ref.at[field], other.at[field], sem.at[field, 1]),
-        ]
-        for field in range(fields)
-    ]
-    for copy in [*loads[0], *tables, *(copy for load in loads[1:] for copy in load)]:
+    loads = [fetch(item) for item in range(fields + 1)]
+    for copy in [*tables, *(copy for load in loads for copy in load)]:
         copy.start()
     lane = lax.broadcasted_iota(jnp.int32, (half * rows, LANES), 1)
     for copy in tables:
         copy.wait()
     weights = wx_ref[...]
+
+    def rows_of(field):
+        for pair in range(half):
+            out = dot(wy_ref[...], packed_ref[field, pair * rows : (pair + 1) * rows])
+            out = out[:MODES] + out[MODES:]
+            modes_ref[field, pair * MODES : (pair + 1) * MODES] = out[:, :LANES] + out[:, LANES:]
+
     for field in range(fields):
         for copy in loads[field]:
             copy.wait()
         sides = []
         for side in range(2):
             part = pl.ds(side * half, half)
-            diff = (held[field, part] - other[field, part]).reshape(half * rows, cols)
+            tile_of = [ext_ref[field, part, tile, main].reshape(half * rows, LANES) for tile in range(tiles)]
+            diff = jnp.concatenate(tile_of, axis=1) - other_ref[field, part].reshape(half * rows, cols)
             high, low = split(diff)
             both = dot(high, weights) + dot(low, weights)
             sides.append(both + pltpu.roll(both, MODES, 1))
         high, low = split(jnp.where(lane < MODES, sides[0], sides[1]))
         packed_ref[field, :, :LANES] = high
         packed_ref[field, :, LANES:] = low
-    for field in range(fields):
-        for pair in range(half):
-            out = dot(wy_ref[...], packed_ref[field, pair * rows : (pair + 1) * rows])
-            out = out[:MODES] + out[MODES:]
-            modes_ref[field, pair * MODES : (pair + 1) * MODES] = out[:, :LANES] + out[:, LANES:]
+        if field:
+            rows_of(field - 1)
+    for copy in loads[fields]:
+        copy.wait()
+    rows_of(fields - 1)
     mine = facts[2]
     for piece in range(pieces):
         source = pl.multiple_of(jnp.bitwise_xor(mine, piece) * chunk, SUB)
         target = keep_ref if piece < pieces // 2 else send_ref
         target[piece % (pieces // 2)] = modes_ref[:, pl.ds(source, chunk)]
+
+    upper = lax.broadcasted_iota(jnp.int32, (SUB, LANES), 0) >= 4
+
+    def pack(bottom):
+        for out_ref, last in ((a_ref, bottom), (b_ref, 1 - bottom)):
+            here = pl.ds(GUARD + SUB + last * (rows - SUB), SUB)
+            for level in range(levels):
+                for tile in range(tiles):
+                    lanes = pl.ds(tile * LANES, LANES)
+                    u, v, w, p, t, s = (ext_ref[item, level, tile, here] for item in range(6))
+                    out_ref[level, 0, :, lanes] = p
+                    out_ref[level, 1, :, lanes] = v
+                    for place, own, more in ((2, u, w), (3, t, s)):
+                        more = pltpu.roll(more, 4, 0)
+                        out_ref[level, place, :, lanes] = jnp.where(upper, own, more) if last else jnp.where(upper, more, own)
+
+    for bottom in range(2):
+        pl.when(facts[4] == bottom)(functools.partial(pack, bottom))
 
 
 def nudge_kernel(facts, rate_ref, ext_ref, own_ref, far_ref, wide_ref, by_ref, out_ref, modes_ref, back_ref, done_ref, sem):
@@ -183,6 +201,7 @@
             back_ref[field, pair * rows : (pair + 1) * rows, :LANES] = high
             back_ref[field, pair * rows : (pair + 1) * rows, LANES:] = low
     main = pl.ds(GUARD + SUB, rows)
+    last_lane = lax.broadcasted_iota(jnp.int32, (rows, LANES), 1) == LANES - 1
     stores = []
     for field in range(fields):
         left = back_ref[field]
@@ -192,11 +211,16 @@
             for tile in range(tiles):
                 lanes = pl.ds(tile * LANES, LANES)
                 column = (level // half) * cols + tile * LANES
-                done_ref[field, level, :, lanes] = (
-                    ext_ref[field, level, tile, main] - tendency[first : first + rows, column : column + LANES]
-                )
-        stores.append(pltpu.make_async_copy(done_ref.at[field], out_ref.at[field], sem.at[field]))
-        stores[-1].start()
+                value = ext_ref[field, level, tile, main]
+                if field == 0:
+                    before = ext_ref[field, level, (tile - 1) % (tiles + 1), main]
+                    value = pltpu.roll(jnp.where(last_lane, before, value), 1, 1)
+                done_ref[field, level, :, lanes] = value - tendency[first : first + rows, column : column + LANES]
+            if level % half == half - 1:
+                part = pl.ds(level + 1 - half, half)
+                place = sem.at[field, level // half]
+                stores.append(pltpu.make_async_copy(done_ref.at[field, part], out_ref.at[field, part], place))
+                stores[-1].start()
     for copy in stores:
         copy.wait()
 
@@ -208,30 +232,17 @@
             yield item, level, REACH_X[item], GROUP_X[item], starts[item] + REACH_X[item] * level
 
 
-def load_kernel(facts, state_ref, sound_ref, a_ref, b_ref, bx_hbm, by_hbm, ext_ref, wide_ref, by_ref, *refs):
+def band_kernel(facts, _, a_ref, b_ref, bx_hbm, by_hbm, ext_ref, wide_ref, by_ref, *refs, rows, cols):
     *bands, sem = refs
-    _, levels, rows, cols = state_ref.shape
+    levels = ext_ref.shape[1]
     tiles = cols // LANES
     main = GUARD + SUB
-    loads = []
-    for tile in dict.fromkeys((0, tiles - 1, *range(tiles))):
-        for item in range(6):
-            source = state_ref.at[item] if item < 5 else sound_ref
-            loads.append(
-                pltpu.make_async_copy(
-                    source.at[:, :, pl.ds(tile * LANES, LANES)],
-                    ext_ref.at[item, :, tile, pl.ds(main, rows)],
-                    sem.at[item, tile],
-                )
-            )
-    tables = [pltpu.make_async_copy(by_hbm.at[facts[1]], by_ref, sem.at[6, 0])]
+    tables = [pltpu.make_async_copy(by_hbm.at[facts[1]], by_ref, sem.at[3, 0])]
     for copy in range(3):
         for side in range(2):
-            target = wide_ref.at[
-                pl.ds((2 * copy + side) * MODES, MODES), pl.ds(side * cols, cols)
-            ]
-            tables.append(pltpu.make_async_copy(bx_hbm.at[facts[0], copy // 2], target, sem.at[7 + copy, side]))
-    for copy in loads + tables:
+            target = wide_ref.at[pl.ds((2 * copy + side) * MODES, MODES), pl.ds(side * cols, cols)]
+            tables.append(pltpu.make_async_copy(bx_hbm.at[facts[0], copy // 2], target, sem.at[copy, side]))
+    for copy in tables:
         copy.start()
 
     blank = jnp.zeros((MODES, cols), wide_ref.dtype)
@@ -257,10 +268,6 @@
 
     for odd in range(2):
         pl.when(facts[6] == odd)(functools.partial(place_slabs, odd))
-    edges = 6 * len({0, tiles - 1})
-    for copy in loads[:edges]:
-        copy.wait()
-
     lane = lax.broadcasted_iota(jnp.int32, (SUB, LANES), 1)
 
     def pack_band(band, right):
@@ -280,12 +287,12 @@
     for index, band in enumerate(bands):
         for right in range(2):
             pl.when((facts[3] ^ index) == right)(functools.partial(pack_band, band, right))
-    for copy in loads[edges:] + tables:
+    for copy in tables:
         copy.wait()
 
 
 def substep_kernel(facts, *refs, step, levels, rows, cols):
-    bands, ext_ref, d_ref = refs[1:-2], refs[-2], refs[-1]
+    bands, ext_ref = refs[1:-1], refs[-1]
     tiles = cols // LANES
     chunks = rows // SUB
     lane = lax.broadcasted_iota(jnp.int32, (SUB, LANES), 1)
@@ -361,14 +368,9 @@
                     slope = slope * (quarter if edge is None else quarter * edge)
                 elif edge is not None:
                     slope = slope * edge
-                fresh.append((ahead(old, tile, 1) if first else old[tile]) - slope)
-            if last:
-                for tile in range(tiles):
-                    made.append((u_ref, level, tile, here, behind(fresh, tile, 1)))
-                    made.append((d_ref, level, tile, here, fresh[tile] - behind(fresh, tile, 2)))
-            else:
-                for tile in range(ring):
-                    made.append((u_ref, level, tile, here, fresh[tile]))
+                fresh.append(old[tile] - slope)
+            for tile in range(ring):
+                made.append((u_ref, level, tile, here, fresh[tile]))
             after = None
             if level + 1 < levels:
                 after = [p_ref[level + 1, tile, here] for tile in range(ring)]
@@ -393,15 +395,12 @@
         before, now = None, [w_ref[0, tile, here] for tile in range(x_tiles)]
         for level in range(levels):
             made = []
-            line = None if last else [u_ref[level, tile, here] for tile in range(ring)]
+            line = [u_ref[level, tile, here] for tile in range(ring)]
             after = None
             if level + 1 < levels:
                 after = [w_ref[level + 1, tile, here] for tile in range(x_tiles)]
             for tile in range(x_tiles):
-                if last:
-                    spread = d_ref[level, tile, here]
-                else:
-                    spread = line[tile] - behind(line, tile, 2)
+                spread = line[tile] - behind(line, tile, 2)
                 spread += v_ref[level, tile, pl.ds(row + 1, SUB)] - v_ref[level, tile, pl.ds(row - 1, SUB)]
                 if level == 0:
                     spread += after[tile]
@@ -422,6 +421,16 @@
             before, now = now, after
             flush(made)
 
+    def shift_rows(part, _):
+        here = pl.ds(pl.multiple_of(part * SUB, SUB) + GUARD, SUB)
+        for level in range(levels):
+            old = [u_ref[level, tile, here] for tile in range(ring)]
+            for tile in range(ring):
+                u_ref[level, tile, here] = ahead(old, tile, 1)
+        return 0
+
+    if first:
+        lax.fori_loop(0, chunks + 2, shift_rows, 0)
     if last:
         winds(0, True)
         winds(chunks + 1, True)
@@ -500,7 +509,7 @@
         hbm = pl.BlockSpec(memory_space=pltpu.HBM)
         vmem = pl.BlockSpec(memory_space=pltpu.VMEM)
 
-        def call(kernel, name, shapes, ins, scratch, operands, flops=0, data=0, prefetch=1, aliases=None):
+        def call(kernel, name, shapes, ins, scratch, operands, flops=0, data=0, prefetch=1, aliases=None, limit=VMEM_LIMIT):
             return pl.pallas_call(
                 kernel,
                 grid_spec=pltpu.PrefetchScalarGridSpec(
@@ -512,7 +521,7 @@
                 ),
                 out_shape=shapes,
                 input_output_aliases=aliases or {},
-                compiler_params=pltpu.CompilerParams(vmem_limit_bytes=VMEM_LIMIT),
+                compiler_params=pltpu.CompilerParams(vmem_limit_bytes=limit),
                 cost_estimate=pl.CostEstimate(flops=flops, bytes_accessed=data, transcendentals=0),
             )(*operands)
 
@@ -521,53 +530,44 @@
 
         tiles = cols // LANES
         slab_shape = (levels, 4, SUB, cols)
-        slab_a, slab_b = call(
-            informed(slab_kernel),
-            "slabs",
-            [array(slab_shape)] * 2,
-            [hbm, hbm],
-            [pltpu.VMEM((2, 2, levels, SUB, cols), jnp.float32), pltpu.SemaphoreType.DMA((2, 6))],
-            (info, state, sound_square),
-        )
-        slab_a = neighbours(slab_a, "gy", ny, 0)
-        slab_b = neighbours(slab_b, "gy", ny, 1)
-
         piece_shape = (pieces // 2, fields, chunk, LANES)
-        keep, send = call(
-            informed(project_kernel),
-            "project",
-            [array(piece_shape)] * 2,
-            [hbm] * 4,
+        ext_shape = (6, levels, tiles + 1, rows + 2 * SUB + 2 * GUARD, LANES)
+        band_shape = (rows + 2 * SUB, 2 * LANES)
+        ext, slab_a, slab_b, keep, send = call(
+            informed(head_kernel),
+            "head",
+            [array(ext_shape), *[array(slab_shape)] * 2, *[array(piece_shape)] * 2],
+            [hbm] * 5,
             [
-                pltpu.VMEM((fields, levels, rows, cols), jnp.float32),
                 pltpu.VMEM((fields, levels, rows, cols), jnp.float32),
                 pltpu.VMEM((cols, 2 * MODES), jnp.bfloat16),
                 pltpu.VMEM((2 * MODES, rows), jnp.bfloat16),
                 pltpu.VMEM((fields, half * rows, 2 * LANES), jnp.bfloat16),
                 pltpu.VMEM((fields, half * MODES, LANES), jnp.float32),
-                pltpu.SemaphoreType.DMA((fields + 1, 2)),
+                pltpu.SemaphoreType.DMA((fields + 2, tiles + 1)),
             ],
-            (info, state, driving, wx, wy),
+            (info, *(pltpu.with_memory_space_constraint(x, pltpu.HBM) for x in (state, driving, sound_square, wx, wy))),
             600_000_000,
-            8_500_000,
+            9_000_000,
         )
-
-        ext_shape = (6, levels, tiles + 1, rows + 2 * SUB + 2 * GUARD, LANES)
-        band_shape = (rows + 2 * SUB, 2 * LANES)
+        slab_a = neighbours(slab_a, "gy", ny, 0)
+        slab_b = neighbours(slab_b, "gy", ny, 1)
+
         ext, wide, back, *bands = call(
-            informed(load_kernel),
-            "load",
+            informed(band_kernel, rows=rows, cols=cols),
+            "band",
             [
                 array(ext_shape),
                 array((6 * MODES, 2 * cols), jnp.bfloat16),
                 array((2 * rows, MODES), jnp.bfloat16),
             ]
             + [array(band_shape)] * x_phases,
-            [hbm, hbm, vmem, vmem, hbm, hbm],
-            [pltpu.SemaphoreType.DMA((10, max(tiles, 2)))],
-            (info, state, sound_square, slab_a, slab_b, bx, by),
+            [vmem, vmem, vmem, hbm, hbm],
+            [pltpu.SemaphoreType.DMA((4, 2))],
+            (info, ext, slab_a, slab_b, bx, by),
             1_000_000,
             10_000_000,
+            aliases={1: 0},
         )
         bands = [neighbours(band, "gx", nx, index) for index, band in enumerate(bands)]
 
@@ -578,7 +578,7 @@
                 f"substep_{step}",
                 [array(ext_shape)],
                 [vmem] * (1 + len(extra)),
-                [pltpu.VMEM(ext_shape[1:], jnp.float32)],
+                [],
                 (info, ext, *extra),
                 10_000_000,
                 8_000_000,
@@ -610,7 +610,7 @@
                 pltpu.VMEM((fields, half * MODES, LANES), jnp.float32),
                 pltpu.VMEM((fields, half * rows, 2 * LANES), jnp.bfloat16),
                 pltpu.VMEM((fields, levels, rows, cols), jnp.float32),
-                pltpu.SemaphoreType.DMA((fields,)),
+                pltpu.SemaphoreType.DMA((fields, 2)),
             ],
             (info, rate, ext, value, far, wide, back),
             600_000_000,

time: 66.4 us -> 58.6 us (0.88)
  local copies, waits for them, and re-layouts: 6.23 us -> 0.03 us
  Pallas kernels: 18.7 us -> 16.6 us
  starting transfers between devices: 14.3 us -> 15.3 us
    unnamed x16 -> x6, local copies, waits for them, and re-layouts: 6.21 us -> 0.01 us
    pallas_call x7 -> x6, Pallas kernels: 18.7 us -> 16.6 us  [call(): pl.pallas_call(kernel, grid_spec=pltpu.PrefetchScalarGridSpec(num_scalar_...]
    ppermute x3, starting transfers between devices: 2.56 us -> 3.6 us  [neighbours(): return lax.ppermute(value, axis, pairs)]
    ppermute x3, waiting for transfers between devices: 14.7 us -> 13.7 us  [neighbours(): return lax.ppermute(value, axis, pairs)]
  transfers between devices with their start and end apart: 14 -> 14, of which waited for: 10 -> 9; matrix products, arithmetic and copies ran while one was open for 0% -> 0% of each run, Pallas kernels for 18% -> 15%
where the time goes in v1:
time: 58.6 us; the launch traced here: 58.5 us
  waiting for transfers between devices  26.3 us (45%)
  Pallas kernels  16.6 us (28%)
  starting transfers between devices  15.3 us (26%)
    pallas_call x6, Pallas kernels, call(): pl.pallas_call(kernel, grid_spec=pltpu.PrefetchScalarGridSpec(num_scalar_...  16.6 us
    ppermute x3, waiting for transfers between devices, neighbours(): return lax.ppermute(value, axis, pairs)  13.7 us
    ppermute x11, waiting for transfers between devices, swap(): lax.ppermute(value, ('gx', 'gy'), [(i, i ^ mask) for i in range(devices)])  12.6 us
    ppermute x11, starting transfers between devices, swap(): lax.ppermute(value, ('gx', 'gy'), [(i, i ^ mask) for i in range(devices)])  11.7 us
    ppermute x3, starting transfers between devices, neighbours(): return lax.ppermute(value, axis, pairs)  3.6 us
  transfers between devices with their start and end apart: 14, of which 9 were waited for; matrix products, arithmetic and copies ran while one was open for 0% of the time, Pallas kernels for 15%

profile of v1, /device:TPU:2, one launch (start us, length us, event | category | flops | bytes accessed | tf_op | source)
XLA Modules:
  0.0 58.5 jit_solution(350727104290193772)
XLA Ops:
  0.0 4.5 %shard_map.82 = (f32[6,8,4,96,128]{4,3,2,1,0:T(8,128)S(1)}, f32[8,4,8,384]{3,2,1,0:T(8,128)S(1)}, f32[8,4,8,384]{3,2,1,0:T(8,128)S(1)}, f32[4,5,32,128]{3,2,1,0:T(8,128)S(1)}, f32[4,5,32,128]{3,2,1,0:T(8,128)S(1)}) custom-call(s32[1]{0:T(128)} %bitcast.info, f32[5,8,64,384]{3,2,1,0:T(8,128)} %refs_0_.2, f32[5,8,64,384]{3,2,1,0:T(8,128)} %refs_1_.1, ...), custom_call_target="tpu_custom_call" | custom-call | flops 600000000 | bytes 9000000 | tf_op jit(solution)/shard_map/pallas_call | solution.py:513
  4.6 1.6 %collective-permute-done.3 = f32[4,5,32,128]{3,2,1,0:T(8,128)S(1)} collective-permute-done((f32[4,5,32,128]{3,2,1,0:T(8,128)S(1)}, f32[4,5,32,128]{3,2,1,0:T(8,128)S(1)}, u32[]{:S(2)}, u32[]{:S(2)}) %collective-permute-start.3) | collective-permute-done | bytes 327712 | tf_op jit(solution)/shard_map/ppermute | solution.py:483
  6.4 3.0 %collective-permute-start.6 = (f32[1,5,32,128]{3,2,1,0:T(8,128)S(1)}, f32[1,5,32,128]{3,2,1,0:T(8,128)S(1)}, u32[]{:S(2)}, u32[]{:S(2)}) collective-permute-start(f32[1,5,32,128]{3,2,1,0:T(8,128)S(1)} %get-tuple-element.24), channel_id=1, source_target_pairs={{0,18},{1,19},{2,16},{3,17},{4,22},{5,23},{6,20},{7,21},{8,26},{9,... | collective-permute-start | bytes 245768 | tf_op jit(solution)/shard_map/ppermute | solution.py:483
  9.4 0.5 collective-permute-start.5
  9.9 1.5 %collective-permute-done.4 = f32[1,5,32,128]{3,2,1,0:T(8,128)S(1)} collective-permute-done((f32[1,5,32,128]{3,2,1,0:T(8,128)S(1)}, f32[1,5,32,128]{3,2,1,0:T(8,128)S(1)}, u32[]{:S(2)}, u32[]{:S(2)}) %collective-permute-start.4) | collective-permute-done | bytes 81952 | tf_op jit(solution)/shard_map/ppermute | solution.py:483
  11.4 2.3 %collective-permute-done.6 = f32[1,5,32,128]{3,2,1,0:T(8,128)S(1)} collective-permute-done((f32[1,5,32,128]{3,2,1,0:T(8,128)S(1)}, f32[1,5,32,128]{3,2,1,0:T(8,128)S(1)}, u32[]{:S(2)}, u32[]{:S(2)}) %collective-permute-start.6) | collective-permute-done | bytes 81952 | tf_op jit(solution)/shard_map/ppermute | solution.py:483
  13.7 1.1 %collective-permute-done.5 = f32[1,5,32,128]{3,2,1,0:T(8,128)S(1)} collective-permute-done((f32[1,5,32,128]{3,2,1,0:T(8,128)S(1)}, f32[1,5,32,128]{3,2,1,0:T(8,128)S(1)}, u32[]{:S(2)}, u32[]{:S(2)}) %collective-permute-start.5) | collective-permute-done | bytes 81952 | tf_op jit(solution)/shard_map/ppermute | solution.py:483
  14.8 3.7 %collective-permute-start.9 = (f32[1,5,32,128]{3,2,1,0:T(8,128)S(1)}, f32[1,5,32,128]{3,2,1,0:T(8,128)S(1)}, u32[]{:S(2)}, u32[]{:S(2)}) collective-permute-start(f32[1,5,32,128]{3,2,1,0:T(8,128)S(1)} %fusion.1), channel_id=1, source_target_pairs={{0,12},{1,13},{2,14},{3,15},{4,8},{5,9},{6,10},{7,11},{8,4},{9,5},... | collective-permute-start | bytes 245768 | tf_op jit(solution)/shard_map/ppermute | solution.py:483
  18.5 0.8 %collective-permute-start.7 = (f32[1,5,32,128]{3,2,1,0:T(8,128)S(1)}, f32[1,5,32,128]{3,2,1,0:T(8,128)S(1)}, u32[]{:S(2)}, u32[]{:S(2)}) collective-permute-start(f32[1,5,32,128]{3,2,1,0:T(8,128)S(1)} %fusion.1), channel_id=1, source_target_pairs={{0,4},{1,5},{2,6},{3,7},{4,0},{5,1},{6,2},{7,3},{8,12},{9,13},{10,... | collective-permute-start | bytes 245768 | tf_op jit(solution)/shard_map/ppermute | solution.py:483
  19.3 2.7 %collective-permute-done.9 = f32[1,5,32,128]{3,2,1,0:T(8,128)S(1)} collective-permute-done((f32[1,5,32,128]{3,2,1,0:T(8,128)S(1)}, f32[1,5,32,128]{3,2,1,0:T(8,128)S(1)}, u32[]{:S(2)}, u32[]{:S(2)}) %collective-permute-start.9) | collective-permute-done | bytes 81952 | tf_op jit(solution)/shard_map/ppermute | solution.py:483
  22.0 3.0 %collective-permute-done.8 = f32[1,5,32,128]{3,2,1,0:T(8,128)S(1)} collective-permute-done((f32[1,5,32,128]{3,2,1,0:T(8,128)S(1)}, f32[1,5,32,128]{3,2,1,0:T(8,128)S(1)}, u32[]{:S(2)}, u32[]{:S(2)}) %collective-permute-start.8) | collective-permute-done | bytes 81952 | tf_op jit(solution)/shard_map/ppermute | solution.py:483
  25.0 0.7 %collective-permute-start.12 = (f32[1,5,32,128]{3,2,1,0:T(8,128)S(1)}, f32[1,5,32,128]{3,2,1,0:T(8,128)S(1)}, u32[]{:S(2)}, u32[]{:S(2)}) collective-permute-start(f32[1,5,32,128]{3,2,1,0:T(8,128)S(1)} %add_add_fusion), channel_id=1, source_target_pairs={{0,18},{1,19},{2,16},{3,17},{4,22},{5,23},{6,20},{7,21},{8,26},{9,... | collective-permute-start | bytes 245768 | tf_op jit(solution)/shard_map/ppermute | solution.py:483
  25.6 1.6 %collective-permute-start.11 = (f32[1,5,32,128]{3,2,1,0:T(8,128)S(1)}, f32[1,5,32,128]{3,2,1,0:T(8,128)S(1)}, u32[]{:S(2)}, u32[]{:S(2)}) collective-permute-start(f32[1,5,32,128]{3,2,1,0:T(8,128)S(1)} %add_add_fusion), channel_id=1, source_target_pairs={{0,16},{1,17},{2,18},{3,19},{4,20},{5,21},{6,22},{7,23},{8,24},{9,... | collective-permute-start | bytes 245768 | tf_op jit(solution)/shard_map/ppermute | solution.py:483
  27.3 1.3 %collective-permute-start.10 = (f32[1,5,32,128]{3,2,1,0:T(8,128)S(1)}, f32[1,5,32,128]{3,2,1,0:T(8,128)S(1)}, u32[]{:S(2)}, u32[]{:S(2)}) collective-permute-start(f32[1,5,32,128]{3,2,1,0:T(8,128)S(1)} %add_add_fusion), channel_id=1, source_target_pairs={{0,2},{1,3},{2,0},{3,1},{4,6},{5,7},{6,4},{7,5},{8,10},{9,11},{10,... | collective-permute-start | bytes 245768 | tf_op jit(solution)/shard_map/ppermute | solution.py:483
  28.5 2.8 %collective-permute-start.1 = (f32[8,4,8,384]{3,2,1,0:T(8,128)S(1)}, f32[8,4,8,384]{3,2,1,0:T(8,128)S(1)}, u32[]{:S(2)}, u32[]{:S(2)}) collective-permute-start(f32[8,4,8,384]{3,2,1,0:T(8,128)S(1)} %get-tuple-element.16), channel_id=1, source_target_pairs={{1,2},{2,1},{3,4},{4,3},{5,6},{6,5},{7,8},{8,7},{9,10},{10,9},{11,... | collective-permute-start | bytes 1179656 | tf_op jit(solution)/shard_map/ppermute | solution.py:489
  31.3 0.4 collective-permute-done.10
  31.8 10.0 %collective-permute-done.1.refs_2_ = f32[8,4,8,384]{3,2,1,0:T(8,128)S(1)} collective-permute-done((f32[8,4,8,384]{3,2,1,0:T(8,128)S(1)}, f32[8,4,8,384]{3,2,1,0:T(8,128)S(1)}, u32[]{:S(2)}, u32[]{:S(2)}) %collective-permute-start.1) | collective-permute-done | bytes 393248 | tf_op jit(solution)/shard_map/ppermute | solution.py:489
  41.8 1.6 %shard_map.83 = (f32[6,8,4,96,128]{4,3,2,1,0:T(8,128)S(1)}, bf16[384,768]{1,0:T(8,128)(2,1)S(1)}, bf16[128,64]{1,0:T(8,128)(2,1)S(1)}, f32[80,256]{1,0:T(8,128)S(1)}) custom-call(s32[1]{0:T(128)} %bitcast.info, f32[6,8,4,96,128]{4,3,2,1,0:T(8,128)S(1)} %get-tuple-element.14.refs_0_, ...), custom_call_target="tpu_custom_call", output_to_operand_aliasing={{0}: (1, {})} | custom-call | flops 1000000 | bytes 10000000 | tf_op jit(solution)/shard_map/pallas_call | solution.py:513
  43.4 0.8 %collective-permute-start.2 = (f32[80,256]{1,0:T(8,128)S(1)}, f32[80,256]{1,0:T(8,128)S(1)}, u32[]{:S(2)}, u32[]{:S(2)}) collective-permute-start(f32[80,256]{1,0:T(8,128)S(1)} %get-tuple-element.18), channel_id=1, source_target_pairs={{0,16},{16,0},{1,17},{17,1},{2,18},{18,2},{3,19},{19,3},{4,20},{20... | collective-permute-start | bytes 245768 | tf_op jit(solution)/shard_map/ppermute | solution.py:489
  44.2 3.7 %collective-permute-done.2.refs_1_ = f32[80,256]{1,0:T(8,128)S(1)} collective-permute-done((f32[80,256]{1,0:T(8,128)S(1)}, f32[80,256]{1,0:T(8,128)S(1)}, u32[]{:S(2)}, u32[]{:S(2)}) %collective-permute-start.2) | collective-permute-done | bytes 81952 | tf_op jit(solution)/shard_map/ppermute | solution.py:489
  47.9 4.0 %shard_map.84.refs_0_ = f32[6,8,4,96,128]{4,3,2,1,0:T(8,128)S(1)} custom-call(s32[1]{0:T(128)} %bitcast.info, f32[6,8,4,96,128]{4,3,2,1,0:T(8,128)S(1)} %get-tuple-element.17.refs_0_, f32[80,256]{1,0:T(8,128)S(1)} %collective-permute-done.2.refs_1_), custom_call_target="tpu_custom_call", output_to_operand_aliasing={{}: (1, {})} | custom-call | flops 10000000 | bytes 8000000 | tf_op jit(solution)/shard_map/pallas_call | solution.py:513
  52.0 1.8 %shard_map.85.refs_0_ = f32[6,8,4,96,128]{4,3,2,1,0:T(8,128)S(1)} custom-call(s32[1]{0:T(128)} %bitcast.info, f32[6,8,4,96,128]{4,3,2,1,0:T(8,128)S(1)} %shard_map.84.refs_0_), custom_call_target="tpu_custom_call", output_to_operand_aliasing={{}: (1, {})} | custom-call | flops 10000000 | bytes 8000000 | tf_op jit(solution)/shard_map/pallas_call | solution.py:513
  53.8 1.2 %shard_map.86.refs_1_ = f32[6,8,4,96,128]{4,3,2,1,0:T(8,128)S(1)} custom-call(s32[1]{0:T(128)} %bitcast.info, f32[6,8,4,96,128]{4,3,2,1,0:T(8,128)S(1)} %shard_map.85.refs_0_), custom_call_target="tpu_custom_call", output_to_operand_aliasing={{}: (1, {})} | custom-call | flops 10000000 | bytes 8000000 | tf_op jit(solution)/shard_map/pallas_call | solution.py:513
  55.0 3.5 %shard_map.87 = f32[5,8,64,384]{3,2,1,0:T(8,128)} custom-call(s32[1]{0:T(128)} %bitcast.info, f32[5,8]{1,0:T(8,128)S(1)} %copy-done.2, f32[6,8,4,96,128]{4,3,2,1,0:T(8,128)S(1)} %shard_map.86.refs_1_, f32[4,5,32,128]{3,2,1,0:T(8,128)S(1)} %pad_maximum_fusion.refs_2_, f32[4,5,32,128]{3,2,1,0:T(8,128)S(1)} %collective-permute-done.13.refs_3_, ...), custom_call_target="tpu_custom_call" | custom-call | flops 600000000 | bytes 8500000 | tf_op jit(solution)/shard_map/pallas_call | solution.py:513
  (21 shorter events, 0.4 us)
Async XLA Ops:
  0.0 41.8 %copy-start = (bf16[16,128,64]{2,1,0:T(8,128)(2,1)S(1)}, bf16[16,128,64]{2,1,0:T(8,128)(2,1)}, u32[]{:S(2)}) copy-start(bf16[16,128,64]{2,1,0:T(8,128)(2,1)} %constant.22.clone.refs_4_) | copy-start | bytes 786436
  0.0 41.8 %copy-start.1 = (bf16[2,2,64,384]{3,2,1,0:T(8,128)(2,1)S(1)}, bf16[2,2,64,384]{3,2,1,0:T(8,128)(2,1)}, u32[]{:S(2)}) copy-start(bf16[2,2,64,384]{3,2,1,0:T(8,128)(2,1)} %constant.21.clone.refs_3_) | copy-start | bytes 589828
  4.5 1.7 %collective-permute-start.3 = (f32[4,5,32,128]{3,2,1,0:T(8,128)S(1)}, f32[4,5,32,128]{3,2,1,0:T(8,128)S(1)}, u32[]{:S(2)}, u32[]{:S(2)}) collective-permute-start(f32[4,5,32,128]{3,2,1,0:T(8,128)S(1)} %get-tuple-element.20), channel_id=1, source_target_pairs={{0,1},{1,0},{2,3},{3,2},{4,5},{5,4},{6,7},{7,6},{8,9},{9,8},{10,11... | collective-permute-start | bytes 983048 | tf_op jit(solution)/shard_map/ppermute | solution.py:483
  6.3 5.1 %collective-permute-start.4 = (f32[1,5,32,128]{3,2,1,0:T(8,128)S(1)}, f32[1,5,32,128]{3,2,1,0:T(8,128)S(1)}, u32[]{:S(2)}, u32[]{:S(2)}) collective-permute-start(f32[1,5,32,128]{3,2,1,0:T(8,128)S(1)} %get-tuple-element.23), channel_id=1, source_target_pairs={{0,2},{1,3},{2,0},{3,1},{4,6},{5,7},{6,4},{7,5},{8,10},{9,11},{10,... | collective-permute-start | bytes 245768 | tf_op jit(solution)/shard_map/ppermute | solution.py:483
  6.4 7.3 %collective-permute-start.6 = (f32[1,5,32,128]{3,2,1,0:T(8,128)S(1)}, f32[1,5,32,128]{3,2,1,0:T(8,128)S(1)}, u32[]{:S(2)}, u32[]{:S(2)}) collective-permute-start(f32[1,5,32,128]{3,2,1,0:T(8,128)S(1)} %get-tuple-element.24), channel_id=1, source_target_pairs={{0,18},{1,19},{2,16},{3,17},{4,22},{5,23},{6,20},{7,21},{8,26},{9,... | collective-permute-start | bytes 245768 | tf_op jit(solution)/shard_map/ppermute | solution.py:483
  9.4 5.4 %collective-permute-start.5 = (f32[1,5,32,128]{3,2,1,0:T(8,128)S(1)}, f32[1,5,32,128]{3,2,1,0:T(8,128)S(1)}, u32[]{:S(2)}, u32[]{:S(2)}) collective-permute-start(f32[1,5,32,128]{3,2,1,0:T(8,128)S(1)} %get-tuple-element.25), channel_id=1, source_target_pairs={{0,16},{1,17},{2,18},{3,19},{4,20},{5,21},{6,22},{7,23},{8,24},{9,... | collective-permute-start | bytes 245768 | tf_op jit(solution)/shard_map/ppermute | solution.py:483
  14.8 7.2 %collective-permute-start.9 = (f32[1,5,32,128]{3,2,1,0:T(8,128)S(1)}, f32[1,5,32,128]{3,2,1,0:T(8,128)S(1)}, u32[]{:S(2)}, u32[]{:S(2)}) collective-permute-start(f32[1,5,32,128]{3,2,1,0:T(8,128)S(1)} %fusion.1), channel_id=1, source_target_pairs={{0,12},{1,13},{2,14},{3,15},{4,8},{5,9},{6,10},{7,11},{8,4},{9,5},... | collective-permute-start | bytes 245768 | tf_op jit(solution)/shard_map/ppermute | solution.py:483
  18.5 6.5 %collective-permute-start.8 = (f32[1,5,32,128]{3,2,1,0:T(8,128)S(1)}, f32[1,5,32,128]{3,2,1,0:T(8,128)S(1)}, u32[]{:S(2)}, u32[]{:S(2)}) collective-permute-start(f32[1,5,32,128]{3,2,1,0:T(8,128)S(1)} %fusion.1), channel_id=1, source_target_pairs={{0,8},{1,9},{2,10},{3,11},{4,12},{5,13},{6,14},{7,15},{8,0},{9,1},... | collective-permute-start | bytes 245768 | tf_op jit(solution)/shard_map/ppermute | solution.py:483
  18.5 6.5 %collective-permute-start.7 = (f32[1,5,32,128]{3,2,1,0:T(8,128)S(1)}, f32[1,5,32,128]{3,2,1,0:T(8,128)S(1)}, u32[]{:S(2)}, u32[]{:S(2)}) collective-permute-start(f32[1,5,32,128]{3,2,1,0:T(8,128)S(1)} %fusion.1), channel_id=1, source_target_pairs={{0,4},{1,5},{2,6},{3,7},{4,0},{5,1},{6,2},{7,3},{8,12},{9,13},{10,... | collective-permute-start | bytes 245768 | tf_op jit(solution)/shard_map/ppermute | solution.py:483
  25.0 6.3 %collective-permute-start.12 = (f32[1,5,32,128]{3,2,1,0:T(8,128)S(1)}, f32[1,5,32,128]{3,2,1,0:T(8,128)S(1)}, u32[]{:S(2)}, u32[]{:S(2)}) collective-permute-start(f32[1,5,32,128]{3,2,1,0:T(8,128)S(1)} %add_add_fusion), channel_id=1, source_target_pairs={{0,18},{1,19},{2,16},{3,17},{4,22},{5,23},{6,20},{7,21},{8,26},{9,... | collective-permute-start | bytes 245768 | tf_op jit(solution)/shard_map/ppermute | solution.py:483
  25.6 5.7 %collective-permute-start.11 = (f32[1,5,32,128]{3,2,1,0:T(8,128)S(1)}, f32[1,5,32,128]{3,2,1,0:T(8,128)S(1)}, u32[]{:S(2)}, u32[]{:S(2)}) collective-permute-start(f32[1,5,32,128]{3,2,1,0:T(8,128)S(1)} %add_add_fusion), channel_id=1, source_target_pairs={{0,16},{1,17},{2,18},{3,19},{4,20},{5,21},{6,22},{7,23},{8,24},{9,... | collective-permute-start | bytes 245768 | tf_op jit(solution)/shard_map/ppermute | solution.py:483
  27.3 4.4 %collective-permute-start.10 = (f32[1,5,32,128]{3,2,1,0:T(8,128)S(1)}, f32[1,5,32,128]{3,2,1,0:T(8,128)S(1)}, u32[]{:S(2)}, u32[]{:S(2)}) collective-permute-start(f32[1,5,32,128]{3,2,1,0:T(8,128)S(1)} %add_add_fusion), channel_id=1, source_target_pairs={{0,2},{1,3},{2,0},{3,1},{4,6},{5,7},{6,4},{7,5},{8,10},{9,11},{10,... | collective-permute-start | bytes 245768 | tf_op jit(solution)/shard_map/ppermute | solution.py:483
  28.5 3.3 %collective-permute-start = (f32[8,4,8,384]{3,2,1,0:T(8,128)S(1)}, f32[8,4,8,384]{3,2,1,0:T(8,128)S(1)}, u32[]{:S(2)}, u32[]{:S(2)}) collective-permute-start(f32[8,4,8,384]{3,2,1,0:T(8,128)S(1)} %get-tuple-element.15), channel_id=1, source_target_pairs={{0,1},{1,0},{2,3},{3,2},{4,5},{5,4},{6,7},{7,6},{8,9},{9,8},{10,11... | collective-permute-start | bytes 1179656 | tf_op jit(solution)/shard_map/ppermute | solution.py:489
  28.5 13.3 %collective-permute-start.1 = (f32[8,4,8,384]{3,2,1,0:T(8,128)S(1)}, f32[8,4,8,384]{3,2,1,0:T(8,128)S(1)}, u32[]{:S(2)}, u32[]{:S(2)}) collective-permute-start(f32[8,4,8,384]{3,2,1,0:T(8,128)S(1)} %get-tuple-element.16), channel_id=1, source_target_pairs={{1,2},{2,1},{3,4},{4,3},{5,6},{6,5},{7,8},{8,7},{9,10},{10,9},{11,... | collective-permute-start | bytes 1179656 | tf_op jit(solution)/shard_map/ppermute | solution.py:489
  31.7 23.3 %collective-permute-start.13 = (f32[4,5,32,128]{3,2,1,0:T(8,128)S(1)}, f32[4,5,32,128]{3,2,1,0:T(8,128)S(1)}, u32[]{:S(2)}, u32[]{:S(2)}) collective-permute-start(f32[4,5,32,128]{3,2,1,0:T(8,128)S(1)} %pad_maximum_fusion.refs_2_), channel_id=1, source_target_pairs={{0,1},{1,0},{2,3},{3,2},{4,5},{5,4},{6,7},{7,6},{8,9},{9,8},{10,11... | collective-permute-start | bytes 983048 | tf_op jit(solution)/shard_map/ppermute | solution.py:483
  43.4 4.5 %collective-permute-start.2 = (f32[80,256]{1,0:T(8,128)S(1)}, f32[80,256]{1,0:T(8,128)S(1)}, u32[]{:S(2)}, u32[]{:S(2)}) collective-permute-start(f32[80,256]{1,0:T(8,128)S(1)} %get-tuple-element.18), channel_id=1, source_target_pairs={{0,16},{16,0},{1,17},{17,1},{2,18},{18,2},{3,19},{19,3},{4,20},{20... | collective-permute-start | bytes 245768 | tf_op jit(solution)/shard_map/ppermute | solution.py:489
  53.8 1.2 %copy-start.2 = (f32[5,8]{1,0:T(8,128)S(1)}, f32[5,8]{1,0:T(8,128)}, u32[]{:S(2)}) copy-start(f32[5,8]{1,0:T(8,128)} %refs_0_.3) | copy-start | bytes 484

commit v2 on v1

--- a/solution.py
+++ b/solution.py
@@ -191,31 +191,37 @@
         source = own_ref if piece < pieces // 2 else far_ref
         modes_ref[:, pl.ds(target, chunk)] = source[piece % (pieces // 2)]
     lane = lax.broadcasted_iota(jnp.int32, (MODES, LANES), 1)
+    lower = lax.broadcasted_iota(jnp.int32, (rows, LANES), 1) < MODES
     for field in range(fields):
         for pair in range(half):
             factor = jnp.where(lane < MODES, rate_ref[field, pair], rate_ref[field, pair + half])
             high, low = split(modes_ref[field, pair * MODES : (pair + 1) * MODES] * factor)
             out = dot(by_ref[...], jnp.concatenate([high, low], axis=1))
             out = out[:rows] + out[rows:]
-            high, low = split(out[:, :LANES] + out[:, LANES:])
-            back_ref[field, pair * rows : (pair + 1) * rows, :LANES] = high
-            back_ref[field, pair * rows : (pair + 1) * rows, LANES:] = low
+            out = out[:, :LANES] + out[:, LANES:]
+            high, low = split(out)
+            high_turned, low_turned = split(pltpu.roll(out, MODES, 1))
+            here = pl.ds(pair * rows, rows)
+            back_ref[field, 0, here, :LANES] = jnp.where(lower, high, low_turned)
+            back_ref[field, 1, here, :LANES] = jnp.where(lower, high_turned, low)
+            for side in range(2):
+                back_ref[field, side, here, LANES:] = high
     main = pl.ds(GUARD + SUB, rows)
     last_lane = lax.broadcasted_iota(jnp.int32, (rows, LANES), 1) == LANES - 1
     stores = []
     for field in range(fields):
-        left = back_ref[field]
-        tendency = dot(left, wide_ref[: 4 * MODES]) + dot(left[:, :LANES], wide_ref[4 * MODES :])
         for level in range(levels):
+            if level % half == 0:
+                side = level // half
+                tendency = dot(back_ref[field, side], wide_ref[side])
             first = (level % half) * rows
             for tile in range(tiles):
                 lanes = pl.ds(tile * LANES, LANES)
-                column = (level // half) * cols + tile * LANES
                 value = ext_ref[field, level, tile, main]
                 if field == 0:
                     before = ext_ref[field, level, (tile - 1) % (tiles + 1), main]
                     value = pltpu.roll(jnp.where(last_lane, before, value), 1, 1)
-                done_ref[field, level, :, lanes] = value - tendency[first : first + rows, column : column + LANES]
+                done_ref[field, level, :, lanes] = value - tendency[first : first + rows, lanes.start : lanes.start + LANES]
             if level % half == half - 1:
                 part = pl.ds(level + 1 - half, half)
                 place = sem.at[field, level // half]
@@ -238,16 +244,14 @@
     tiles = cols // LANES
     main = GUARD + SUB
     tables = [pltpu.make_async_copy(by_hbm.at[facts[1]], by_ref, sem.at[3, 0])]
-    for copy in range(3):
-        for side in range(2):
-            target = wide_ref.at[pl.ds((2 * copy + side) * MODES, MODES), pl.ds(side * cols, cols)]
-            tables.append(pltpu.make_async_copy(bx_hbm.at[facts[0], copy // 2], target, sem.at[copy, side]))
+    for side in range(2):
+        for block, part in ((0, 0), (1, 0), (2 + side, 1)):
+            target = wide_ref.at[side, pl.ds(block * MODES, MODES)]
+            tables.append(pltpu.make_async_copy(bx_hbm.at[facts[0], part], target, sem.at[min(block, 2), side]))
     for copy in tables:
         copy.start()
-
-    blank = jnp.zeros((MODES, cols), wide_ref.dtype)
-    for block in range(6):
-        wide_ref[block * MODES : (block + 1) * MODES, (1 - block % 2) * cols : (2 - block % 2) * cols] = blank
+    for side in range(2):
+        wide_ref[side, (3 - side) * MODES : (4 - side) * MODES] = jnp.zeros((MODES, cols), wide_ref.dtype)
     zero = jnp.zeros((SUB, LANES), jnp.float32)
     for item in (1, 3):
         for level in range(levels):
@@ -271,18 +275,17 @@
     lane = lax.broadcasted_iota(jnp.int32, (SUB, LANES), 1)
 
     def pack_band(band, right):
-        def pack_rows(part, _):
-            row = pl.multiple_of(part * SUB, SUB)
-            packed = [jnp.zeros((SUB, LANES), jnp.float32) for _ in range(2)]
-            for item, level, width, group, first in band_lanes(levels):
-                tile = ext_ref[item, level, (tiles - 1) * right, pl.ds(row + GUARD, SUB)]
+        parts = rows // SUB + 2
+        packed = [[jnp.zeros((SUB, LANES), jnp.float32) for _ in range(2)] for _ in range(parts)]
+        for item, level, width, group, first in band_lanes(levels):
+            inside = (lane >= first) & (lane < first + width)
+            for part in range(parts):
+                tile = ext_ref[item, level, (tiles - 1) * right, pl.ds(part * SUB + GUARD, SUB)]
                 moved = pltpu.roll(tile, (first + right * width) % LANES, 1)
-                packed[group] = jnp.where((lane >= first) & (lane < first + width), moved, packed[group])
+                packed[part][group] = jnp.where(inside, moved, packed[part][group])
+        for part in range(parts):
             for group in range(2):
-                band[pl.ds(row, SUB), group * LANES : (group + 1) * LANES] = packed[group]
-            return 0
-
-        lax.fori_loop(0, rows // SUB + 2, pack_rows, 0)
+                band[pl.ds(part * SUB, SUB), group * LANES : (group + 1) * LANES] = packed[part][group]
 
     for index, band in enumerate(bands):
         for right in range(2):
@@ -298,21 +301,15 @@
     lane = lax.broadcasted_iota(jnp.int32, (SUB, LANES), 1)
 
     def unpack_bands(odd):
-        def unpack_rows(part, _):
-            row = pl.multiple_of(part * SUB, SUB)
-            sources = [
-                [band[pl.ds(row, SUB), group * LANES : (group + 1) * LANES] for group in range(2)] for band in bands
-            ]
-            for item, level, width, group, first in band_lanes(levels):
+        for item, level, width, group, first in band_lanes(levels):
+            for part in range(chunks + 2):
                 value = jnp.zeros((SUB, LANES), jnp.float32)
-                for phase, source in enumerate(sources):
+                for phase, band in enumerate(bands):
                     left = odd if phase == 0 else 1 - odd
-                    moved = pltpu.roll(source[group], (2 * LANES - first - left * width) % LANES, 1)
+                    source = band[pl.ds(part * SUB, SUB), group * LANES : (group + 1) * LANES]
+                    moved = pltpu.roll(source, (2 * LANES - first - left * width) % LANES, 1)
                     value = jnp.where(lane >= LANES - width if left else lane < width, moved, value)
-                ext_ref[item, level, tiles, pl.ds(row + GUARD, SUB)] = value
-            return 0
-
-        lax.fori_loop(0, chunks + 2, unpack_rows, 0)
+                ext_ref[item, level, tiles, pl.ds(part * SUB + GUARD, SUB)] = value
 
     if step == 0:
         for odd in range(2):
@@ -422,15 +419,17 @@
             flush(made)
 
     def shift_rows(part, _):
-        here = pl.ds(pl.multiple_of(part * SUB, SUB) + GUARD, SUB)
-        for level in range(levels):
-            old = [u_ref[level, tile, here] for tile in range(ring)]
-            for tile in range(ring):
-                u_ref[level, tile, here] = ahead(old, tile, 1)
+        base = part * (chunks // 2 + 1) * SUB + GUARD
+        for index in range(chunks // 2 + 1):
+            here = pl.ds(pl.multiple_of(base + index * SUB, SUB), SUB)
+            for level in range(levels):
+                old = [u_ref[level, tile, here] for tile in range(ring)]
+                for tile in range(ring):
+                    u_ref[level, tile, here] = ahead(old, tile, 1)
         return 0
 
     if first:
-        lax.fori_loop(0, chunks + 2, shift_rows, 0)
+        lax.fori_loop(0, 2, shift_rows, 0)
     if last:
         winds(0, True)
         winds(chunks + 1, True)
@@ -558,7 +557,7 @@
             "band",
             [
                 array(ext_shape),
-                array((6 * MODES, 2 * cols), jnp.bfloat16),
+                array((2, 4 * MODES, cols), jnp.bfloat16),
                 array((2 * rows, MODES), jnp.bfloat16),
             ]
             + [array(band_shape)] * x_phases,
@@ -608,7 +607,7 @@
             [vmem] * 5,
             [
                 pltpu.VMEM((fields, half * MODES, LANES), jnp.float32),
-                pltpu.VMEM((fields, half * rows, 2 * LANES), jnp.bfloat16),
+                pltpu.VMEM((fields, 2, half * rows, 2 * LANES), jnp.bfloat16),
                 pltpu.VMEM((fields, levels, rows, cols), jnp.float32),
                 pltpu.SemaphoreType.DMA((fields, 2)),
             ],

time: 58.6 us -> 57.4 us (0.980)
  Pallas kernels: 16.6 us -> 15.2 us
    pallas_call x6, Pallas kernels: 16.6 us -> 15.2 us  [call(): pl.pallas_call(kernel, grid_spec=pltpu.PrefetchScalarGridSpec(num_scalar_...]
  transfers between devices with their start and end apart: 14 -> 14, of which waited for: 9 -> 9; matrix products, arithmetic and copies ran while one was open for 0% -> 0% of each run, Pallas kernels for 15% -> 13%
where the time goes in v2:
time: 57.4 us; the launch traced here: 57.3 us
  waiting for transfers between devices  26.3 us (46%)
  starting transfers between devices  15.3 us (27%)
  Pallas kernels  15.2 us (26%)
    pallas_call x6, Pallas kernels, call(): pl.pallas_call(kernel, grid_spec=pltpu.PrefetchScalarGridSpec(num_scalar_...  15.2 us
    ppermute x3, waiting for transfers between devices, neighbours(): return lax.ppermute(value, axis, pairs)  13.7 us
    ppermute x11, waiting for transfers between devices, swap(): lax.ppermute(value, ('gx', 'gy'), [(i, i ^ mask) for i in range(devices)])  12.6 us
    ppermute x11, starting transfers between devices, swap(): lax.ppermute(value, ('gx', 'gy'), [(i, i ^ mask) for i in range(devices)])  11.7 us
    ppermute x3, starting transfers between devices, neighbours(): return lax.ppermute(value, axis, pairs)  3.62 us
  transfers between devices with their start and end apart: 14, of which 9 were waited for; matrix products, arithmetic and copies ran while one was open for 0% of the time, Pallas kernels for 13%

profile of v2, /device:TPU:2, one launch (start us, length us, event | category | flops | bytes accessed | tf_op | source)
XLA Modules:
  0.0 57.3 jit_solution(9207205595221824619)
XLA Ops:
  0.0 4.5 %shard_map.82 = (f32[6,8,4,96,128]{4,3,2,1,0:T(8,128)S(1)}, f32[8,4,8,384]{3,2,1,0:T(8,128)S(1)}, f32[8,4,8,384]{3,2,1,0:T(8,128)S(1)}, f32[4,5,32,128]{3,2,1,0:T(8,128)S(1)}, f32[4,5,32,128]{3,2,1,0:T(8,128)S(1)}) custom-call(s32[1]{0:T(128)} %bitcast.info, f32[5,8,64,384]{3,2,1,0:T(8,128)} %refs_0_.2, f32[5,8,64,384]{3,2,1,0:T(8,128)} %refs_1_.1, ...), custom_call_target="tpu_custom_call" | custom-call | flops 600000000 | bytes 9000000 | tf_op jit(solution)/shard_map/pallas_call | solution.py:512
  4.6 1.6 %collective-permute-done.3 = f32[4,5,32,128]{3,2,1,0:T(8,128)S(1)} collective-permute-done((f32[4,5,32,128]{3,2,1,0:T(8,128)S(1)}, f32[4,5,32,128]{3,2,1,0:T(8,128)S(1)}, u32[]{:S(2)}, u32[]{:S(2)}) %collective-permute-start.3) | collective-permute-done | bytes 327712 | tf_op jit(solution)/shard_map/ppermute | solution.py:482
  6.4 3.0 %collective-permute-start.6 = (f32[1,5,32,128]{3,2,1,0:T(8,128)S(1)}, f32[1,5,32,128]{3,2,1,0:T(8,128)S(1)}, u32[]{:S(2)}, u32[]{:S(2)}) collective-permute-start(f32[1,5,32,128]{3,2,1,0:T(8,128)S(1)} %get-tuple-element.24), channel_id=1, source_target_pairs={{0,18},{1,19},{2,16},{3,17},{4,22},{5,23},{6,20},{7,21},{8,26},{9,... | collective-permute-start | bytes 245768 | tf_op jit(solution)/shard_map/ppermute | solution.py:482
  9.4 0.5 collective-permute-start.5
  9.9 1.5 %collective-permute-done.4 = f32[1,5,32,128]{3,2,1,0:T(8,128)S(1)} collective-permute-done((f32[1,5,32,128]{3,2,1,0:T(8,128)S(1)}, f32[1,5,32,128]{3,2,1,0:T(8,128)S(1)}, u32[]{:S(2)}, u32[]{:S(2)}) %collective-permute-start.4) | collective-permute-done | bytes 81952 | tf_op jit(solution)/shard_map/ppermute | solution.py:482
  11.4 2.3 %collective-permute-done.6 = f32[1,5,32,128]{3,2,1,0:T(8,128)S(1)} collective-permute-done((f32[1,5,32,128]{3,2,1,0:T(8,128)S(1)}, f32[1,5,32,128]{3,2,1,0:T(8,128)S(1)}, u32[]{:S(2)}, u32[]{:S(2)}) %collective-permute-start.6) | collective-permute-done | bytes 81952 | tf_op jit(solution)/shard_map/ppermute | solution.py:482
  13.7 1.1 %collective-permute-done.5 = f32[1,5,32,128]{3,2,1,0:T(8,128)S(1)} collective-permute-done((f32[1,5,32,128]{3,2,1,0:T(8,128)S(1)}, f32[1,5,32,128]{3,2,1,0:T(8,128)S(1)}, u32[]{:S(2)}, u32[]{:S(2)}) %collective-permute-start.5) | collective-permute-done | bytes 81952 | tf_op jit(solution)/shard_map/ppermute | solution.py:482
  14.8 3.7 %collective-permute-start.9 = (f32[1,5,32,128]{3,2,1,0:T(8,128)S(1)}, f32[1,5,32,128]{3,2,1,0:T(8,128)S(1)}, u32[]{:S(2)}, u32[]{:S(2)}) collective-permute-start(f32[1,5,32,128]{3,2,1,0:T(8,128)S(1)} %fusion.1), channel_id=1, source_target_pairs={{0,12},{1,13},{2,14},{3,15},{4,8},{5,9},{6,10},{7,11},{8,4},{9,5},... | collective-permute-start | bytes 245768 | tf_op jit(solution)/shard_map/ppermute | solution.py:482
  18.5 0.8 %collective-permute-start.7 = (f32[1,5,32,128]{3,2,1,0:T(8,128)S(1)}, f32[1,5,32,128]{3,2,1,0:T(8,128)S(1)}, u32[]{:S(2)}, u32[]{:S(2)}) collective-permute-start(f32[1,5,32,128]{3,2,1,0:T(8,128)S(1)} %fusion.1), channel_id=1, source_target_pairs={{0,4},{1,5},{2,6},{3,7},{4,0},{5,1},{6,2},{7,3},{8,12},{9,13},{10,... | collective-permute-start | bytes 245768 | tf_op jit(solution)/shard_map/ppermute | solution.py:482
  19.2 2.7 %collective-permute-done.9 = f32[1,5,32,128]{3,2,1,0:T(8,128)S(1)} collective-permute-done((f32[1,5,32,128]{3,2,1,0:T(8,128)S(1)}, f32[1,5,32,128]{3,2,1,0:T(8,128)S(1)}, u32[]{:S(2)}, u32[]{:S(2)}) %collective-permute-start.9) | collective-permute-done | bytes 81952 | tf_op jit(solution)/shard_map/ppermute | solution.py:482
  22.0 3.0 %collective-permute-done.8 = f32[1,5,32,128]{3,2,1,0:T(8,128)S(1)} collective-permute-done((f32[1,5,32,128]{3,2,1,0:T(8,128)S(1)}, f32[1,5,32,128]{3,2,1,0:T(8,128)S(1)}, u32[]{:S(2)}, u32[]{:S(2)}) %collective-permute-start.8) | collective-permute-done | bytes 81952 | tf_op jit(solution)/shard_map/ppermute | solution.py:482
  25.0 0.7 %collective-permute-start.12 = (f32[1,5,32,128]{3,2,1,0:T(8,128)S(1)}, f32[1,5,32,128]{3,2,1,0:T(8,128)S(1)}, u32[]{:S(2)}, u32[]{:S(2)}) collective-permute-start(f32[1,5,32,128]{3,2,1,0:T(8,128)S(1)} %add_add_fusion), channel_id=1, source_target_pairs={{0,18},{1,19},{2,16},{3,17},{4,22},{5,23},{6,20},{7,21},{8,26},{9,... | collective-permute-start | bytes 245768 | tf_op jit(solution)/shard_map/ppermute | solution.py:482
  25.6 1.6 %collective-permute-start.11 = (f32[1,5,32,128]{3,2,1,0:T(8,128)S(1)}, f32[1,5,32,128]{3,2,1,0:T(8,128)S(1)}, u32[]{:S(2)}, u32[]{:S(2)}) collective-permute-start(f32[1,5,32,128]{3,2,1,0:T(8,128)S(1)} %add_add_fusion), channel_id=1, source_target_pairs={{0,16},{1,17},{2,18},{3,19},{4,20},{5,21},{6,22},{7,23},{8,24},{9,... | collective-permute-start | bytes 245768 | tf_op jit(solution)/shard_map/ppermute | solution.py:482
  27.3 1.3 %collective-permute-start.10 = (f32[1,5,32,128]{3,2,1,0:T(8,128)S(1)}, f32[1,5,32,128]{3,2,1,0:T(8,128)S(1)}, u32[]{:S(2)}, u32[]{:S(2)}) collective-permute-start(f32[1,5,32,128]{3,2,1,0:T(8,128)S(1)} %add_add_fusion), channel_id=1, source_target_pairs={{0,2},{1,3},{2,0},{3,1},{4,6},{5,7},{6,4},{7,5},{8,10},{9,11},{10,... | collective-permute-start | bytes 245768 | tf_op jit(solution)/shard_map/ppermute | solution.py:482
  28.5 2.8 %collective-permute-start.1 = (f32[8,4,8,384]{3,2,1,0:T(8,128)S(1)}, f32[8,4,8,384]{3,2,1,0:T(8,128)S(1)}, u32[]{:S(2)}, u32[]{:S(2)}) collective-permute-start(f32[8,4,8,384]{3,2,1,0:T(8,128)S(1)} %get-tuple-element.16), channel_id=1, source_target_pairs={{1,2},{2,1},{3,4},{4,3},{5,6},{6,5},{7,8},{8,7},{9,10},{10,9},{11,... | collective-permute-start | bytes 1179656 | tf_op jit(solution)/shard_map/ppermute | solution.py:488
  31.3 0.4 collective-permute-done.10
  31.8 10.0 %collective-permute-done.1.refs_2_ = f32[8,4,8,384]{3,2,1,0:T(8,128)S(1)} collective-permute-done((f32[8,4,8,384]{3,2,1,0:T(8,128)S(1)}, f32[8,4,8,384]{3,2,1,0:T(8,128)S(1)}, u32[]{:S(2)}, u32[]{:S(2)}) %collective-permute-start.1) | collective-permute-done | bytes 393248 | tf_op jit(solution)/shard_map/ppermute | solution.py:488
  41.8 1.3 %shard_map.83 = (f32[6,8,4,96,128]{4,3,2,1,0:T(8,128)S(1)}, bf16[2,256,384]{2,1,0:T(8,128)(2,1)S(1)}, bf16[128,64]{1,0:T(8,128)(2,1)S(1)}, f32[80,256]{1,0:T(8,128)S(1)}) custom-call(s32[1]{0:T(128)} %bitcast.info, f32[6,8,4,96,128]{4,3,2,1,0:T(8,128)S(1)} %get-tuple-element.14.refs_0_, ...), custom_call_target="tpu_custom_call", output_to_operand_aliasing={{0}: (1, {})} | custom-call | flops 1000000 | bytes 10000000 | tf_op jit(solution)/shard_map/pallas_call | solution.py:512
  43.1 0.8 %collective-permute-start.2 = (f32[80,256]{1,0:T(8,128)S(1)}, f32[80,256]{1,0:T(8,128)S(1)}, u32[]{:S(2)}, u32[]{:S(2)}) collective-permute-start(f32[80,256]{1,0:T(8,128)S(1)} %get-tuple-element.18), channel_id=1, source_target_pairs={{0,16},{16,0},{1,17},{17,1},{2,18},{18,2},{3,19},{19,3},{4,20},{20... | collective-permute-start | bytes 245768 | tf_op jit(solution)/shard_map/ppermute | solution.py:488
  44.0 3.7 %collective-permute-done.2.refs_1_ = f32[80,256]{1,0:T(8,128)S(1)} collective-permute-done((f32[80,256]{1,0:T(8,128)S(1)}, f32[80,256]{1,0:T(8,128)S(1)}, u32[]{:S(2)}, u32[]{:S(2)}) %collective-permute-start.2) | collective-permute-done | bytes 81952 | tf_op jit(solution)/shard_map/ppermute | solution.py:488
  47.6 3.1 %shard_map.84.refs_0_ = f32[6,8,4,96,128]{4,3,2,1,0:T(8,128)S(1)} custom-call(s32[1]{0:T(128)} %bitcast.info, f32[6,8,4,96,128]{4,3,2,1,0:T(8,128)S(1)} %get-tuple-element.17.refs_0_, f32[80,256]{1,0:T(8,128)S(1)} %collective-permute-done.2.refs_1_), custom_call_target="tpu_custom_call", output_to_operand_aliasing={{}: (1, {})} | custom-call | flops 10000000 | bytes 8000000 | tf_op jit(solution)/shard_map/pallas_call | solution.py:512
  50.7 1.8 %shard_map.85.refs_0_ = f32[6,8,4,96,128]{4,3,2,1,0:T(8,128)S(1)} custom-call(s32[1]{0:T(128)} %bitcast.info, f32[6,8,4,96,128]{4,3,2,1,0:T(8,128)S(1)} %shard_map.84.refs_0_), custom_call_target="tpu_custom_call", output_to_operand_aliasing={{}: (1, {})} | custom-call | flops 10000000 | bytes 8000000 | tf_op jit(solution)/shard_map/pallas_call | solution.py:512
  52.6 1.2 %shard_map.86.refs_1_ = f32[6,8,4,96,128]{4,3,2,1,0:T(8,128)S(1)} custom-call(s32[1]{0:T(128)} %bitcast.info, f32[6,8,4,96,128]{4,3,2,1,0:T(8,128)S(1)} %shard_map.85.refs_0_), custom_call_target="tpu_custom_call", output_to_operand_aliasing={{}: (1, {})} | custom-call | flops 10000000 | bytes 8000000 | tf_op jit(solution)/shard_map/pallas_call | solution.py:512
  53.7 3.4 %shard_map.87 = f32[5,8,64,384]{3,2,1,0:T(8,128)} custom-call(s32[1]{0:T(128)} %bitcast.info, f32[5,8]{1,0:T(8,128)S(1)} %copy-done.2, f32[6,8,4,96,128]{4,3,2,1,0:T(8,128)S(1)} %shard_map.86.refs_1_, f32[4,5,32,128]{3,2,1,0:T(8,128)S(1)} %pad_maximum_fusion.refs_2_, f32[4,5,32,128]{3,2,1,0:T(8,128)S(1)} %collective-permute-done.13.refs_3_, ...), custom_call_target="tpu_custom_call" | custom-call | flops 600000000 | bytes 8500000 | tf_op jit(solution)/shard_map/pallas_call | solution.py:512
  (21 shorter events, 0.4 us)
Async XLA Ops:
  0.0 41.8 %copy-start = (bf16[16,128,64]{2,1,0:T(8,128)(2,1)S(1)}, bf16[16,128,64]{2,1,0:T(8,128)(2,1)}, u32[]{:S(2)}) copy-start(bf16[16,128,64]{2,1,0:T(8,128)(2,1)} %constant.22.clone.refs_4_) | copy-start | bytes 786436
  0.0 41.8 %copy-start.1 = (bf16[2,2,64,384]{3,2,1,0:T(8,128)(2,1)S(1)}, bf16[2,2,64,384]{3,2,1,0:T(8,128)(2,1)}, u32[]{:S(2)}) copy-start(bf16[2,2,64,384]{3,2,1,0:T(8,128)(2,1)} %constant.21.clone.refs_3_) | copy-start | bytes 589828
  4.5 1.7 %collective-permute-start.3 = (f32[4,5,32,128]{3,2,1,0:T(8,128)S(1)}, f32[4,5,32,128]{3,2,1,0:T(8,128)S(1)}, u32[]{:S(2)}, u32[]{:S(2)}) collective-permute-start(f32[4,5,32,128]{3,2,1,0:T(8,128)S(1)} %get-tuple-element.20), channel_id=1, source_target_pairs={{0,1},{1,0},{2,3},{3,2},{4,5},{5,4},{6,7},{7,6},{8,9},{9,8},{10,11... | collective-permute-start | bytes 983048 | tf_op jit(solution)/shard_map/ppermute | solution.py:482
  6.3 5.1 %collective-permute-start.4 = (f32[1,5,32,128]{3,2,1,0:T(8,128)S(1)}, f32[1,5,32,128]{3,2,1,0:T(8,128)S(1)}, u32[]{:S(2)}, u32[]{:S(2)}) collective-permute-start(f32[1,5,32,128]{3,2,1,0:T(8,128)S(1)} %get-tuple-element.23), channel_id=1, source_target_pairs={{0,2},{1,3},{2,0},{3,1},{4,6},{5,7},{6,4},{7,5},{8,10},{9,11},{10,... | collective-permute-start | bytes 245768 | tf_op jit(solution)/shard_map/ppermute | solution.py:482
  6.4 7.3 %collective-permute-start.6 = (f32[1,5,32,128]{3,2,1,0:T(8,128)S(1)}, f32[1,5,32,128]{3,2,1,0:T(8,128)S(1)}, u32[]{:S(2)}, u32[]{:S(2)}) collective-permute-start(f32[1,5,32,128]{3,2,1,0:T(8,128)S(1)} %get-tuple-element.24), channel_id=1, source_target_pairs={{0,18},{1,19},{2,16},{3,17},{4,22},{5,23},{6,20},{7,21},{8,26},{9,... | collective-permute-start | bytes 245768 | tf_op jit(solution)/shard_map/ppermute | solution.py:482
  9.4 5.4 %collective-permute-start.5 = (f32[1,5,32,128]{3,2,1,0:T(8,128)S(1)}, f32[1,5,32,128]{3,2,1,0:T(8,128)S(1)}, u32[]{:S(2)}, u32[]{:S(2)}) collective-permute-start(f32[1,5,32,128]{3,2,1,0:T(8,128)S(1)} %get-tuple-element.25), channel_id=1, source_target_pairs={{0,16},{1,17},{2,18},{3,19},{4,20},{5,21},{6,22},{7,23},{8,24},{9,... | collective-permute-start | bytes 245768 | tf_op jit(solution)/shard_map/ppermute | solution.py:482
  14.8 7.2 %collective-permute-start.9 = (f32[1,5,32,128]{3,2,1,0:T(8,128)S(1)}, f32[1,5,32,128]{3,2,1,0:T(8,128)S(1)}, u32[]{:S(2)}, u32[]{:S(2)}) collective-permute-start(f32[1,5,32,128]{3,2,1,0:T(8,128)S(1)} %fusion.1), channel_id=1, source_target_pairs={{0,12},{1,13},{2,14},{3,15},{4,8},{5,9},{6,10},{7,11},{8,4},{9,5},... | collective-permute-start | bytes 245768 | tf_op jit(solution)/shard_map/ppermute | solution.py:482
  18.5 6.5 %collective-permute-start.8 = (f32[1,5,32,128]{3,2,1,0:T(8,128)S(1)}, f32[1,5,32,128]{3,2,1,0:T(8,128)S(1)}, u32[]{:S(2)}, u32[]{:S(2)}) collective-permute-start(f32[1,5,32,128]{3,2,1,0:T(8,128)S(1)} %fusion.1), channel_id=1, source_target_pairs={{0,8},{1,9},{2,10},{3,11},{4,12},{5,13},{6,14},{7,15},{8,0},{9,1},... | collective-permute-start | bytes 245768 | tf_op jit(solution)/shard_map/ppermute | solution.py:482
  18.5 6.5 %collective-permute-start.7 = (f32[1,5,32,128]{3,2,1,0:T(8,128)S(1)}, f32[1,5,32,128]{3,2,1,0:T(8,128)S(1)}, u32[]{:S(2)}, u32[]{:S(2)}) collective-permute-start(f32[1,5,32,128]{3,2,1,0:T(8,128)S(1)} %fusion.1), channel_id=1, source_target_pairs={{0,4},{1,5},{2,6},{3,7},{4,0},{5,1},{6,2},{7,3},{8,12},{9,13},{10,... | collective-permute-start | bytes 245768 | tf_op jit(solution)/shard_map/ppermute | solution.py:482
  25.0 6.3 %collective-permute-start.12 = (f32[1,5,32,128]{3,2,1,0:T(8,128)S(1)}, f32[1,5,32,128]{3,2,1,0:T(8,128)S(1)}, u32[]{:S(2)}, u32[]{:S(2)}) collective-permute-start(f32[1,5,32,128]{3,2,1,0:T(8,128)S(1)} %add_add_fusion), channel_id=1, source_target_pairs={{0,18},{1,19},{2,16},{3,17},{4,22},{5,23},{6,20},{7,21},{8,26},{9,... | collective-permute-start | bytes 245768 | tf_op jit(solution)/shard_map/ppermute | solution.py:482
  25.6 5.7 %collective-permute-start.11 = (f32[1,5,32,128]{3,2,1,0:T(8,128)S(1)}, f32[1,5,32,128]{3,2,1,0:T(8,128)S(1)}, u32[]{:S(2)}, u32[]{:S(2)}) collective-permute-start(f32[1,5,32,128]{3,2,1,0:T(8,128)S(1)} %add_add_fusion), channel_id=1, source_target_pairs={{0,16},{1,17},{2,18},{3,19},{4,20},{5,21},{6,22},{7,23},{8,24},{9,... | collective-permute-start | bytes 245768 | tf_op jit(solution)/shard_map/ppermute | solution.py:482
  27.3 4.4 %collective-permute-start.10 = (f32[1,5,32,128]{3,2,1,0:T(8,128)S(1)}, f32[1,5,32,128]{3,2,1,0:T(8,128)S(1)}, u32[]{:S(2)}, u32[]{:S(2)}) collective-permute-start(f32[1,5,32,128]{3,2,1,0:T(8,128)S(1)} %add_add_fusion), channel_id=1, source_target_pairs={{0,2},{1,3},{2,0},{3,1},{4,6},{5,7},{6,4},{7,5},{8,10},{9,11},{10,... | collective-permute-start | bytes 245768 | tf_op jit(solution)/shard_map/ppermute | solution.py:482
  28.5 3.3 %collective-permute-start = (f32[8,4,8,384]{3,2,1,0:T(8,128)S(1)}, f32[8,4,8,384]{3,2,1,0:T(8,128)S(1)}, u32[]{:S(2)}, u32[]{:S(2)}) collective-permute-start(f32[8,4,8,384]{3,2,1,0:T(8,128)S(1)} %get-tuple-element.15), channel_id=1, source_target_pairs={{0,1},{1,0},{2,3},{3,2},{4,5},{5,4},{6,7},{7,6},{8,9},{9,8},{10,11... | collective-permute-start | bytes 1179656 | tf_op jit(solution)/shard_map/ppermute | solution.py:488
  28.5 13.3 %collective-permute-start.1 = (f32[8,4,8,384]{3,2,1,0:T(8,128)S(1)}, f32[8,4,8,384]{3,2,1,0:T(8,128)S(1)}, u32[]{:S(2)}, u32[]{:S(2)}) collective-permute-start(f32[8,4,8,384]{3,2,1,0:T(8,128)S(1)} %get-tuple-element.16), channel_id=1, source_target_pairs={{1,2},{2,1},{3,4},{4,3},{5,6},{6,5},{7,8},{8,7},{9,10},{10,9},{11,... | collective-permute-start | bytes 1179656 | tf_op jit(solution)/shard_map/ppermute | solution.py:488
  31.7 22.0 %collective-permute-start.13 = (f32[4,5,32,128]{3,2,1,0:T(8,128)S(1)}, f32[4,5,32,128]{3,2,1,0:T(8,128)S(1)}, u32[]{:S(2)}, u32[]{:S(2)}) collective-permute-start(f32[4,5,32,128]{3,2,1,0:T(8,128)S(1)} %pad_maximum_fusion.refs_2_), channel_id=1, source_target_pairs={{0,1},{1,0},{2,3},{3,2},{4,5},{5,4},{6,7},{7,6},{8,9},{9,8},{10,11... | collective-permute-start | bytes 983048 | tf_op jit(solution)/shard_map/ppermute | solution.py:482
  43.1 4.5 %collective-permute-start.2 = (f32[80,256]{1,0:T(8,128)S(1)}, f32[80,256]{1,0:T(8,128)S(1)}, u32[]{:S(2)}, u32[]{:S(2)}) collective-permute-start(f32[80,256]{1,0:T(8,128)S(1)} %get-tuple-element.18), channel_id=1, source_target_pairs={{0,16},{16,0},{1,17},{17,1},{2,18},{18,2},{3,19},{19,3},{4,20},{20... | collective-permute-start | bytes 245768 | tf_op jit(solution)/shard_map/ppermute | solution.py:488
  52.5 1.2 %copy-start.2 = (f32[5,8]{1,0:T(8,128)S(1)}, f32[5,8]{1,0:T(8,128)}, u32[]{:S(2)}) copy-start(f32[5,8]{1,0:T(8,128)} %refs_0_.3) | copy-start | bytes 484

commit v3 on v2

--- a/solution.py
+++ b/solution.py
@@ -192,7 +192,10 @@
         modes_ref[:, pl.ds(target, chunk)] = source[piece % (pieces // 2)]
     lane = lax.broadcasted_iota(jnp.int32, (MODES, LANES), 1)
     lower = lax.broadcasted_iota(jnp.int32, (rows, LANES), 1) < MODES
-    for field in range(fields):
+    main = pl.ds(GUARD + SUB, rows)
+    last_lane = lax.broadcasted_iota(jnp.int32, (rows, LANES), 1) == LANES - 1
+
+    def back(field):
         for pair in range(half):
             factor = jnp.where(lane < MODES, rate_ref[field, pair], rate_ref[field, pair + half])
             high, low = split(modes_ref[field, pair * MODES : (pair + 1) * MODES] * factor)
@@ -206,10 +209,12 @@
             back_ref[field, 1, here, :LANES] = jnp.where(lower, high_turned, low)
             for side in range(2):
                 back_ref[field, side, here, LANES:] = high
-    main = pl.ds(GUARD + SUB, rows)
-    last_lane = lax.broadcasted_iota(jnp.int32, (rows, LANES), 1) == LANES - 1
+
+    back(0)
     stores = []
     for field in range(fields):
+        if field + 1 < fields:
+            back(field + 1)
         for level in range(levels):
             if level % half == 0:
                 side = level // half
@@ -238,11 +243,43 @@
             yield item, level, REACH_X[item], GROUP_X[item], starts[item] + REACH_X[item] * level
 
 
-def band_kernel(facts, _, a_ref, b_ref, bx_hbm, by_hbm, ext_ref, wide_ref, by_ref, *refs, rows, cols):
+def pack_bands(facts, bands, ext_ref, parts, tiles):
+    levels = ext_ref.shape[1]
+    lane = lax.broadcasted_iota(jnp.int32, (SUB, LANES), 1)
+
+    def pack(band, right):
+        packed = [[jnp.zeros((SUB, LANES), jnp.float32) for _ in range(2)] for _ in parts]
+        for item, level, width, group, first in band_lanes(levels):
+            inside = (lane >= first) & (lane < first + width)
+            for place, part in enumerate(parts):
+                tile = ext_ref[item, level, (tiles - 1) * right, pl.ds(part * SUB + GUARD, SUB)]
+                moved = pltpu.roll(tile, (first + right * width) % LANES, 1)
+                packed[place][group] = jnp.where(inside, moved, packed[place][group])
+        for place, part in enumerate(parts):
+            for group in range(2):
+                band[pl.ds(part * SUB, SUB), group * LANES : (group + 1) * LANES] = packed[place][group]
+
+    for index, band in enumerate(bands):
+        for right in range(2):
+            pl.when((facts[3] ^ index) == right)(functools.partial(pack, band, right))
+
+
+def shift_down(ext_ref, parts, tiles):
+    lane = lax.broadcasted_iota(jnp.int32, (SUB, LANES), 1)
+    for part in parts:
+        here = pl.ds(part * SUB + GUARD, SUB)
+        for level in range(ext_ref.shape[1]):
+            old = [ext_ref[0, level, tile, here] for tile in range(tiles)]
+            old += [old[0], old[0]]
+            for tile in range(tiles + 1):
+                value = old[tile] if tile >= tiles - 1 else jnp.where(lane == 0, old[tile + 1], old[tile])
+                ext_ref[0, level, tile, here] = pltpu.roll(value, LANES - 1, 1)
+
+
+def prepare_kernel(facts, _, bx_hbm, by_hbm, ext_ref, wide_ref, by_ref, *refs, rows, cols):
     *bands, sem = refs
     levels = ext_ref.shape[1]
     tiles = cols // LANES
-    main = GUARD + SUB
     tables = [pltpu.make_async_copy(by_hbm.at[facts[1]], by_ref, sem.at[3, 0])]
     for side in range(2):
         for block, part in ((0, 0), (1, 0), (2 + side, 1)):
@@ -257,41 +294,37 @@
         for level in range(levels):
             for tile in range(tiles + 1):
                 ext_ref[item, level, tile, pl.ds(0, SUB)] = zero
-                ext_ref[item, level, tile, pl.ds(main + rows + SUB, SUB)] = zero
+                ext_ref[item, level, tile, pl.ds(GUARD + 2 * SUB + rows, SUB)] = zero
+    parts = range(1, rows // SUB + 1)
+    pack_bands(facts, bands, ext_ref, parts, tiles)
+    shift_down(ext_ref, parts, tiles)
+    for copy in tables:
+        copy.wait()
+
+
+def band_kernel(facts, *refs, x_phases, slabs, rows, cols):
+    a_ref, b_refs = refs[1 + x_phases], refs[2 + x_phases : 2 + x_phases + slabs]
+    ext_ref, *bands = refs[2 + x_phases + slabs :]
+    levels = ext_ref.shape[1]
+    tiles = cols // LANES
 
     def place_slabs(odd):
-        for phase, slab in enumerate((a_ref, b_ref)):
-            base = GUARD if (odd == 1) == (phase == 0) else main + rows
+        for phase, sources in enumerate(((a_ref,), b_refs)):
+            base = GUARD if (odd == 1) == (phase == 0) else GUARD + SUB + rows
             for item, place, turn in ((3, 0, 0), (1, 1, 0), (0, 2, 0), (2, 2, 4), (4, 3, 0), (5, 3, 4)):
                 for level in range(levels):
                     for tile in range(tiles):
-                        value = slab[level, place, :, tile * LANES : (tile + 1) * LANES]
+                        lanes = slice(tile * LANES, (tile + 1) * LANES)
+                        value = functools.reduce(jnp.add, [ref[level, place, :, lanes] for ref in sources])
                         if turn:
                             value = pltpu.roll(value, turn, 0)
                         ext_ref[item, level, tile, pl.ds(base, SUB)] = value
 
     for odd in range(2):
         pl.when(facts[6] == odd)(functools.partial(place_slabs, odd))
-    lane = lax.broadcasted_iota(jnp.int32, (SUB, LANES), 1)
-
-    def pack_band(band, right):
-        parts = rows // SUB + 2
-        packed = [[jnp.zeros((SUB, LANES), jnp.float32) for _ in range(2)] for _ in range(parts)]
-        for item, level, width, group, first in band_lanes(levels):
-            inside = (lane >= first) & (lane < first + width)
-            for part in range(parts):
-                tile = ext_ref[item, level, (tiles - 1) * right, pl.ds(part * SUB + GUARD, SUB)]
-                moved = pltpu.roll(tile, (first + right * width) % LANES, 1)
-                packed[part][group] = jnp.where(inside, moved, packed[part][group])
-        for part in range(parts):
-            for group in range(2):
-                band[pl.ds(part * SUB, SUB), group * LANES : (group + 1) * LANES] = packed[part][group]
-
-    for index, band in enumerate(bands):
-        for right in range(2):
-            pl.when((facts[3] ^ index) == right)(functools.partial(pack_band, band, right))
-    for copy in tables:
-        copy.wait()
+    parts = (0, rows // SUB + 1)
+    pack_bands(facts, bands, ext_ref, parts, tiles)
+    shift_down(ext_ref, parts, tiles)
 
 
 def substep_kernel(facts, *refs, step, levels, rows, cols):
@@ -302,14 +335,26 @@
 
     def unpack_bands(odd):
         for item, level, width, group, first in band_lanes(levels):
+            down = 1 if item == 0 else 0
             for part in range(chunks + 2):
-                value = jnp.zeros((SUB, LANES), jnp.float32)
+                here = pl.ds(part * SUB + GUARD, SUB)
+                value = edge = jnp.zeros((SUB, LANES), jnp.float32)
+                if down:
+                    value = jnp.where(lane == LANES - 1, ext_ref[0, level, tiles, here], value)
                 for phase, band in enumerate(bands):
                     left = odd if phase == 0 else 1 - odd
                     source = band[pl.ds(part * SUB, SUB), group * LANES : (group + 1) * LANES]
-                    moved = pltpu.roll(source, (2 * LANES - first - left * width) % LANES, 1)
-                    value = jnp.where(lane >= LANES - width if left else lane < width, moved, value)
-                ext_ref[item, level, tiles, pl.ds(part * SUB + GUARD, SUB)] = value
+                    moved = pltpu.roll(source, (2 * LANES - first - left * width - down) % LANES, 1)
+                    if left:
+                        inside = (lane >= LANES - width - down) & (lane < LANES - down)
+                    else:
+                        inside = lane < width - down
+                        edge = moved
+                    value = jnp.where(inside, moved, value)
+                ext_ref[item, level, tiles, here] = value
+                if down:
+                    old = ext_ref[0, level, tiles - 1, here]
+                    ext_ref[0, level, tiles - 1, here] = jnp.where(lane == LANES - 1, edge, old)
 
     if step == 0:
         for odd in range(2):
@@ -418,18 +463,6 @@
             before, now = now, after
             flush(made)
 
-    def shift_rows(part, _):
-        base = part * (chunks // 2 + 1) * SUB + GUARD
-        for index in range(chunks // 2 + 1):
-            here = pl.ds(pl.multiple_of(base + index * SUB, SUB), SUB)
-            for level in range(levels):
-                old = [u_ref[level, tile, here] for tile in range(ring)]
-                for tile in range(ring):
-                    u_ref[level, tile, here] = ahead(old, tile, 1)
-        return 0
-
-    if first:
-        lax.fori_loop(0, 2, shift_rows, 0)
     if last:
         winds(0, True)
         winds(chunks + 1, True)
@@ -481,10 +514,11 @@
     def swap(value, mask):
         return lax.ppermute(value, ("gx", "gy"), [(i, i ^ mask) for i in range(devices)])
 
-    def neighbours(value, axis, count, phase):
+    def neighbours(value, axis, count, phase, far=None):
         pairs = []
         for low in range(phase, count - 1, 2):
-            pairs += [(low, low + 1), (low + 1, low)]
+            if far is None or ((low + 1) % 4 == 0) == far:
+                pairs += [(low, low + 1), (low + 1, low)]
         return lax.ppermute(value, axis, pairs)
 
     def on_device(state, driving, rate, sound_square):
@@ -550,23 +584,34 @@
             9_000_000,
         )
         slab_a = neighbours(slab_a, "gy", ny, 0)
-        slab_b = neighbours(slab_b, "gy", ny, 1)
+        slabs_b = [
+            neighbours(slab_b, "gy", ny, 1, far)
+            for far in (True, False)
+            if any(((low + 1) % 4 == 0) == far for low in range(1, ny - 1, 2))
+        ]
 
         ext, wide, back, *bands = call(
-            informed(band_kernel, rows=rows, cols=cols),
+            informed(prepare_kernel, rows=rows, cols=cols),
+            "prepare",
+            [array(ext_shape), array((2, 4 * MODES, cols), jnp.bfloat16), array((2 * rows, MODES), jnp.bfloat16)]
+            + [array(band_shape)] * x_phases,
+            [vmem, hbm, hbm],
+            [pltpu.SemaphoreType.DMA((4, 2))],
+            (info, ext, bx, by),
+            1_000_000,
+            5_000_000,
+            aliases={1: 0},
+        )
+        ext, *bands = call(
+            informed(band_kernel, x_phases=x_phases, slabs=len(slabs_b), rows=rows, cols=cols),
             "band",
-            [
-                array(ext_shape),
-                array((2, 4 * MODES, cols), jnp.bfloat16),
-                array((2 * rows, MODES), jnp.bfloat16),
-            ]
-            + [array(band_shape)] * x_phases,
-            [vmem, vmem, vmem, hbm, hbm],
-            [pltpu.SemaphoreType.DMA((4, 2))],
-            (info, ext, slab_a, slab_b, bx, by),
+            [array(ext_shape)] + [array(band_shape)] * x_phases,
+            [vmem] * (2 + x_phases + len(slabs_b)),
+            [],
+            (info, ext, *bands, slab_a, *slabs_b),
             1_000_000,
-            10_000_000,
-            aliases={1: 0},
+            5_000_000,
+            aliases={1 + index: index for index in range(1 + x_phases)},
         )
         bands = [neighbours(band, "gx", nx, index) for index, band in enumerate(bands)]
 

time: 57.4 us -> 56.8 us (0.990)
  waiting for transfers between devices: 26.3 us -> 22.7 us
  starting transfers between devices: 15.3 us -> 17.5 us
  Pallas kernels: 15.2 us -> 15.9 us
    ppermute x3 -> x4, waiting for transfers between devices: 13.7 us -> 10.5 us  [neighbours(): return lax.ppermute(value, axis, pairs)]
    ppermute x11, starting transfers between devices: 11.7 us -> 13.2 us  [swap(): lax.ppermute(value, ('gx', 'gy'), [(i, i ^ mask) for i in range(devices)])]
    ppermute x3 -> x4, starting transfers between devices: 3.62 us -> 4.32 us  [neighbours(): return lax.ppermute(value, axis, pairs)]
    pallas_call x6 -> x7, Pallas kernels: 15.2 us -> 15.9 us  [call(): pl.pallas_call(kernel, grid_spec=pltpu.PrefetchScalarGridSpec(num_scalar_...]
  transfers between devices with their start and end apart: 14 -> 15, of which waited for: 9 -> 8; matrix products, arithmetic and copies ran while one was open for 0% -> 0% of each run, Pallas kernels for 13% -> 13%
where the time goes in v3:
time: 56.8 us; the launch traced here: 56.6 us
  waiting for transfers between devices  22.7 us (40%)
  starting transfers between devices  17.5 us (31%)
  Pallas kernels  15.9 us (28%)
    pallas_call x7, Pallas kernels, call(): pl.pallas_call(kernel, grid_spec=pltpu.PrefetchScalarGridSpec(num_scalar_...  15.9 us
    ppermute x11, starting transfers between devices, swap(): lax.ppermute(value, ('gx', 'gy'), [(i, i ^ mask) for i in range(devices)])  13.2 us
    ppermute x11, waiting for transfers between devices, swap(): lax.ppermute(value, ('gx', 'gy'), [(i, i ^ mask) for i in range(devices)])  12.2 us
    ppermute x4, waiting for transfers between devices, neighbours(): return lax.ppermute(value, axis, pairs)  10.5 us
    ppermute x4, starting transfers between devices, neighbours(): return lax.ppermute(value, axis, pairs)  4.32 us
  transfers between devices with their start and end apart: 15, of which 8 were waited for; matrix products, arithmetic and copies ran while one was open for 0% of the time, Pallas kernels for 13%

profile of v3, /device:TPU:2, one launch (start us, length us, event | category | flops | bytes accessed | tf_op | source)
XLA Modules:
  0.0 56.6 jit_solution(8240479496087863767)
XLA Ops:
  0.0 4.5 %shard_map.82 = (f32[6,8,4,96,128]{4,3,2,1,0:T(8,128)S(1)}, f32[8,4,8,384]{3,2,1,0:T(8,128)S(1)}, f32[8,4,8,384]{3,2,1,0:T(8,128)S(1)}, f32[4,5,32,128]{3,2,1,0:T(8,128)S(1)}, f32[4,5,32,128]{3,2,1,0:T(8,128)S(1)}) custom-call(s32[1]{0:T(128)} %bitcast.info, f32[5,8,64,384]{3,2,1,0:T(8,128)} %refs_0_.2, f32[5,8,64,384]{3,2,1,0:T(8,128)} %refs_1_.2, ...), custom_call_target="tpu_custom_call" | custom-call | flops 600000000 | bytes 9000000 | tf_op jit(solution)/shard_map/pallas_call | solution.py:546
  4.6 1.6 %collective-permute-done.4 = f32[4,5,32,128]{3,2,1,0:T(8,128)S(1)} collective-permute-done((f32[4,5,32,128]{3,2,1,0:T(8,128)S(1)}, f32[4,5,32,128]{3,2,1,0:T(8,128)S(1)}, u32[]{:S(2)}, u32[]{:S(2)}) %collective-permute-start.4) | collective-permute-done | bytes 327712 | tf_op jit(solution)/shard_map/ppermute | solution.py:515
  6.4 3.0 %collective-permute-start.7 = (f32[1,5,32,128]{3,2,1,0:T(8,128)S(1)}, f32[1,5,32,128]{3,2,1,0:T(8,128)S(1)}, u32[]{:S(2)}, u32[]{:S(2)}) collective-permute-start(f32[1,5,32,128]{3,2,1,0:T(8,128)S(1)} %get-tuple-element.28), channel_id=1, source_target_pairs={{0,18},{1,19},{2,16},{3,17},{4,22},{5,23},{6,20},{7,21},{8,26},{9,... | collective-permute-start | bytes 245768 | tf_op jit(solution)/shard_map/ppermute | solution.py:515
  9.9 1.5 %collective-permute-done.5 = f32[1,5,32,128]{3,2,1,0:T(8,128)S(1)} collective-permute-done((f32[1,5,32,128]{3,2,1,0:T(8,128)S(1)}, f32[1,5,32,128]{3,2,1,0:T(8,128)S(1)}, u32[]{:S(2)}, u32[]{:S(2)}) %collective-permute-start.5) | collective-permute-done | bytes 81952 | tf_op jit(solution)/shard_map/ppermute | solution.py:515
  11.4 2.3 %collective-permute-done.7 = f32[1,5,32,128]{3,2,1,0:T(8,128)S(1)} collective-permute-done((f32[1,5,32,128]{3,2,1,0:T(8,128)S(1)}, f32[1,5,32,128]{3,2,1,0:T(8,128)S(1)}, u32[]{:S(2)}, u32[]{:S(2)}) %collective-permute-start.7) | collective-permute-done | bytes 81952 | tf_op jit(solution)/shard_map/ppermute | solution.py:515
  13.7 1.1 %collective-permute-done.6 = f32[1,5,32,128]{3,2,1,0:T(8,128)S(1)} collective-permute-done((f32[1,5,32,128]{3,2,1,0:T(8,128)S(1)}, f32[1,5,32,128]{3,2,1,0:T(8,128)S(1)}, u32[]{:S(2)}, u32[]{:S(2)}) %collective-permute-start.6) | collective-permute-done | bytes 81952 | tf_op jit(solution)/shard_map/ppermute | solution.py:515
  14.8 3.7 %collective-permute-start.10 = (f32[1,5,32,128]{3,2,1,0:T(8,128)S(1)}, f32[1,5,32,128]{3,2,1,0:T(8,128)S(1)}, u32[]{:S(2)}, u32[]{:S(2)}) collective-permute-start(f32[1,5,32,128]{3,2,1,0:T(8,128)S(1)} %fusion.1), channel_id=1, source_target_pairs={{0,12},{1,13},{2,14},{3,15},{4,8},{5,9},{6,10},{7,11},{8,4},{9,5},... | collective-permute-start | bytes 245768 | tf_op jit(solution)/shard_map/ppermute | solution.py:515
  18.5 0.8 %collective-permute-start.8 = (f32[1,5,32,128]{3,2,1,0:T(8,128)S(1)}, f32[1,5,32,128]{3,2,1,0:T(8,128)S(1)}, u32[]{:S(2)}, u32[]{:S(2)}) collective-permute-start(f32[1,5,32,128]{3,2,1,0:T(8,128)S(1)} %fusion.1), channel_id=1, source_target_pairs={{0,4},{1,5},{2,6},{3,7},{4,0},{5,1},{6,2},{7,3},{8,12},{9,13},{10,... | collective-permute-start | bytes 245768 | tf_op jit(solution)/shard_map/ppermute | solution.py:515
  19.2 2.7 %collective-permute-done.10 = f32[1,5,32,128]{3,2,1,0:T(8,128)S(1)} collective-permute-done((f32[1,5,32,128]{3,2,1,0:T(8,128)S(1)}, f32[1,5,32,128]{3,2,1,0:T(8,128)S(1)}, u32[]{:S(2)}, u32[]{:S(2)}) %collective-permute-start.10) | collective-permute-done | bytes 81952 | tf_op jit(solution)/shard_map/ppermute | solution.py:515
  22.0 3.0 %collective-permute-done.9 = f32[1,5,32,128]{3,2,1,0:T(8,128)S(1)} collective-permute-done((f32[1,5,32,128]{3,2,1,0:T(8,128)S(1)}, f32[1,5,32,128]{3,2,1,0:T(8,128)S(1)}, u32[]{:S(2)}, u32[]{:S(2)}) %collective-permute-start.9) | collective-permute-done | bytes 81952 | tf_op jit(solution)/shard_map/ppermute | solution.py:515
  25.0 0.7 %collective-permute-start.13 = (f32[1,5,32,128]{3,2,1,0:T(8,128)S(1)}, f32[1,5,32,128]{3,2,1,0:T(8,128)S(1)}, u32[]{:S(2)}, u32[]{:S(2)}) collective-permute-start(f32[1,5,32,128]{3,2,1,0:T(8,128)S(1)} %add_add_fusion), channel_id=1, source_target_pairs={{0,18},{1,19},{2,16},{3,17},{4,22},{5,23},{6,20},{7,21},{8,26},{9,... | collective-permute-start | bytes 245768 | tf_op jit(solution)/shard_map/ppermute | solution.py:515
  25.6 1.6 %collective-permute-start.12 = (f32[1,5,32,128]{3,2,1,0:T(8,128)S(1)}, f32[1,5,32,128]{3,2,1,0:T(8,128)S(1)}, u32[]{:S(2)}, u32[]{:S(2)}) collective-permute-start(f32[1,5,32,128]{3,2,1,0:T(8,128)S(1)} %add_add_fusion), channel_id=1, source_target_pairs={{0,16},{1,17},{2,18},{3,19},{4,20},{5,21},{6,22},{7,23},{8,24},{9,... | collective-permute-start | bytes 245768 | tf_op jit(solution)/shard_map/ppermute | solution.py:515
  27.3 1.3 %collective-permute-start.11 = (f32[1,5,32,128]{3,2,1,0:T(8,128)S(1)}, f32[1,5,32,128]{3,2,1,0:T(8,128)S(1)}, u32[]{:S(2)}, u32[]{:S(2)}) collective-permute-start(f32[1,5,32,128]{3,2,1,0:T(8,128)S(1)} %add_add_fusion), channel_id=1, source_target_pairs={{0,2},{1,3},{2,0},{3,1},{4,6},{5,7},{6,4},{7,5},{8,10},{9,11},{10,... | collective-permute-start | bytes 245768 | tf_op jit(solution)/shard_map/ppermute | solution.py:515
  28.5 2.8 %collective-permute-start.2 = (f32[8,4,8,384]{3,2,1,0:T(8,128)S(1)}, f32[8,4,8,384]{3,2,1,0:T(8,128)S(1)}, u32[]{:S(2)}, u32[]{:S(2)}) collective-permute-start(f32[8,4,8,384]{3,2,1,0:T(8,128)S(1)} %get-tuple-element.20), channel_id=1, source_target_pairs={{1,2},{2,1},{5,6},{6,5},{9,10},{10,9},{13,14},{14,13},{17,18},{18,... | collective-permute-start | bytes 1179656 | tf_op jit(solution)/shard_map/ppermute | solution.py:522
  31.3 0.7 %collective-permute-start.1 = (f32[8,4,8,384]{3,2,1,0:T(8,128)S(1)}, f32[8,4,8,384]{3,2,1,0:T(8,128)S(1)}, u32[]{:S(2)}, u32[]{:S(2)}) collective-permute-start(f32[8,4,8,384]{3,2,1,0:T(8,128)S(1)} %get-tuple-element.20), channel_id=1, source_target_pairs={{3,4},{4,3},{7,8},{8,7},{11,12},{12,11},{19,20},{20,19},{23,24},{2... | collective-permute-start | bytes 1179656 | tf_op jit(solution)/shard_map/ppermute | solution.py:522
  32.1 1.5 %collective-permute-start.14 = (f32[4,5,32,128]{3,2,1,0:T(8,128)S(1)}, f32[4,5,32,128]{3,2,1,0:T(8,128)S(1)}, u32[]{:S(2)}, u32[]{:S(2)}) collective-permute-start(f32[4,5,32,128]{3,2,1,0:T(8,128)S(1)} %pad_maximum_fusion.refs_2_), channel_id=1, source_target_pairs={{0,1},{1,0},{2,3},{3,2},{4,5},{5,4},{6,7},{7,6},{8,9},{9,8},{10,11... | collective-permute-start | bytes 983048 | tf_op jit(solution)/shard_map/ppermute | solution.py:515
  33.6 1.4 %shard_map.83 = (f32[6,8,4,96,128]{4,3,2,1,0:T(8,128)S(1)}, bf16[2,256,384]{2,1,0:T(8,128)(2,1)S(1)}, bf16[128,64]{1,0:T(8,128)(2,1)S(1)}, f32[80,256]{1,0:T(8,128)S(1)}) custom-call(s32[1]{0:T(128)} %bitcast.info, f32[6,8,4,96,128]{4,3,2,1,0:T(8,128)S(1)} %get-tuple-element.16.refs_0_, ...), custom_call_target="tpu_custom_call", output_to_operand_aliasing={{0}: (1, {})} | custom-call | flops 1000000 | bytes 5000000 | tf_op jit(solution)/shard_map/pallas_call | solution.py:546
  35.0 6.8 %collective-permute-done.2.refs_4_ = f32[8,4,8,384]{3,2,1,0:T(8,128)S(1)} collective-permute-done((f32[8,4,8,384]{3,2,1,0:T(8,128)S(1)}, f32[8,4,8,384]{3,2,1,0:T(8,128)S(1)}, u32[]{:S(2)}, u32[]{:S(2)}) %collective-permute-start.2) | collective-permute-done | bytes 393248 | tf_op jit(solution)/shard_map/ppermute | solution.py:522
  42.3 0.9 %collective-permute-start.3 = (f32[80,256]{1,0:T(8,128)S(1)}, f32[80,256]{1,0:T(8,128)S(1)}, u32[]{:S(2)}, u32[]{:S(2)}) collective-permute-start(f32[80,256]{1,0:T(8,128)S(1)} %get-tuple-element.22), channel_id=1, source_target_pairs={{0,16},{16,0},{1,17},{17,1},{2,18},{18,2},{3,19},{19,3},{4,20},{20... | collective-permute-start | bytes 245768 | tf_op jit(solution)/shard_map/ppermute | solution.py:522
  43.2 3.6 %collective-permute-done.3.refs_1_ = f32[80,256]{1,0:T(8,128)S(1)} collective-permute-done((f32[80,256]{1,0:T(8,128)S(1)}, f32[80,256]{1,0:T(8,128)S(1)}, u32[]{:S(2)}, u32[]{:S(2)}) %collective-permute-start.3) | collective-permute-done | bytes 81952 | tf_op jit(solution)/shard_map/ppermute | solution.py:522
  46.8 2.6 %shard_map.85.refs_0_ = f32[6,8,4,96,128]{4,3,2,1,0:T(8,128)S(1)} custom-call(s32[1]{0:T(128)} %bitcast.info, f32[6,8,4,96,128]{4,3,2,1,0:T(8,128)S(1)} %get-tuple-element.21.refs_0_, f32[80,256]{1,0:T(8,128)S(1)} %collective-permute-done.3.refs_1_), custom_call_target="tpu_custom_call", output_to_operand_aliasing={{}: (1, {})} | custom-call | flops 10000000 | bytes 8000000 | tf_op jit(solution)/shard_map/pallas_call | solution.py:546
  49.4 1.8 %shard_map.86.refs_0_ = f32[6,8,4,96,128]{4,3,2,1,0:T(8,128)S(1)} custom-call(s32[1]{0:T(128)} %bitcast.info, f32[6,8,4,96,128]{4,3,2,1,0:T(8,128)S(1)} %shard_map.85.refs_0_), custom_call_target="tpu_custom_call", output_to_operand_aliasing={{}: (1, {})} | custom-call | flops 10000000 | bytes 8000000 | tf_op jit(solution)/shard_map/pallas_call | solution.py:546
  51.3 1.2 %shard_map.87.refs_1_ = f32[6,8,4,96,128]{4,3,2,1,0:T(8,128)S(1)} custom-call(s32[1]{0:T(128)} %bitcast.info, f32[6,8,4,96,128]{4,3,2,1,0:T(8,128)S(1)} %shard_map.86.refs_0_), custom_call_target="tpu_custom_call", output_to_operand_aliasing={{}: (1, {})} | custom-call | flops 10000000 | bytes 8000000 | tf_op jit(solution)/shard_map/pallas_call | solution.py:546
  52.4 4.0 %shard_map.88 = f32[5,8,64,384]{3,2,1,0:T(8,128)} custom-call(s32[1]{0:T(128)} %bitcast.info, f32[5,8]{1,0:T(8,128)S(1)} %copy-done.2, f32[6,8,4,96,128]{4,3,2,1,0:T(8,128)S(1)} %shard_map.87.refs_1_, f32[4,5,32,128]{3,2,1,0:T(8,128)S(1)} %pad_maximum_fusion.refs_2_, f32[4,5,32,128]{3,2,1,0:T(8,128)S(1)} %collective-permute-done.14.refs_3_, ...), custom_call_target="tpu_custom_call" | custom-call | flops 600000000 | bytes 8500000 | tf_op jit(solution)/shard_map/pallas_call | solution.py:546
  (24 shorter events, 1.3 us)
Async XLA Ops:
  0.0 33.6 %copy-start = (bf16[16,128,64]{2,1,0:T(8,128)(2,1)S(1)}, bf16[16,128,64]{2,1,0:T(8,128)(2,1)}, u32[]{:S(2)}) copy-start(bf16[16,128,64]{2,1,0:T(8,128)(2,1)} %constant.22.clone.refs_2_) | copy-start | bytes 786436
  0.0 33.6 %copy-start.1 = (bf16[2,2,64,384]{3,2,1,0:T(8,128)(2,1)S(1)}, bf16[2,2,64,384]{3,2,1,0:T(8,128)(2,1)}, u32[]{:S(2)}) copy-start(bf16[2,2,64,384]{3,2,1,0:T(8,128)(2,1)} %constant.21.clone.refs_1_) | copy-start | bytes 589828
  4.5 1.7 %collective-permute-start.4 = (f32[4,5,32,128]{3,2,1,0:T(8,128)S(1)}, f32[4,5,32,128]{3,2,1,0:T(8,128)S(1)}, u32[]{:S(2)}, u32[]{:S(2)}) collective-permute-start(f32[4,5,32,128]{3,2,1,0:T(8,128)S(1)} %get-tuple-element.24), channel_id=1, source_target_pairs={{0,1},{1,0},{2,3},{3,2},{4,5},{5,4},{6,7},{7,6},{8,9},{9,8},{10,11... | collective-permute-start | bytes 983048 | tf_op jit(solution)/shard_map/ppermute | solution.py:515
  6.3 5.1 %collective-permute-start.5 = (f32[1,5,32,128]{3,2,1,0:T(8,128)S(1)}, f32[1,5,32,128]{3,2,1,0:T(8,128)S(1)}, u32[]{:S(2)}, u32[]{:S(2)}) collective-permute-start(f32[1,5,32,128]{3,2,1,0:T(8,128)S(1)} %get-tuple-element.27), channel_id=1, source_target_pairs={{0,2},{1,3},{2,0},{3,1},{4,6},{5,7},{6,4},{7,5},{8,10},{9,11},{10,... | collective-permute-start | bytes 245768 | tf_op jit(solution)/shard_map/ppermute | solution.py:515
  6.4 7.3 %collective-permute-start.7 = (f32[1,5,32,128]{3,2,1,0:T(8,128)S(1)}, f32[1,5,32,128]{3,2,1,0:T(8,128)S(1)}, u32[]{:S(2)}, u32[]{:S(2)}) collective-permute-start(f32[1,5,32,128]{3,2,1,0:T(8,128)S(1)} %get-tuple-element.28), channel_id=1, source_target_pairs={{0,18},{1,19},{2,16},{3,17},{4,22},{5,23},{6,20},{7,21},{8,26},{9,... | collective-permute-start | bytes 245768 | tf_op jit(solution)/shard_map/ppermute | solution.py:515
  9.4 5.4 %collective-permute-start.6 = (f32[1,5,32,128]{3,2,1,0:T(8,128)S(1)}, f32[1,5,32,128]{3,2,1,0:T(8,128)S(1)}, u32[]{:S(2)}, u32[]{:S(2)}) collective-permute-start(f32[1,5,32,128]{3,2,1,0:T(8,128)S(1)} %get-tuple-element.29), channel_id=1, source_target_pairs={{0,16},{1,17},{2,18},{3,19},{4,20},{5,21},{6,22},{7,23},{8,24},{9,... | collective-permute-start | bytes 245768 | tf_op jit(solution)/shard_map/ppermute | solution.py:515
  14.8 7.2 %collective-permute-start.10 = (f32[1,5,32,128]{3,2,1,0:T(8,128)S(1)}, f32[1,5,32,128]{3,2,1,0:T(8,128)S(1)}, u32[]{:S(2)}, u32[]{:S(2)}) collective-permute-start(f32[1,5,32,128]{3,2,1,0:T(8,128)S(1)} %fusion.1), channel_id=1, source_target_pairs={{0,12},{1,13},{2,14},{3,15},{4,8},{5,9},{6,10},{7,11},{8,4},{9,5},... | collective-permute-start | bytes 245768 | tf_op jit(solution)/shard_map/ppermute | solution.py:515
  18.5 6.5 %collective-permute-start.9 = (f32[1,5,32,128]{3,2,1,0:T(8,128)S(1)}, f32[1,5,32,128]{3,2,1,0:T(8,128)S(1)}, u32[]{:S(2)}, u32[]{:S(2)}) collective-permute-start(f32[1,5,32,128]{3,2,1,0:T(8,128)S(1)} %fusion.1), channel_id=1, source_target_pairs={{0,8},{1,9},{2,10},{3,11},{4,12},{5,13},{6,14},{7,15},{8,0},{9,1},... | collective-permute-start | bytes 245768 | tf_op jit(solution)/shard_map/ppermute | solution.py:515
  18.5 6.5 %collective-permute-start.8 = (f32[1,5,32,128]{3,2,1,0:T(8,128)S(1)}, f32[1,5,32,128]{3,2,1,0:T(8,128)S(1)}, u32[]{:S(2)}, u32[]{:S(2)}) collective-permute-start(f32[1,5,32,128]{3,2,1,0:T(8,128)S(1)} %fusion.1), channel_id=1, source_target_pairs={{0,4},{1,5},{2,6},{3,7},{4,0},{5,1},{6,2},{7,3},{8,12},{9,13},{10,... | collective-permute-start | bytes 245768 | tf_op jit(solution)/shard_map/ppermute | solution.py:515
  25.0 6.3 %collective-permute-start.13 = (f32[1,5,32,128]{3,2,1,0:T(8,128)S(1)}, f32[1,5,32,128]{3,2,1,0:T(8,128)S(1)}, u32[]{:S(2)}, u32[]{:S(2)}) collective-permute-start(f32[1,5,32,128]{3,2,1,0:T(8,128)S(1)} %add_add_fusion), channel_id=1, source_target_pairs={{0,18},{1,19},{2,16},{3,17},{4,22},{5,23},{6,20},{7,21},{8,26},{9,... | collective-permute-start | bytes 245768 | tf_op jit(solution)/shard_map/ppermute | solution.py:515
  25.6 6.4 %collective-permute-start.12 = (f32[1,5,32,128]{3,2,1,0:T(8,128)S(1)}, f32[1,5,32,128]{3,2,1,0:T(8,128)S(1)}, u32[]{:S(2)}, u32[]{:S(2)}) collective-permute-start(f32[1,5,32,128]{3,2,1,0:T(8,128)S(1)} %add_add_fusion), channel_id=1, source_target_pairs={{0,16},{1,17},{2,18},{3,19},{4,20},{5,21},{6,22},{7,23},{8,24},{9,... | collective-permute-start | bytes 245768 | tf_op jit(solution)/shard_map/ppermute | solution.py:515
  27.3 4.8 %collective-permute-start.11 = (f32[1,5,32,128]{3,2,1,0:T(8,128)S(1)}, f32[1,5,32,128]{3,2,1,0:T(8,128)S(1)}, u32[]{:S(2)}, u32[]{:S(2)}) collective-permute-start(f32[1,5,32,128]{3,2,1,0:T(8,128)S(1)} %add_add_fusion), channel_id=1, source_target_pairs={{0,2},{1,3},{2,0},{3,1},{4,6},{5,7},{6,4},{7,5},{8,10},{9,11},{10,... | collective-permute-start | bytes 245768 | tf_op jit(solution)/shard_map/ppermute | solution.py:515
  28.5 6.5 %collective-permute-start = (f32[8,4,8,384]{3,2,1,0:T(8,128)S(1)}, f32[8,4,8,384]{3,2,1,0:T(8,128)S(1)}, u32[]{:S(2)}, u32[]{:S(2)}) collective-permute-start(f32[8,4,8,384]{3,2,1,0:T(8,128)S(1)} %get-tuple-element.19), channel_id=1, source_target_pairs={{0,1},{1,0},{2,3},{3,2},{4,5},{5,4},{6,7},{7,6},{8,9},{9,8},{10,11... | collective-permute-start | bytes 1179656 | tf_op jit(solution)/shard_map/ppermute | solution.py:522
  28.5 13.3 %collective-permute-start.2 = (f32[8,4,8,384]{3,2,1,0:T(8,128)S(1)}, f32[8,4,8,384]{3,2,1,0:T(8,128)S(1)}, u32[]{:S(2)}, u32[]{:S(2)}) collective-permute-start(f32[8,4,8,384]{3,2,1,0:T(8,128)S(1)} %get-tuple-element.20), channel_id=1, source_target_pairs={{1,2},{2,1},{5,6},{6,5},{9,10},{10,9},{13,14},{14,13},{17,18},{18,... | collective-permute-start | bytes 1179656 | tf_op jit(solution)/shard_map/ppermute | solution.py:522
  31.3 10.5 %collective-permute-start.1 = (f32[8,4,8,384]{3,2,1,0:T(8,128)S(1)}, f32[8,4,8,384]{3,2,1,0:T(8,128)S(1)}, u32[]{:S(2)}, u32[]{:S(2)}) collective-permute-start(f32[8,4,8,384]{3,2,1,0:T(8,128)S(1)} %get-tuple-element.20), channel_id=1, source_target_pairs={{3,4},{4,3},{7,8},{8,7},{11,12},{12,11},{19,20},{20,19},{23,24},{2... | collective-permute-start | bytes 1179656 | tf_op jit(solution)/shard_map/ppermute | solution.py:522
  32.1 20.4 %collective-permute-start.14 = (f32[4,5,32,128]{3,2,1,0:T(8,128)S(1)}, f32[4,5,32,128]{3,2,1,0:T(8,128)S(1)}, u32[]{:S(2)}, u32[]{:S(2)}) collective-permute-start(f32[4,5,32,128]{3,2,1,0:T(8,128)S(1)} %pad_maximum_fusion.refs_2_), channel_id=1, source_target_pairs={{0,1},{1,0},{2,3},{3,2},{4,5},{5,4},{6,7},{7,6},{8,9},{9,8},{10,11... | collective-permute-start | bytes 983048 | tf_op jit(solution)/shard_map/ppermute | solution.py:515
  42.3 4.5 %collective-permute-start.3 = (f32[80,256]{1,0:T(8,128)S(1)}, f32[80,256]{1,0:T(8,128)S(1)}, u32[]{:S(2)}, u32[]{:S(2)}) collective-permute-start(f32[80,256]{1,0:T(8,128)S(1)} %get-tuple-element.22), channel_id=1, source_target_pairs={{0,16},{16,0},{1,17},{17,1},{2,18},{18,2},{3,19},{19,3},{4,20},{20... | collective-permute-start | bytes 245768 | tf_op jit(solution)/shard_map/ppermute | solution.py:522
  51.2 1.2 %copy-start.2 = (f32[5,8]{1,0:T(8,128)S(1)}, f32[5,8]{1,0:T(8,128)}, u32[]{:S(2)}) copy-start(f32[5,8]{1,0:T(8,128)} %refs_0_.3) | copy-start | bytes 484

commit v4 on v3

--- a/solution.py
+++ b/solution.py
@@ -210,11 +210,10 @@
             for side in range(2):
                 back_ref[field, side, here, LANES:] = high
 
-    back(0)
+    for field in range(fields):
+        back(field)
     stores = []
     for field in range(fields):
-        if field + 1 < fields:
-            back(field + 1)
         for level in range(levels):
             if level % half == 0:
                 side = level // half
@@ -302,20 +301,20 @@
         copy.wait()
 
 
-def band_kernel(facts, *refs, x_phases, slabs, rows, cols):
-    a_ref, b_refs = refs[1 + x_phases], refs[2 + x_phases : 2 + x_phases + slabs]
-    ext_ref, *bands = refs[2 + x_phases + slabs :]
+def band_kernel(facts, *refs, x_phases, rows, cols):
+    slabs = refs[1 + x_phases : 3 + x_phases]
+    ext_ref, *bands = refs[3 + x_phases :]
     levels = ext_ref.shape[1]
     tiles = cols // LANES
 
     def place_slabs(odd):
-        for phase, sources in enumerate(((a_ref,), b_refs)):
+        for phase, slab in enumerate(slabs):
             base = GUARD if (odd == 1) == (phase == 0) else GUARD + SUB + rows
             for item, place, turn in ((3, 0, 0), (1, 1, 0), (0, 2, 0), (2, 2, 4), (4, 3, 0), (5, 3, 4)):
                 for level in range(levels):
                     for tile in range(tiles):
                         lanes = slice(tile * LANES, (tile + 1) * LANES)
-                        value = functools.reduce(jnp.add, [ref[level, place, :, lanes] for ref in sources])
+                        value = slab[level, place, :, lanes]
                         if turn:
                             value = pltpu.roll(value, turn, 0)
                         ext_ref[item, level, tile, pl.ds(base, SUB)] = value
@@ -514,11 +513,10 @@
     def swap(value, mask):
         return lax.ppermute(value, ("gx", "gy"), [(i, i ^ mask) for i in range(devices)])
 
-    def neighbours(value, axis, count, phase, far=None):
+    def neighbours(value, axis, count, phase):
         pairs = []
         for low in range(phase, count - 1, 2):
-            if far is None or ((low + 1) % 4 == 0) == far:
-                pairs += [(low, low + 1), (low + 1, low)]
+            pairs += [(low, low + 1), (low + 1, low)]
         return lax.ppermute(value, axis, pairs)
 
     def on_device(state, driving, rate, sound_square):
@@ -584,11 +582,7 @@
             9_000_000,
         )
         slab_a = neighbours(slab_a, "gy", ny, 0)
-        slabs_b = [
-            neighbours(slab_b, "gy", ny, 1, far)
-            for far in (True, False)
-            if any(((low + 1) % 4 == 0) == far for low in range(1, ny - 1, 2))
-        ]
+        slab_b = neighbours(slab_b, "gy", ny, 1)
 
         ext, wide, back, *bands = call(
             informed(prepare_kernel, rows=rows, cols=cols),
@@ -603,12 +597,12 @@
             aliases={1: 0},
         )
         ext, *bands = call(
-            informed(band_kernel, x_phases=x_phases, slabs=len(slabs_b), rows=rows, cols=cols),
+            informed(band_kernel, x_phases=x_phases, rows=rows, cols=cols),
             "band",
             [array(ext_shape)] + [array(band_shape)] * x_phases,
-            [vmem] * (2 + x_phases + len(slabs_b)),
+            [vmem] * (3 + x_phases),
             [],
-            (info, ext, *bands, slab_a, *slabs_b),
+            (info, ext, *bands, slab_a, slab_b),
             1_000_000,
             5_000_000,
             aliases={1 + index: index for index in range(1 + x_phases)},

time: 56.8 us -> 56.1 us (0.988)
  starting transfers between devices: 17.5 us -> 15.3 us
  waiting for transfers between devices: 22.7 us -> 24.8 us
  Pallas kernels: 15.9 us -> 15.3 us
    ppermute x4 -> x3, waiting for transfers between devices: 10.5 us -> 12.2 us  [neighbours(): return lax.ppermute(value, axis, pairs)]
    ppermute x11, starting transfers between devices: 13.2 us -> 11.7 us  [swap(): lax.ppermute(value, ('gx', 'gy'), [(i, i ^ mask) for i in range(devices)])]
    ppermute x4 -> x3, starting transfers between devices: 4.32 us -> 3.64 us  [neighbours(): return lax.ppermute(value, axis, pairs)]
    pallas_call x7, Pallas kernels: 15.9 us -> 15.3 us  [call(): pl.pallas_call(kernel, grid_spec=pltpu.PrefetchScalarGridSpec(num_scalar_...]
  transfers between devices with their start and end apart: 15 -> 14, of which waited for: 8 -> 9; matrix products, arithmetic and copies ran while one was open for 0% -> 0% of each run, Pallas kernels for 13% -> 13%
where the time goes in v4:
time: 56.1 us; the launch traced here: 56 us
  waiting for transfers between devices  24.8 us (44%)
  Pallas kernels  15.3 us (27%)
  starting transfers between devices  15.3 us (27%)
    pallas_call x7, Pallas kernels, call(): pl.pallas_call(kernel, grid_spec=pltpu.PrefetchScalarGridSpec(num_scalar_...  15.3 us
    ppermute x11, waiting for transfers between devices, swap(): lax.ppermute(value, ('gx', 'gy'), [(i, i ^ mask) for i in range(devices)])  12.6 us
    ppermute x3, waiting for transfers between devices, neighbours(): return lax.ppermute(value, axis, pairs)  12.2 us
    ppermute x11, starting transfers between devices, swap(): lax.ppermute(value, ('gx', 'gy'), [(i, i ^ mask) for i in range(devices)])  11.7 us
    ppermute x3, starting transfers between devices, neighbours(): return lax.ppermute(value, axis, pairs)  3.64 us
  transfers between devices with their start and end apart: 14, of which 9 were waited for; matrix products, arithmetic and copies ran while one was open for 0% of the time, Pallas kernels for 13%

profile of v4, /device:TPU:2, one launch (start us, length us, event | category | flops | bytes accessed | tf_op | source)
XLA Modules:
  0.0 56.0 jit_solution(5770944028883817881)
XLA Ops:
  0.0 4.5 %shard_map.82 = (f32[6,8,4,96,128]{4,3,2,1,0:T(8,128)S(1)}, f32[8,4,8,384]{3,2,1,0:T(8,128)S(1)}, f32[8,4,8,384]{3,2,1,0:T(8,128)S(1)}, f32[4,5,32,128]{3,2,1,0:T(8,128)S(1)}, f32[4,5,32,128]{3,2,1,0:T(8,128)S(1)}) custom-call(s32[1]{0:T(128)} %bitcast.info, f32[5,8,64,384]{3,2,1,0:T(8,128)} %refs_0_.2, f32[5,8,64,384]{3,2,1,0:T(8,128)} %refs_1_.2, ...), custom_call_target="tpu_custom_call" | custom-call | flops 600000000 | bytes 9000000 | tf_op jit(solution)/shard_map/pallas_call | solution.py:544
  4.6 1.6 %collective-permute-done.3 = f32[4,5,32,128]{3,2,1,0:T(8,128)S(1)} collective-permute-done((f32[4,5,32,128]{3,2,1,0:T(8,128)S(1)}, f32[4,5,32,128]{3,2,1,0:T(8,128)S(1)}, u32[]{:S(2)}, u32[]{:S(2)}) %collective-permute-start.3) | collective-permute-done | bytes 327712 | tf_op jit(solution)/shard_map/ppermute | solution.py:514
  6.4 3.0 %collective-permute-start.6 = (f32[1,5,32,128]{3,2,1,0:T(8,128)S(1)}, f32[1,5,32,128]{3,2,1,0:T(8,128)S(1)}, u32[]{:S(2)}, u32[]{:S(2)}) collective-permute-start(f32[1,5,32,128]{3,2,1,0:T(8,128)S(1)} %get-tuple-element.28), channel_id=1, source_target_pairs={{0,18},{1,19},{2,16},{3,17},{4,22},{5,23},{6,20},{7,21},{8,26},{9,... | collective-permute-start | bytes 245768 | tf_op jit(solution)/shard_map/ppermute | solution.py:514
  9.4 0.5 collective-permute-start.5
  9.9 1.5 %collective-permute-done.4 = f32[1,5,32,128]{3,2,1,0:T(8,128)S(1)} collective-permute-done((f32[1,5,32,128]{3,2,1,0:T(8,128)S(1)}, f32[1,5,32,128]{3,2,1,0:T(8,128)S(1)}, u32[]{:S(2)}, u32[]{:S(2)}) %collective-permute-start.4) | collective-permute-done | bytes 81952 | tf_op jit(solution)/shard_map/ppermute | solution.py:514
  11.4 2.3 %collective-permute-done.6 = f32[1,5,32,128]{3,2,1,0:T(8,128)S(1)} collective-permute-done((f32[1,5,32,128]{3,2,1,0:T(8,128)S(1)}, f32[1,5,32,128]{3,2,1,0:T(8,128)S(1)}, u32[]{:S(2)}, u32[]{:S(2)}) %collective-permute-start.6) | collective-permute-done | bytes 81952 | tf_op jit(solution)/shard_map/ppermute | solution.py:514
  13.7 1.1 %collective-permute-done.5 = f32[1,5,32,128]{3,2,1,0:T(8,128)S(1)} collective-permute-done((f32[1,5,32,128]{3,2,1,0:T(8,128)S(1)}, f32[1,5,32,128]{3,2,1,0:T(8,128)S(1)}, u32[]{:S(2)}, u32[]{:S(2)}) %collective-permute-start.5) | collective-permute-done | bytes 81952 | tf_op jit(solution)/shard_map/ppermute | solution.py:514
  14.8 3.7 %collective-permute-start.9 = (f32[1,5,32,128]{3,2,1,0:T(8,128)S(1)}, f32[1,5,32,128]{3,2,1,0:T(8,128)S(1)}, u32[]{:S(2)}, u32[]{:S(2)}) collective-permute-start(f32[1,5,32,128]{3,2,1,0:T(8,128)S(1)} %fusion.1), channel_id=1, source_target_pairs={{0,12},{1,13},{2,14},{3,15},{4,8},{5,9},{6,10},{7,11},{8,4},{9,5},... | collective-permute-start | bytes 245768 | tf_op jit(solution)/shard_map/ppermute | solution.py:514
  18.5 0.8 %collective-permute-start.7 = (f32[1,5,32,128]{3,2,1,0:T(8,128)S(1)}, f32[1,5,32,128]{3,2,1,0:T(8,128)S(1)}, u32[]{:S(2)}, u32[]{:S(2)}) collective-permute-start(f32[1,5,32,128]{3,2,1,0:T(8,128)S(1)} %fusion.1), channel_id=1, source_target_pairs={{0,4},{1,5},{2,6},{3,7},{4,0},{5,1},{6,2},{7,3},{8,12},{9,13},{10,... | collective-permute-start | bytes 245768 | tf_op jit(solution)/shard_map/ppermute | solution.py:514
  19.2 2.7 %collective-permute-done.9 = f32[1,5,32,128]{3,2,1,0:T(8,128)S(1)} collective-permute-done((f32[1,5,32,128]{3,2,1,0:T(8,128)S(1)}, f32[1,5,32,128]{3,2,1,0:T(8,128)S(1)}, u32[]{:S(2)}, u32[]{:S(2)}) %collective-permute-start.9) | collective-permute-done | bytes 81952 | tf_op jit(solution)/shard_map/ppermute | solution.py:514
  22.0 3.0 %collective-permute-done.8 = f32[1,5,32,128]{3,2,1,0:T(8,128)S(1)} collective-permute-done((f32[1,5,32,128]{3,2,1,0:T(8,128)S(1)}, f32[1,5,32,128]{3,2,1,0:T(8,128)S(1)}, u32[]{:S(2)}, u32[]{:S(2)}) %collective-permute-start.8) | collective-permute-done | bytes 81952 | tf_op jit(solution)/shard_map/ppermute | solution.py:514
  25.0 0.7 %collective-permute-start.12 = (f32[1,5,32,128]{3,2,1,0:T(8,128)S(1)}, f32[1,5,32,128]{3,2,1,0:T(8,128)S(1)}, u32[]{:S(2)}, u32[]{:S(2)}) collective-permute-start(f32[1,5,32,128]{3,2,1,0:T(8,128)S(1)} %add_add_fusion), channel_id=1, source_target_pairs={{0,18},{1,19},{2,16},{3,17},{4,22},{5,23},{6,20},{7,21},{8,26},{9,... | collective-permute-start | bytes 245768 | tf_op jit(solution)/shard_map/ppermute | solution.py:514
  25.6 1.6 %collective-permute-start.11 = (f32[1,5,32,128]{3,2,1,0:T(8,128)S(1)}, f32[1,5,32,128]{3,2,1,0:T(8,128)S(1)}, u32[]{:S(2)}, u32[]{:S(2)}) collective-permute-start(f32[1,5,32,128]{3,2,1,0:T(8,128)S(1)} %add_add_fusion), channel_id=1, source_target_pairs={{0,16},{1,17},{2,18},{3,19},{4,20},{5,21},{6,22},{7,23},{8,24},{9,... | collective-permute-start | bytes 245768 | tf_op jit(solution)/shard_map/ppermute | solution.py:514
  27.3 1.3 %collective-permute-start.10 = (f32[1,5,32,128]{3,2,1,0:T(8,128)S(1)}, f32[1,5,32,128]{3,2,1,0:T(8,128)S(1)}, u32[]{:S(2)}, u32[]{:S(2)}) collective-permute-start(f32[1,5,32,128]{3,2,1,0:T(8,128)S(1)} %add_add_fusion), channel_id=1, source_target_pairs={{0,2},{1,3},{2,0},{3,1},{4,6},{5,7},{6,4},{7,5},{8,10},{9,11},{10,... | collective-permute-start | bytes 245768 | tf_op jit(solution)/shard_map/ppermute | solution.py:514
  28.5 2.8 %collective-permute-start.1 = (f32[8,4,8,384]{3,2,1,0:T(8,128)S(1)}, f32[8,4,8,384]{3,2,1,0:T(8,128)S(1)}, u32[]{:S(2)}, u32[]{:S(2)}) collective-permute-start(f32[8,4,8,384]{3,2,1,0:T(8,128)S(1)} %get-tuple-element.20), channel_id=1, source_target_pairs={{1,2},{2,1},{3,4},{4,3},{5,6},{6,5},{7,8},{8,7},{9,10},{10,9},{11,... | collective-permute-start | bytes 1179656 | tf_op jit(solution)/shard_map/ppermute | solution.py:520
  31.8 1.4 %shard_map.83 = (f32[6,8,4,96,128]{4,3,2,1,0:T(8,128)S(1)}, bf16[2,256,384]{2,1,0:T(8,128)(2,1)S(1)}, bf16[128,64]{1,0:T(8,128)(2,1)S(1)}, f32[80,256]{1,0:T(8,128)S(1)}) custom-call(s32[1]{0:T(128)} %bitcast.info, f32[6,8,4,96,128]{4,3,2,1,0:T(8,128)S(1)} %get-tuple-element.16.refs_0_, ...), custom_call_target="tpu_custom_call", output_to_operand_aliasing={{0}: (1, {})} | custom-call | flops 1000000 | bytes 5000000 | tf_op jit(solution)/shard_map/pallas_call | solution.py:544
  33.2 8.6 %collective-permute-done.1.refs_3_ = f32[8,4,8,384]{3,2,1,0:T(8,128)S(1)} collective-permute-done((f32[8,4,8,384]{3,2,1,0:T(8,128)S(1)}, f32[8,4,8,384]{3,2,1,0:T(8,128)S(1)}, u32[]{:S(2)}, u32[]{:S(2)}) %collective-permute-start.1) | collective-permute-done | bytes 393248 | tf_op jit(solution)/shard_map/ppermute | solution.py:520
  41.8 0.5 shard_map.84
  42.3 0.9 %collective-permute-start.2 = (f32[80,256]{1,0:T(8,128)S(1)}, f32[80,256]{1,0:T(8,128)S(1)}, u32[]{:S(2)}, u32[]{:S(2)}) collective-permute-start(f32[80,256]{1,0:T(8,128)S(1)} %get-tuple-element.22), channel_id=1, source_target_pairs={{0,16},{16,0},{1,17},{17,1},{2,18},{18,2},{3,19},{19,3},{4,20},{20... | collective-permute-start | bytes 245768 | tf_op jit(solution)/shard_map/ppermute | solution.py:520
  43.2 3.6 %collective-permute-done.2.refs_1_ = f32[80,256]{1,0:T(8,128)S(1)} collective-permute-done((f32[80,256]{1,0:T(8,128)S(1)}, f32[80,256]{1,0:T(8,128)S(1)}, u32[]{:S(2)}, u32[]{:S(2)}) %collective-permute-start.2) | collective-permute-done | bytes 81952 | tf_op jit(solution)/shard_map/ppermute | solution.py:520
  46.8 2.6 %shard_map.85.refs_0_ = f32[6,8,4,96,128]{4,3,2,1,0:T(8,128)S(1)} custom-call(s32[1]{0:T(128)} %bitcast.info, f32[6,8,4,96,128]{4,3,2,1,0:T(8,128)S(1)} %get-tuple-element.21.refs_0_, f32[80,256]{1,0:T(8,128)S(1)} %collective-permute-done.2.refs_1_), custom_call_target="tpu_custom_call", output_to_operand_aliasing={{}: (1, {})} | custom-call | flops 10000000 | bytes 8000000 | tf_op jit(solution)/shard_map/pallas_call | solution.py:544
  49.4 1.8 %shard_map.86.refs_0_ = f32[6,8,4,96,128]{4,3,2,1,0:T(8,128)S(1)} custom-call(s32[1]{0:T(128)} %bitcast.info, f32[6,8,4,96,128]{4,3,2,1,0:T(8,128)S(1)} %shard_map.85.refs_0_), custom_call_target="tpu_custom_call", output_to_operand_aliasing={{}: (1, {})} | custom-call | flops 10000000 | bytes 8000000 | tf_op jit(solution)/shard_map/pallas_call | solution.py:544
  51.2 1.2 %shard_map.87.refs_1_ = f32[6,8,4,96,128]{4,3,2,1,0:T(8,128)S(1)} custom-call(s32[1]{0:T(128)} %bitcast.info, f32[6,8,4,96,128]{4,3,2,1,0:T(8,128)S(1)} %shard_map.86.refs_0_), custom_call_target="tpu_custom_call", output_to_operand_aliasing={{}: (1, {})} | custom-call | flops 10000000 | bytes 8000000 | tf_op jit(solution)/shard_map/pallas_call | solution.py:544
  52.4 3.4 %shard_map.88 = f32[5,8,64,384]{3,2,1,0:T(8,128)} custom-call(s32[1]{0:T(128)} %bitcast.info, f32[5,8]{1,0:T(8,128)S(1)} %copy-done.2, f32[6,8,4,96,128]{4,3,2,1,0:T(8,128)S(1)} %shard_map.87.refs_1_, f32[4,5,32,128]{3,2,1,0:T(8,128)S(1)} %pad_maximum_fusion.refs_2_, f32[4,5,32,128]{3,2,1,0:T(8,128)S(1)} %collective-permute-done.13.refs_3_, ...), custom_call_target="tpu_custom_call" | custom-call | flops 600000000 | bytes 8500000 | tf_op jit(solution)/shard_map/pallas_call | solution.py:544
  (22 shorter events, 0.8 us)
Async XLA Ops:
  0.0 31.8 %copy-start = (bf16[16,128,64]{2,1,0:T(8,128)(2,1)S(1)}, bf16[16,128,64]{2,1,0:T(8,128)(2,1)}, u32[]{:S(2)}) copy-start(bf16[16,128,64]{2,1,0:T(8,128)(2,1)} %constant.22.clone.refs_2_) | copy-start | bytes 786436
  0.0 31.8 %copy-start.1 = (bf16[2,2,64,384]{3,2,1,0:T(8,128)(2,1)S(1)}, bf16[2,2,64,384]{3,2,1,0:T(8,128)(2,1)}, u32[]{:S(2)}) copy-start(bf16[2,2,64,384]{3,2,1,0:T(8,128)(2,1)} %constant.21.clone.refs_1_) | copy-start | bytes 589828
  4.5 1.7 %collective-permute-start.3 = (f32[4,5,32,128]{3,2,1,0:T(8,128)S(1)}, f32[4,5,32,128]{3,2,1,0:T(8,128)S(1)}, u32[]{:S(2)}, u32[]{:S(2)}) collective-permute-start(f32[4,5,32,128]{3,2,1,0:T(8,128)S(1)} %get-tuple-element.24), channel_id=1, source_target_pairs={{0,1},{1,0},{2,3},{3,2},{4,5},{5,4},{6,7},{7,6},{8,9},{9,8},{10,11... | collective-permute-start | bytes 983048 | tf_op jit(solution)/shard_map/ppermute | solution.py:514
  6.3 5.1 %collective-permute-start.4 = (f32[1,5,32,128]{3,2,1,0:T(8,128)S(1)}, f32[1,5,32,128]{3,2,1,0:T(8,128)S(1)}, u32[]{:S(2)}, u32[]{:S(2)}) collective-permute-start(f32[1,5,32,128]{3,2,1,0:T(8,128)S(1)} %get-tuple-element.27), channel_id=1, source_target_pairs={{0,2},{1,3},{2,0},{3,1},{4,6},{5,7},{6,4},{7,5},{8,10},{9,11},{10,... | collective-permute-start | bytes 245768 | tf_op jit(solution)/shard_map/ppermute | solution.py:514
  6.4 7.3 %collective-permute-start.6 = (f32[1,5,32,128]{3,2,1,0:T(8,128)S(1)}, f32[1,5,32,128]{3,2,1,0:T(8,128)S(1)}, u32[]{:S(2)}, u32[]{:S(2)}) collective-permute-start(f32[1,5,32,128]{3,2,1,0:T(8,128)S(1)} %get-tuple-element.28), channel_id=1, source_target_pairs={{0,18},{1,19},{2,16},{3,17},{4,22},{5,23},{6,20},{7,21},{8,26},{9,... | collective-permute-start | bytes 245768 | tf_op jit(solution)/shard_map/ppermute | solution.py:514
  9.4 5.4 %collective-permute-start.5 = (f32[1,5,32,128]{3,2,1,0:T(8,128)S(1)}, f32[1,5,32,128]{3,2,1,0:T(8,128)S(1)}, u32[]{:S(2)}, u32[]{:S(2)}) collective-permute-start(f32[1,5,32,128]{3,2,1,0:T(8,128)S(1)} %get-tuple-element.29), channel_id=1, source_target_pairs={{0,16},{1,17},{2,18},{3,19},{4,20},{5,21},{6,22},{7,23},{8,24},{9,... | collective-permute-start | bytes 245768 | tf_op jit(solution)/shard_map/ppermute | solution.py:514
  14.8 7.2 %collective-permute-start.9 = (f32[1,5,32,128]{3,2,1,0:T(8,128)S(1)}, f32[1,5,32,128]{3,2,1,0:T(8,128)S(1)}, u32[]{:S(2)}, u32[]{:S(2)}) collective-permute-start(f32[1,5,32,128]{3,2,1,0:T(8,128)S(1)} %fusion.1), channel_id=1, source_target_pairs={{0,12},{1,13},{2,14},{3,15},{4,8},{5,9},{6,10},{7,11},{8,4},{9,5},... | collective-permute-start | bytes 245768 | tf_op jit(solution)/shard_map/ppermute | solution.py:514
  18.5 6.5 %collective-permute-start.8 = (f32[1,5,32,128]{3,2,1,0:T(8,128)S(1)}, f32[1,5,32,128]{3,2,1,0:T(8,128)S(1)}, u32[]{:S(2)}, u32[]{:S(2)}) collective-permute-start(f32[1,5,32,128]{3,2,1,0:T(8,128)S(1)} %fusion.1), channel_id=1, source_target_pairs={{0,8},{1,9},{2,10},{3,11},{4,12},{5,13},{6,14},{7,15},{8,0},{9,1},... | collective-permute-start | bytes 245768 | tf_op jit(solution)/shard_map/ppermute | solution.py:514
  18.5 6.5 %collective-permute-start.7 = (f32[1,5,32,128]{3,2,1,0:T(8,128)S(1)}, f32[1,5,32,128]{3,2,1,0:T(8,128)S(1)}, u32[]{:S(2)}, u32[]{:S(2)}) collective-permute-start(f32[1,5,32,128]{3,2,1,0:T(8,128)S(1)} %fusion.1), channel_id=1, source_target_pairs={{0,4},{1,5},{2,6},{3,7},{4,0},{5,1},{6,2},{7,3},{8,12},{9,13},{10,... | collective-permute-start | bytes 245768 | tf_op jit(solution)/shard_map/ppermute | solution.py:514
  25.0 6.3 %collective-permute-start.12 = (f32[1,5,32,128]{3,2,1,0:T(8,128)S(1)}, f32[1,5,32,128]{3,2,1,0:T(8,128)S(1)}, u32[]{:S(2)}, u32[]{:S(2)}) collective-permute-start(f32[1,5,32,128]{3,2,1,0:T(8,128)S(1)} %add_add_fusion), channel_id=1, source_target_pairs={{0,18},{1,19},{2,16},{3,17},{4,22},{5,23},{6,20},{7,21},{8,26},{9,... | collective-permute-start | bytes 245768 | tf_op jit(solution)/shard_map/ppermute | solution.py:514
  25.6 5.7 %collective-permute-start.11 = (f32[1,5,32,128]{3,2,1,0:T(8,128)S(1)}, f32[1,5,32,128]{3,2,1,0:T(8,128)S(1)}, u32[]{:S(2)}, u32[]{:S(2)}) collective-permute-start(f32[1,5,32,128]{3,2,1,0:T(8,128)S(1)} %add_add_fusion), channel_id=1, source_target_pairs={{0,16},{1,17},{2,18},{3,19},{4,20},{5,21},{6,22},{7,23},{8,24},{9,... | collective-permute-start | bytes 245768 | tf_op jit(solution)/shard_map/ppermute | solution.py:514
  27.3 4.4 %collective-permute-start.10 = (f32[1,5,32,128]{3,2,1,0:T(8,128)S(1)}, f32[1,5,32,128]{3,2,1,0:T(8,128)S(1)}, u32[]{:S(2)}, u32[]{:S(2)}) collective-permute-start(f32[1,5,32,128]{3,2,1,0:T(8,128)S(1)} %add_add_fusion), channel_id=1, source_target_pairs={{0,2},{1,3},{2,0},{3,1},{4,6},{5,7},{6,4},{7,5},{8,10},{9,11},{10,... | collective-permute-start | bytes 245768 | tf_op jit(solution)/shard_map/ppermute | solution.py:514
  28.5 4.7 %collective-permute-start = (f32[8,4,8,384]{3,2,1,0:T(8,128)S(1)}, f32[8,4,8,384]{3,2,1,0:T(8,128)S(1)}, u32[]{:S(2)}, u32[]{:S(2)}) collective-permute-start(f32[8,4,8,384]{3,2,1,0:T(8,128)S(1)} %get-tuple-element.19), channel_id=1, source_target_pairs={{0,1},{1,0},{2,3},{3,2},{4,5},{5,4},{6,7},{7,6},{8,9},{9,8},{10,11... | collective-permute-start | bytes 1179656 | tf_op jit(solution)/shard_map/ppermute | solution.py:520
  28.5 13.3 %collective-permute-start.1 = (f32[8,4,8,384]{3,2,1,0:T(8,128)S(1)}, f32[8,4,8,384]{3,2,1,0:T(8,128)S(1)}, u32[]{:S(2)}, u32[]{:S(2)}) collective-permute-start(f32[8,4,8,384]{3,2,1,0:T(8,128)S(1)} %get-tuple-element.20), channel_id=1, source_target_pairs={{1,2},{2,1},{3,4},{4,3},{5,6},{6,5},{7,8},{8,7},{9,10},{10,9},{11,... | collective-permute-start | bytes 1179656 | tf_op jit(solution)/shard_map/ppermute | solution.py:520
  31.7 20.7 %collective-permute-start.13 = (f32[4,5,32,128]{3,2,1,0:T(8,128)S(1)}, f32[4,5,32,128]{3,2,1,0:T(8,128)S(1)}, u32[]{:S(2)}, u32[]{:S(2)}) collective-permute-start(f32[4,5,32,128]{3,2,1,0:T(8,128)S(1)} %pad_maximum_fusion.refs_2_), channel_id=1, source_target_pairs={{0,1},{1,0},{2,3},{3,2},{4,5},{5,4},{6,7},{7,6},{8,9},{9,8},{10,11... | collective-permute-start | bytes 983048 | tf_op jit(solution)/shard_map/ppermute | solution.py:514
  42.3 4.5 %collective-permute-start.2 = (f32[80,256]{1,0:T(8,128)S(1)}, f32[80,256]{1,0:T(8,128)S(1)}, u32[]{:S(2)}, u32[]{:S(2)}) collective-permute-start(f32[80,256]{1,0:T(8,128)S(1)} %get-tuple-element.22), channel_id=1, source_target_pairs={{0,16},{16,0},{1,17},{17,1},{2,18},{18,2},{3,19},{19,3},{4,20},{20... | collective-permute-start | bytes 245768 | tf_op jit(solution)/shard_map/ppermute | solution.py:520
  51.2 1.2 %copy-start.2 = (f32[5,8]{1,0:T(8,128)S(1)}, f32[5,8]{1,0:T(8,128)}, u32[]{:S(2)}) copy-start(f32[5,8]{1,0:T(8,128)} %refs_0_.3) | copy-start | bytes 484

commit v5 on v4

--- a/solution.py
+++ b/solution.py
@@ -326,7 +326,7 @@
     shift_down(ext_ref, parts, tiles)
 
 
-def substep_kernel(facts, *refs, step, levels, rows, cols):
+def substep_kernel(facts, *refs, step, levels, rows, cols, early=None):
     bands, ext_ref = refs[1:-1], refs[-1]
     tiles = cols // LANES
     chunks = rows // SUB
@@ -355,7 +355,7 @@
                     old = ext_ref[0, level, tiles - 1, here]
                     ext_ref[0, level, tiles - 1, here] = jnp.where(lane == LANES - 1, edge, old)
 
-    if step == 0:
+    if step == 0 and not early:
         for odd in range(2):
             pl.when(facts[5] == odd)(functools.partial(unpack_bands, odd))
 
@@ -380,6 +380,12 @@
     def flush(pending):
         for ref, level, tile, here, value in pending:
             ref[level, tile, here] = value
+
+    def wanted(kind, chunk, tile):
+        if early is None:
+            return True
+        low, high, count = {"u": (1, chunks, tiles - 1), "v": (2, chunks - 1, tiles), "w": (1, chunks, tiles)}[kind]
+        return (low <= chunk <= high and tile < count) == early
 
     def winds(chunk, only_v=False):
         row = GUARD + chunk * SUB
@@ -391,6 +397,8 @@
         for level in range(levels):
             made = []
             for tile in range(x_tiles):
+                if not wanted("v", chunk, tile):
+                    continue
                 slope = p_ref[level, tile, pl.ds(row + 1, SUB)] - p_ref[level, tile, pl.ds(row - 1, SUB)]
                 if first:
                     slope = slope * (quarter if limit is None else quarter * limit)
@@ -400,22 +408,22 @@
             if only_v:
                 flush(made)
                 continue
-            old = [u_ref[level, tile, here] for tile in range(ring)]
-            fresh = []
             for tile in range(ring):
+                if not wanted("u", chunk, tile):
+                    continue
                 slope = ahead(line, tile, 2) - line[tile]
                 edge = {tiles - 1: inner, tiles: outer}.get(tile)
                 if first:
                     slope = slope * (quarter if edge is None else quarter * edge)
                 elif edge is not None:
                     slope = slope * edge
-                fresh.append(old[tile] - slope)
-            for tile in range(ring):
-                made.append((u_ref, level, tile, here, fresh[tile]))
+                made.append((u_ref, level, tile, here, u_ref[level, tile, here] - slope))
             after = None
             if level + 1 < levels:
                 after = [p_ref[level + 1, tile, here] for tile in range(ring)]
             for tile in range(x_tiles):
+                if not wanted("w", chunk, tile):
+                    continue
                 if level == 0:
                     lift = after[tile]
                 elif level == levels - 1:
@@ -465,11 +473,12 @@
     if last:
         winds(0, True)
         winds(chunks + 1, True)
-    span = range(1, chunks + 1) if last else range(chunks + 2)
+    span = range(1, chunks + 1) if last or early else range(chunks + 2)
     for chunk in span:
         winds(chunk)
-    for chunk in span:
-        scalars(chunk)
+    if not early:
+        for chunk in span:
+            scalars(chunk)
 
 
 def solution(mesh):
@@ -596,6 +605,17 @@
             5_000_000,
             aliases={1: 0},
         )
+        (ext,) = call(
+            informed(substep_kernel, step=0, levels=levels, rows=rows, cols=cols, early=True),
+            "early",
+            [array(ext_shape)],
+            [vmem],
+            [],
+            (info, ext),
+            10_000_000,
+            8_000_000,
+            aliases={1: 0},
+        )
         ext, *bands = call(
             informed(band_kernel, x_phases=x_phases, rows=rows, cols=cols),
             "band",
@@ -612,7 +632,9 @@
         for step in range(SUBSTEPS):
             extra = bands if step == 0 else []
             (ext,) = call(
-                informed(substep_kernel, step=step, levels=levels, rows=rows, cols=cols),
+                informed(
+                    substep_kernel, step=step, levels=levels, rows=rows, cols=cols, early=None if step else False
+                ),
                 f"substep_{step}",
                 [array(ext_shape)],
                 [vmem] * (1 + len(extra)),

time: 56.1 us -> 55.9 us (level)
    pallas_call x7 -> x8, Pallas kernels: 15.3 us -> 15.6 us  [call(): pl.pallas_call(kernel, grid_spec=pltpu.PrefetchScalarGridSpec(num_scalar_...]
  transfers between devices with their start and end apart: 14 -> 14, of which waited for: 9 -> 9; matrix products, arithmetic and copies ran while one was open for 0% -> 0% of each run, Pallas kernels for 13% -> 14%
where the time goes in v5:
time: 55.9 us; the launch traced here: 55.7 us
  waiting for transfers between devices  24.3 us (43%)
  Pallas kernels  15.6 us (28%)
  starting transfers between devices  15.3 us (27%)
    pallas_call x8, Pallas kernels, call(): pl.pallas_call(kernel, grid_spec=pltpu.PrefetchScalarGridSpec(num_scalar_...  15.6 us
    ppermute x11, waiting for transfers between devices, swap(): lax.ppermute(value, ('gx', 'gy'), [(i, i ^ mask) for i in range(devices)])  12.6 us
    ppermute x3, waiting for transfers between devices, neighbours(): return lax.ppermute(value, axis, pairs)  11.7 us
    ppermute x11, starting transfers between devices, swap(): lax.ppermute(value, ('gx', 'gy'), [(i, i ^ mask) for i in range(devices)])  11.7 us
    ppermute x3, starting transfers between devices, neighbours(): return lax.ppermute(value, axis, pairs)  3.64 us
  transfers between devices with their start and end apart: 14, of which 9 were waited for; matrix products, arithmetic and copies ran while one was open for 0% of the time, Pallas kernels for 14%

profile of v5, /device:TPU:2, one launch (start us, length us, event | category | flops | bytes accessed | tf_op | source)
XLA Modules:
  0.0 55.7 jit_solution(18269633475097711490)
XLA Ops:
  0.0 4.5 %shard_map.82 = (f32[6,8,4,96,128]{4,3,2,1,0:T(8,128)S(1)}, f32[8,4,8,384]{3,2,1,0:T(8,128)S(1)}, f32[8,4,8,384]{3,2,1,0:T(8,128)S(1)}, f32[4,5,32,128]{3,2,1,0:T(8,128)S(1)}, f32[4,5,32,128]{3,2,1,0:T(8,128)S(1)}) custom-call(s32[1]{0:T(128)} %bitcast.info, f32[5,8,64,384]{3,2,1,0:T(8,128)} %refs_0_.2, f32[5,8,64,384]{3,2,1,0:T(8,128)} %refs_1_.2, ...), custom_call_target="tpu_custom_call" | custom-call | flops 600000000 | bytes 9000000 | tf_op jit(solution)/shard_map/pallas_call | solution.py:553
  4.6 1.6 %collective-permute-done.3 = f32[4,5,32,128]{3,2,1,0:T(8,128)S(1)} collective-permute-done((f32[4,5,32,128]{3,2,1,0:T(8,128)S(1)}, f32[4,5,32,128]{3,2,1,0:T(8,128)S(1)}, u32[]{:S(2)}, u32[]{:S(2)}) %collective-permute-start.3) | collective-permute-done | bytes 327712 | tf_op jit(solution)/shard_map/ppermute | solution.py:523
  6.4 3.0 %collective-permute-start.6 = (f32[1,5,32,128]{3,2,1,0:T(8,128)S(1)}, f32[1,5,32,128]{3,2,1,0:T(8,128)S(1)}, u32[]{:S(2)}, u32[]{:S(2)}) collective-permute-start(f32[1,5,32,128]{3,2,1,0:T(8,128)S(1)} %get-tuple-element.28), channel_id=1, source_target_pairs={{0,18},{1,19},{2,16},{3,17},{4,22},{5,23},{6,20},{7,21},{8,26},{9,... | collective-permute-start | bytes 245768 | tf_op jit(solution)/shard_map/ppermute | solution.py:523
  9.4 0.5 collective-permute-start.5
  9.9 1.5 %collective-permute-done.4 = f32[1,5,32,128]{3,2,1,0:T(8,128)S(1)} collective-permute-done((f32[1,5,32,128]{3,2,1,0:T(8,128)S(1)}, f32[1,5,32,128]{3,2,1,0:T(8,128)S(1)}, u32[]{:S(2)}, u32[]{:S(2)}) %collective-permute-start.4) | collective-permute-done | bytes 81952 | tf_op jit(solution)/shard_map/ppermute | solution.py:523
  11.4 2.3 %collective-permute-done.6 = f32[1,5,32,128]{3,2,1,0:T(8,128)S(1)} collective-permute-done((f32[1,5,32,128]{3,2,1,0:T(8,128)S(1)}, f32[1,5,32,128]{3,2,1,0:T(8,128)S(1)}, u32[]{:S(2)}, u32[]{:S(2)}) %collective-permute-start.6) | collective-permute-done | bytes 81952 | tf_op jit(solution)/shard_map/ppermute | solution.py:523
  13.7 1.1 %collective-permute-done.5 = f32[1,5,32,128]{3,2,1,0:T(8,128)S(1)} collective-permute-done((f32[1,5,32,128]{3,2,1,0:T(8,128)S(1)}, f32[1,5,32,128]{3,2,1,0:T(8,128)S(1)}, u32[]{:S(2)}, u32[]{:S(2)}) %collective-permute-start.5) | collective-permute-done | bytes 81952 | tf_op jit(solution)/shard_map/ppermute | solution.py:523
  14.8 3.7 %collective-permute-start.9 = (f32[1,5,32,128]{3,2,1,0:T(8,128)S(1)}, f32[1,5,32,128]{3,2,1,0:T(8,128)S(1)}, u32[]{:S(2)}, u32[]{:S(2)}) collective-permute-start(f32[1,5,32,128]{3,2,1,0:T(8,128)S(1)} %fusion.1), channel_id=1, source_target_pairs={{0,12},{1,13},{2,14},{3,15},{4,8},{5,9},{6,10},{7,11},{8,4},{9,5},... | collective-permute-start | bytes 245768 | tf_op jit(solution)/shard_map/ppermute | solution.py:523
  18.5 0.8 %collective-permute-start.7 = (f32[1,5,32,128]{3,2,1,0:T(8,128)S(1)}, f32[1,5,32,128]{3,2,1,0:T(8,128)S(1)}, u32[]{:S(2)}, u32[]{:S(2)}) collective-permute-start(f32[1,5,32,128]{3,2,1,0:T(8,128)S(1)} %fusion.1), channel_id=1, source_target_pairs={{0,4},{1,5},{2,6},{3,7},{4,0},{5,1},{6,2},{7,3},{8,12},{9,13},{10,... | collective-permute-start | bytes 245768 | tf_op jit(solution)/shard_map/ppermute | solution.py:523
  19.2 2.7 %collective-permute-done.9 = f32[1,5,32,128]{3,2,1,0:T(8,128)S(1)} collective-permute-done((f32[1,5,32,128]{3,2,1,0:T(8,128)S(1)}, f32[1,5,32,128]{3,2,1,0:T(8,128)S(1)}, u32[]{:S(2)}, u32[]{:S(2)}) %collective-permute-start.9) | collective-permute-done | bytes 81952 | tf_op jit(solution)/shard_map/ppermute | solution.py:523
  22.0 3.0 %collective-permute-done.8 = f32[1,5,32,128]{3,2,1,0:T(8,128)S(1)} collective-permute-done((f32[1,5,32,128]{3,2,1,0:T(8,128)S(1)}, f32[1,5,32,128]{3,2,1,0:T(8,128)S(1)}, u32[]{:S(2)}, u32[]{:S(2)}) %collective-permute-start.8) | collective-permute-done | bytes 81952 | tf_op jit(solution)/shard_map/ppermute | solution.py:523
  25.0 0.7 %collective-permute-start.12 = (f32[1,5,32,128]{3,2,1,0:T(8,128)S(1)}, f32[1,5,32,128]{3,2,1,0:T(8,128)S(1)}, u32[]{:S(2)}, u32[]{:S(2)}) collective-permute-start(f32[1,5,32,128]{3,2,1,0:T(8,128)S(1)} %add_add_fusion), channel_id=1, source_target_pairs={{0,18},{1,19},{2,16},{3,17},{4,22},{5,23},{6,20},{7,21},{8,26},{9,... | collective-permute-start | bytes 245768 | tf_op jit(solution)/shard_map/ppermute | solution.py:523
  25.6 1.6 %collective-permute-start.11 = (f32[1,5,32,128]{3,2,1,0:T(8,128)S(1)}, f32[1,5,32,128]{3,2,1,0:T(8,128)S(1)}, u32[]{:S(2)}, u32[]{:S(2)}) collective-permute-start(f32[1,5,32,128]{3,2,1,0:T(8,128)S(1)} %add_add_fusion), channel_id=1, source_target_pairs={{0,16},{1,17},{2,18},{3,19},{4,20},{5,21},{6,22},{7,23},{8,24},{9,... | collective-permute-start | bytes 245768 | tf_op jit(solution)/shard_map/ppermute | solution.py:523
  27.3 1.3 %collective-permute-start.10 = (f32[1,5,32,128]{3,2,1,0:T(8,128)S(1)}, f32[1,5,32,128]{3,2,1,0:T(8,128)S(1)}, u32[]{:S(2)}, u32[]{:S(2)}) collective-permute-start(f32[1,5,32,128]{3,2,1,0:T(8,128)S(1)} %add_add_fusion), channel_id=1, source_target_pairs={{0,2},{1,3},{2,0},{3,1},{4,6},{5,7},{6,4},{7,5},{8,10},{9,11},{10,... | collective-permute-start | bytes 245768 | tf_op jit(solution)/shard_map/ppermute | solution.py:523
  28.5 2.8 %collective-permute-start.1 = (f32[8,4,8,384]{3,2,1,0:T(8,128)S(1)}, f32[8,4,8,384]{3,2,1,0:T(8,128)S(1)}, u32[]{:S(2)}, u32[]{:S(2)}) collective-permute-start(f32[8,4,8,384]{3,2,1,0:T(8,128)S(1)} %get-tuple-element.20), channel_id=1, source_target_pairs={{1,2},{2,1},{3,4},{4,3},{5,6},{6,5},{7,8},{8,7},{9,10},{10,9},{11,... | collective-permute-start | bytes 1179656 | tf_op jit(solution)/shard_map/ppermute | solution.py:529
  31.8 1.4 %shard_map.83 = (f32[6,8,4,96,128]{4,3,2,1,0:T(8,128)S(1)}, bf16[2,256,384]{2,1,0:T(8,128)(2,1)S(1)}, bf16[128,64]{1,0:T(8,128)(2,1)S(1)}, f32[80,256]{1,0:T(8,128)S(1)}) custom-call(s32[1]{0:T(128)} %bitcast.info, f32[6,8,4,96,128]{4,3,2,1,0:T(8,128)S(1)} %get-tuple-element.16.refs_0_, ...), custom_call_target="tpu_custom_call", output_to_operand_aliasing={{0}: (1, {})} | custom-call | flops 1000000 | bytes 5000000 | tf_op jit(solution)/shard_map/pallas_call | solution.py:553
  33.2 0.5 shard_map.84.refs_0_
  33.7 8.1 %collective-permute-done.1.refs_3_ = f32[8,4,8,384]{3,2,1,0:T(8,128)S(1)} collective-permute-done((f32[8,4,8,384]{3,2,1,0:T(8,128)S(1)}, f32[8,4,8,384]{3,2,1,0:T(8,128)S(1)}, u32[]{:S(2)}, u32[]{:S(2)}) %collective-permute-start.1) | collective-permute-done | bytes 393248 | tf_op jit(solution)/shard_map/ppermute | solution.py:529
  42.3 0.9 %collective-permute-start.2 = (f32[80,256]{1,0:T(8,128)S(1)}, f32[80,256]{1,0:T(8,128)S(1)}, u32[]{:S(2)}, u32[]{:S(2)}) collective-permute-start(f32[80,256]{1,0:T(8,128)S(1)} %get-tuple-element.22), channel_id=1, source_target_pairs={{0,16},{16,0},{1,17},{17,1},{2,18},{18,2},{3,19},{19,3},{4,20},{20... | collective-permute-start | bytes 245768 | tf_op jit(solution)/shard_map/ppermute | solution.py:529
  43.2 3.6 %collective-permute-done.2.refs_1_ = f32[80,256]{1,0:T(8,128)S(1)} collective-permute-done((f32[80,256]{1,0:T(8,128)S(1)}, f32[80,256]{1,0:T(8,128)S(1)}, u32[]{:S(2)}, u32[]{:S(2)}) %collective-permute-start.2) | collective-permute-done | bytes 81952 | tf_op jit(solution)/shard_map/ppermute | solution.py:529
  46.8 2.4 %shard_map.86.refs_0_ = f32[6,8,4,96,128]{4,3,2,1,0:T(8,128)S(1)} custom-call(s32[1]{0:T(128)} %bitcast.info, f32[6,8,4,96,128]{4,3,2,1,0:T(8,128)S(1)} %get-tuple-element.21.refs_0_, f32[80,256]{1,0:T(8,128)S(1)} %collective-permute-done.2.refs_1_), custom_call_target="tpu_custom_call", output_to_operand_aliasing={{}: (1, {})} | custom-call | flops 10000000 | bytes 8000000 | tf_op jit(solution)/shard_map/pallas_call | solution.py:553
  49.2 1.8 %shard_map.87.refs_0_ = f32[6,8,4,96,128]{4,3,2,1,0:T(8,128)S(1)} custom-call(s32[1]{0:T(128)} %bitcast.info, f32[6,8,4,96,128]{4,3,2,1,0:T(8,128)S(1)} %shard_map.86.refs_0_), custom_call_target="tpu_custom_call", output_to_operand_aliasing={{}: (1, {})} | custom-call | flops 10000000 | bytes 8000000 | tf_op jit(solution)/shard_map/pallas_call | solution.py:553
  51.0 1.2 %shard_map.88.refs_1_ = f32[6,8,4,96,128]{4,3,2,1,0:T(8,128)S(1)} custom-call(s32[1]{0:T(128)} %bitcast.info, f32[6,8,4,96,128]{4,3,2,1,0:T(8,128)S(1)} %shard_map.87.refs_0_), custom_call_target="tpu_custom_call", output_to_operand_aliasing={{}: (1, {})} | custom-call | flops 10000000 | bytes 8000000 | tf_op jit(solution)/shard_map/pallas_call | solution.py:553
  52.2 3.4 %shard_map.89 = f32[5,8,64,384]{3,2,1,0:T(8,128)} custom-call(s32[1]{0:T(128)} %bitcast.info, f32[5,8]{1,0:T(8,128)S(1)} %copy-done.2, f32[6,8,4,96,128]{4,3,2,1,0:T(8,128)S(1)} %shard_map.88.refs_1_, f32[4,5,32,128]{3,2,1,0:T(8,128)S(1)} %pad_maximum_fusion.refs_2_, f32[4,5,32,128]{3,2,1,0:T(8,128)S(1)} %collective-permute-done.13.refs_3_, ...), custom_call_target="tpu_custom_call" | custom-call | flops 600000000 | bytes 8500000 | tf_op jit(solution)/shard_map/pallas_call | solution.py:553
  (23 shorter events, 1.2 us)
Async XLA Ops:
  0.0 31.8 %copy-start = (bf16[16,128,64]{2,1,0:T(8,128)(2,1)S(1)}, bf16[16,128,64]{2,1,0:T(8,128)(2,1)}, u32[]{:S(2)}) copy-start(bf16[16,128,64]{2,1,0:T(8,128)(2,1)} %constant.22.clone.refs_2_) | copy-start | bytes 786436
  0.0 31.8 %copy-start.1 = (bf16[2,2,64,384]{3,2,1,0:T(8,128)(2,1)S(1)}, bf16[2,2,64,384]{3,2,1,0:T(8,128)(2,1)}, u32[]{:S(2)}) copy-start(bf16[2,2,64,384]{3,2,1,0:T(8,128)(2,1)} %constant.21.clone.refs_1_) | copy-start | bytes 589828
  4.5 1.7 %collective-permute-start.3 = (f32[4,5,32,128]{3,2,1,0:T(8,128)S(1)}, f32[4,5,32,128]{3,2,1,0:T(8,128)S(1)}, u32[]{:S(2)}, u32[]{:S(2)}) collective-permute-start(f32[4,5,32,128]{3,2,1,0:T(8,128)S(1)} %get-tuple-element.24), channel_id=1, source_target_pairs={{0,1},{1,0},{2,3},{3,2},{4,5},{5,4},{6,7},{7,6},{8,9},{9,8},{10,11... | collective-permute-start | bytes 983048 | tf_op jit(solution)/shard_map/ppermute | solution.py:523
  6.3 5.1 %collective-permute-start.4 = (f32[1,5,32,128]{3,2,1,0:T(8,128)S(1)}, f32[1,5,32,128]{3,2,1,0:T(8,128)S(1)}, u32[]{:S(2)}, u32[]{:S(2)}) collective-permute-start(f32[1,5,32,128]{3,2,1,0:T(8,128)S(1)} %get-tuple-element.27), channel_id=1, source_target_pairs={{0,2},{1,3},{2,0},{3,1},{4,6},{5,7},{6,4},{7,5},{8,10},{9,11},{10,... | collective-permute-start | bytes 245768 | tf_op jit(solution)/shard_map/ppermute | solution.py:523
  6.4 7.3 %collective-permute-start.6 = (f32[1,5,32,128]{3,2,1,0:T(8,128)S(1)}, f32[1,5,32,128]{3,2,1,0:T(8,128)S(1)}, u32[]{:S(2)}, u32[]{:S(2)}) collective-permute-start(f32[1,5,32,128]{3,2,1,0:T(8,128)S(1)} %get-tuple-element.28), channel_id=1, source_target_pairs={{0,18},{1,19},{2,16},{3,17},{4,22},{5,23},{6,20},{7,21},{8,26},{9,... | collective-permute-start | bytes 245768 | tf_op jit(solution)/shard_map/ppermute | solution.py:523
  9.4 5.4 %collective-permute-start.5 = (f32[1,5,32,128]{3,2,1,0:T(8,128)S(1)}, f32[1,5,32,128]{3,2,1,0:T(8,128)S(1)}, u32[]{:S(2)}, u32[]{:S(2)}) collective-permute-start(f32[1,5,32,128]{3,2,1,0:T(8,128)S(1)} %get-tuple-element.29), channel_id=1, source_target_pairs={{0,16},{1,17},{2,18},{3,19},{4,20},{5,21},{6,22},{7,23},{8,24},{9,... | collective-permute-start | bytes 245768 | tf_op jit(solution)/shard_map/ppermute | solution.py:523
  14.8 7.2 %collective-permute-start.9 = (f32[1,5,32,128]{3,2,1,0:T(8,128)S(1)}, f32[1,5,32,128]{3,2,1,0:T(8,128)S(1)}, u32[]{:S(2)}, u32[]{:S(2)}) collective-permute-start(f32[1,5,32,128]{3,2,1,0:T(8,128)S(1)} %fusion.1), channel_id=1, source_target_pairs={{0,12},{1,13},{2,14},{3,15},{4,8},{5,9},{6,10},{7,11},{8,4},{9,5},... | collective-permute-start | bytes 245768 | tf_op jit(solution)/shard_map/ppermute | solution.py:523
  18.5 6.5 %collective-permute-start.8 = (f32[1,5,32,128]{3,2,1,0:T(8,128)S(1)}, f32[1,5,32,128]{3,2,1,0:T(8,128)S(1)}, u32[]{:S(2)}, u32[]{:S(2)}) collective-permute-start(f32[1,5,32,128]{3,2,1,0:T(8,128)S(1)} %fusion.1), channel_id=1, source_target_pairs={{0,8},{1,9},{2,10},{3,11},{4,12},{5,13},{6,14},{7,15},{8,0},{9,1},... | collective-permute-start | bytes 245768 | tf_op jit(solution)/shard_map/ppermute | solution.py:523
  18.5 6.5 %collective-permute-start.7 = (f32[1,5,32,128]{3,2,1,0:T(8,128)S(1)}, f32[1,5,32,128]{3,2,1,0:T(8,128)S(1)}, u32[]{:S(2)}, u32[]{:S(2)}) collective-permute-start(f32[1,5,32,128]{3,2,1,0:T(8,128)S(1)} %fusion.1), channel_id=1, source_target_pairs={{0,4},{1,5},{2,6},{3,7},{4,0},{5,1},{6,2},{7,3},{8,12},{9,13},{10,... | collective-permute-start | bytes 245768 | tf_op jit(solution)/shard_map/ppermute | solution.py:523
  25.0 6.3 %collective-permute-start.12 = (f32[1,5,32,128]{3,2,1,0:T(8,128)S(1)}, f32[1,5,32,128]{3,2,1,0:T(8,128)S(1)}, u32[]{:S(2)}, u32[]{:S(2)}) collective-permute-start(f32[1,5,32,128]{3,2,1,0:T(8,128)S(1)} %add_add_fusion), channel_id=1, source_target_pairs={{0,18},{1,19},{2,16},{3,17},{4,22},{5,23},{6,20},{7,21},{8,26},{9,... | collective-permute-start | bytes 245768 | tf_op jit(solution)/shard_map/ppermute | solution.py:523
  25.6 5.7 %collective-permute-start.11 = (f32[1,5,32,128]{3,2,1,0:T(8,128)S(1)}, f32[1,5,32,128]{3,2,1,0:T(8,128)S(1)}, u32[]{:S(2)}, u32[]{:S(2)}) collective-permute-start(f32[1,5,32,128]{3,2,1,0:T(8,128)S(1)} %add_add_fusion), channel_id=1, source_target_pairs={{0,16},{1,17},{2,18},{3,19},{4,20},{5,21},{6,22},{7,23},{8,24},{9,... | collective-permute-start | bytes 245768 | tf_op jit(solution)/shard_map/ppermute | solution.py:523
  27.3 4.4 %collective-permute-start.10 = (f32[1,5,32,128]{3,2,1,0:T(8,128)S(1)}, f32[1,5,32,128]{3,2,1,0:T(8,128)S(1)}, u32[]{:S(2)}, u32[]{:S(2)}) collective-permute-start(f32[1,5,32,128]{3,2,1,0:T(8,128)S(1)} %add_add_fusion), channel_id=1, source_target_pairs={{0,2},{1,3},{2,0},{3,1},{4,6},{5,7},{6,4},{7,5},{8,10},{9,11},{10,... | collective-permute-start | bytes 245768 | tf_op jit(solution)/shard_map/ppermute | solution.py:523
  28.5 5.2 %collective-permute-start = (f32[8,4,8,384]{3,2,1,0:T(8,128)S(1)}, f32[8,4,8,384]{3,2,1,0:T(8,128)S(1)}, u32[]{:S(2)}, u32[]{:S(2)}) collective-permute-start(f32[8,4,8,384]{3,2,1,0:T(8,128)S(1)} %get-tuple-element.19), channel_id=1, source_target_pairs={{0,1},{1,0},{2,3},{3,2},{4,5},{5,4},{6,7},{7,6},{8,9},{9,8},{10,11... | collective-permute-start | bytes 1179656 | tf_op jit(solution)/shard_map/ppermute | solution.py:529
  28.5 13.3 %collective-permute-start.1 = (f32[8,4,8,384]{3,2,1,0:T(8,128)S(1)}, f32[8,4,8,384]{3,2,1,0:T(8,128)S(1)}, u32[]{:S(2)}, u32[]{:S(2)}) collective-permute-start(f32[8,4,8,384]{3,2,1,0:T(8,128)S(1)} %get-tuple-element.20), channel_id=1, source_target_pairs={{1,2},{2,1},{3,4},{4,3},{5,6},{6,5},{7,8},{8,7},{9,10},{10,9},{11,... | collective-permute-start | bytes 1179656 | tf_op jit(solution)/shard_map/ppermute | solution.py:529
  31.7 20.4 %collective-permute-start.13 = (f32[4,5,32,128]{3,2,1,0:T(8,128)S(1)}, f32[4,5,32,128]{3,2,1,0:T(8,128)S(1)}, u32[]{:S(2)}, u32[]{:S(2)}) collective-permute-start(f32[4,5,32,128]{3,2,1,0:T(8,128)S(1)} %pad_maximum_fusion.refs_2_), channel_id=1, source_target_pairs={{0,1},{1,0},{2,3},{3,2},{4,5},{5,4},{6,7},{7,6},{8,9},{9,8},{10,11... | collective-permute-start | bytes 983048 | tf_op jit(solution)/shard_map/ppermute | solution.py:523
  42.3 4.5 %collective-permute-start.2 = (f32[80,256]{1,0:T(8,128)S(1)}, f32[80,256]{1,0:T(8,128)S(1)}, u32[]{:S(2)}, u32[]{:S(2)}) collective-permute-start(f32[80,256]{1,0:T(8,128)S(1)} %get-tuple-element.22), channel_id=1, source_target_pairs={{0,16},{16,0},{1,17},{17,1},{2,18},{18,2},{3,19},{19,3},{4,20},{20... | collective-permute-start | bytes 245768 | tf_op jit(solution)/shard_map/ppermute | solution.py:529
  51.0 1.2 %copy-start.2 = (f32[5,8]{1,0:T(8,128)S(1)}, f32[5,8]{1,0:T(8,128)}, u32[]{:S(2)}) copy-start(f32[5,8]{1,0:T(8,128)} %refs_0_.3) | copy-start | bytes 484
